TPU v7x, 256 devices: a whole 4x4x8 slice. The times are simulated.
256 devices in a mesh: dp: 32 (over y, x, core), seq: 8 (over z).
Axes of the slice: x: 4, y: 4, z: 8, core: 2. Of those that a mesh axis runs over, the one named last changes fastest.
Arguments:
- tokens: bfloat16 [65536, 2048], P(('dp', 'seq')), may hold values from -24 to 24
- queries: bfloat16 [65536, 1024], P(('dp', 'seq')), may hold values from -6 to 6
- kv_weight: bfloat16 [2048, 2048], P('seq'), may hold values from -0.0625 to 0.0625
- out_grad: bfloat16 [65536, 1024], P(('dp', 'seq')), may hold values from -6 to 6
Outputs:
- output: bfloat16 [65536, 1024], P(('dp', 'seq'))
- token_grad: bfloat16 [65536, 2048], P(('dp', 'seq'))
- query_grad: bfloat16 [65536, 1024], P(('dp', 'seq'))
- weight_grad: float32 [2048, 2048], P(('dp', 'seq'))
All inputs are finite; a program needn't handle non-finite values.
Results may differ from a plain program's by a relative error of at most 0.014.
Values may be sent and summed in bfloat16 or wider, within the bound.
No kernel may reach another device: no remote copies, remote signals or barrier semaphores. Data moves between devices by JAX's collectives and lax.ppermute only.
A program may use at most 128 MiB of HBM per device.

v0:
```python
import math

import jax
import jax.numpy as jnp
from jax import lax
from jax.experimental import pallas as pl
from jax.experimental.pallas import tpu as pltpu
from jax.sharding import Mesh
from jax.sharding import PartitionSpec as P


HD = 128
EPSILON = 1e-05
BF = jnp.bfloat16
F32 = jnp.float32
VMEM = pl.BlockSpec(memory_space=pltpu.VMEM)
ANY = pl.BlockSpec(memory_space=pl.ANY)


def feature(u):
    return jnp.where(u > 0, u + 1.0, jnp.exp(jnp.minimum(u, 0.0)))


def slope(u):
    return jnp.where(u > 0, 1.0, jnp.exp(jnp.minimum(u, 0.0)))


def dot(a, b, da, db):
    return lax.dot_general(a, b, (((da,), (db,)), ((), ())), preferred_element_type=F32)


def call(body, outs, *args, in_specs=None, out_specs=None, scratch=(), flops=0):
    size = sum(math.prod(a.shape) * a.dtype.itemsize for a in args)
    size += sum(math.prod(s) * jnp.dtype(d).itemsize for s, d in outs)
    return pl.pallas_call(
        body,
        out_shape=[jax.ShapeDtypeStruct(s, d) for s, d in outs],
        in_specs=in_specs or [VMEM] * len(args),
        out_specs=out_specs or [VMEM] * len(outs),
        scratch_shapes=list(scratch),
        cost_estimate=pl.CostEstimate(flops=flops, bytes_accessed=size, transcendentals=0),
    )(*args)


def shift(x, axis, step):
    size = lax.axis_size(axis)
    return lax.ppermute(x, axis, [(i, (i + step) % size) for i in range(size)])


def turn_kernel(own, sib, both, turned):
    both[:256] = own[...]
    both[256:] = sib[...]
    for n in range(16):
        at = slice(n * HD, n * HD + HD)
        turned[n, :, :256] = own[:, at].T
        turned[n, :, 256:] = sib[:, at].T


def key_value_kernel(tok, *refs):
    pieces, (w_out, kv, state, w_ref, sems, out_sems) = refs[:8], refs[8:]
    y, x = lax.axis_index("y"), lax.axis_index("x")
    copies = []
    for half in range(2):
        for e in range(4):
            for d in range(4):
                py, px = (y - e, x - d) if half == 0 else (y - d, x - e)
                place = lax.rem(py + 4, 4) * 4 + lax.rem(px + 4, 4)
                copies.append(
                    pltpu.make_async_copy(
                        pieces[half * 4 + e].at[d],
                        w_ref.at[:, place, :, pl.ds(half * 512, 512)],
                        sems.at[len(copies)],
                    )
                )
    for c in copies:
        c.start()
    stored = []
    for half in range(2):
        for c in copies[half * 16 : half * 16 + 16]:
            c.wait()
        at = pl.ds(half * 512, 512)
        stored.append(
            pltpu.make_async_copy(
                w_ref.at[:, :, :, at], w_out.at[:, :, :, at], out_sems.at[half]
            )
        )
        stored[-1].start()

        def tile(n, _):
            at = pl.ds(pl.multiple_of(n * 256, 256), 256)
            w = w_ref[:, :, :, at].reshape(2048, 256)
            kv[:, at] = dot(tok[...], w, 1, 0).astype(BF)
            return 0

        lax.fori_loop(half * 2, half * 2 + 2, tile, 0)
    for s in range(2):
        rows = slice(s * 256, s * 256 + 256)
        for h in range(4):
            k = feature(kv[rows, h * HD : (h + 1) * HD].astype(F32)).astype(BF)
            v = kv[rows, 512 + h * HD : 512 + (h + 1) * HD]
            state[s * 4 + h] = dot(k, v, 0, 0).astype(BF)
    for c in stored:
        c.wait()


def sums_kernel(later, states, out):
    order = list(range(states.shape[0]))
    if later:
        order.reverse()
    total = jnp.zeros(states.shape[1:], F32)
    for k in order:
        out[k] = total.astype(BF)
        total = total + states[k].astype(F32)


def causal():
    shape = (256, 256)
    return lax.broadcasted_iota(jnp.int32, shape, 0) >= lax.broadcasted_iota(jnp.int32, shape, 1)


def spots():
    for s in range(2):
        for h in range(4):
            rows = slice(s * 256, s * 256 + 256)
            yield (
                s * 4 + h,
                rows,
                slice(h * HD, (h + 1) * HD),
                slice(512 + h * HD, 512 + (h + 1) * HD),
            )


def local_kernel(q_own, q_sib, kv, qu, qf, scores, local):
    mask = causal()
    at = lax.axis_index("core") * 512
    qu[:256] = q_own[:, pl.ds(pl.multiple_of(at, 512), 512)]
    qu[256:] = q_sib[...]
    for n, rows, at, vat in spots():
        q = feature(qu[rows, at].astype(F32)).astype(BF)
        qf[rows, at] = q
        k = feature(kv[rows, at].astype(F32)).astype(BF)
        score = jnp.where(mask, dot(q, k, 1, 1), 0.0).astype(BF)
        scores[n] = score
        local[rows, at] = dot(score, kv[rows, vat], 1, 0)


def forward_kernel(qf, g_own, g_sib, local, before, out, grad_att, state):
    core = lax.axis_index("core")
    for n, rows, at, _ in spots():
        q = qf[rows, at]
        attended = local[rows, at] + dot(q, before[n], 1, 0)
        if n < 4:
            g = g_own[:, pl.ds(pl.multiple_of(core * 512 + n * HD, HD), HD)].astype(F32)
        else:
            g = g_sib[:, at].astype(F32)
        power = jnp.mean(attended * attended, axis=-1, keepdims=True) + EPSILON
        inverse = lax.rsqrt(power)
        normed = attended * inverse
        along = jnp.mean(g * normed, axis=-1, keepdims=True)
        grad = ((g - normed * along) * inverse).astype(BF)
        out[rows, at] = normed.astype(BF)
        grad_att[rows, at] = grad
        state[n] = dot(q, grad, 0, 0).astype(BF)


def mixed_kernel(qu, qf, kv, scores, grad_att, before, dq, local):
    mask = causal()
    for n, rows, at, vat in spots():
        u, q = qu[rows, at].astype(F32), qf[rows, at]
        k = feature(kv[rows, at].astype(F32)).astype(BF)
        a = grad_att[rows, at]
        mixed = jnp.where(mask, dot(a, kv[rows, vat], 1, 1), 0.0).astype(BF)
        grad_q = dot(mixed, k, 1, 0) + dot(a, before[n], 1, 1)
        dq[rows, at] = (grad_q * slope(u)).astype(BF)
        local[rows, at] = dot(mixed, q, 0, 0)
        local[rows, vat] = dot(scores[n], a, 0, 0)


def chunk(half, d, turned, dkv):
    if half == 0:
        to = lax.rem(lax.axis_index("x") + d, 4)
        tok = jnp.concatenate([turned[n * 4 + to] for n in range(4)], axis=0)
    else:
        to = lax.rem(lax.axis_index("y") + d, 4)
        tok = turned[pl.ds(to * 4, 4)].reshape(512, 512)
    part = dot(tok, dkv[:, half * 512 : half * 512 + 512], 1, 0)
    return part.astype(BF).reshape(4, 128, 512)


STEPS = (2, 1, 3)


def backward_kernel(kv, local, after, turned_hbm, dkv, *refs):
    outs, (turned, held, sem, sems) = refs[:6], refs[6:]
    load = pltpu.make_async_copy(turned_hbm, turned, sem)
    load.start()
    for n, rows, at, vat in spots():
        u = kv[rows, at].astype(F32)
        k, v = feature(u).astype(BF), kv[rows, vat]
        grad_k = local[rows, at] + dot(v, after[n], 1, 1)
        grad_v = local[rows, vat] + dot(k, after[n], 1, 0)
        dkv[rows, at] = (grad_k * slope(u)).astype(BF)
        dkv[rows, vat] = grad_v.astype(BF)
    load.wait()
    stores = []
    for i, d in enumerate(STEPS):
        for half in range(2):
            n = 2 * i + half
            held[n] = chunk(half, d, turned, dkv)
            stores.append(pltpu.make_async_copy(held.at[n], outs[n], sems.at[n]))
            stores[-1].start()
    for c in stores:
        c.wait()


def own_kernel(turned, dkv, _, a_ref, b_ref):
    a_ref[...] = chunk(0, 0, turned, dkv)
    b_ref[...] = chunk(1, 0, turned, dkv)


def pack_kernel(dkv, dq, out, _, back):
    back[:, :1024] = dkv[256:]
    back[:, 1024:1536] = dq[256:]
    back[:, 1536:] = out[256:]


def plane_kernel(*refs):
    ins, outs, (held, sems) = refs[:8], refs[9:17], refs[17:]
    y, x = lax.axis_index("y"), lax.axis_index("x")
    loads = {}
    for e in (2, 1, 3, 0):
        for half, here in ((0, y), (1, x)):
            at = lax.rem(here + e, 4)
            for k in range(4):
                n = (e * 2 + half) * 4 + k
                loads[n] = pltpu.make_async_copy(ins[half * 4 + k].at[at], held.at[n], sems.at[n])
                loads[n].start()
    for e in (2, 1, 3, 0):
        for half in range(2):
            first = (e * 2 + half) * 4
            for n in range(first, first + 4):
                loads[n].wait()
            total = held[first].astype(F32)
            for n in range(first + 1, first + 4):
                total = total + held[n].astype(F32)
            to = outs[half * 4 + e]
            to[...] = total.astype(to.dtype)


def column_kernel(*refs):
    out = refs[-1]
    for half in range(2):
        total = refs[half * 4][...]
        for r in refs[half * 4 + 1 : half * 4 + 4]:
            total = total + r[...].astype(F32)
        out[:, :, half * 512 : half * 512 + 512] = total.reshape(16, 8, 512).astype(BF)


def last_kernel(scale, parts, out):
    for c in range(2):
        total = parts[c * 8].astype(F32)
        for k in range(1, 8):
            total = total + parts[c * 8 + k].astype(F32)
        total = total * scale
        for half in range(2):
            at = half * 1024 + c * 512
            out[:, at : at + 512] = total[:, half * 512 : half * 512 + 512]


def token_kernel(dkv, got, o, dq, w, w_sib, out, o_out, dq_out):
    total = dot(dkv[:256], w[0].reshape(256, 1024), 1, 1)
    total += dot(got[:, :1024], w_sib[0].reshape(256, 1024), 1, 1)
    out[...] = total.astype(BF)

    @pl.when(pl.program_id(0) == 0)
    def _():
        core = lax.axis_index("core")
        mine = pl.ds(pl.multiple_of(core * 512, 512), 512)
        other = pl.ds(pl.multiple_of((1 - core) * 512, 512), 512)
        o_out[:, mine] = o[:256]
        o_out[:, other] = got[:, 1536:]
        dq_out[:, mine] = dq[:256]
        dq_out[:, other] = got[:, 1024:1536]


def token_call(rows, *args):
    def fixed(shape):
        return pl.BlockSpec(shape, lambda n: (0,) * len(shape))

    tile = pl.BlockSpec((1, 16, 16, 1024), lambda n: (n, 0, 0, 0))
    return pl.pallas_call(
        token_kernel,
        grid=(8,),
        out_shape=[jax.ShapeDtypeStruct((rows, n), BF) for n in (2048, 1024, 1024)],
        in_specs=[fixed(a.shape) for a in args[:4]] + [tile] * 2,
        out_specs=[pl.BlockSpec((rows, 256), lambda n: (0, n))] + [fixed((rows, 1024))] * 2,
        cost_estimate=pl.CostEstimate(
            flops=4 * 2 * rows * 2048 * 2048, bytes_accessed=12 << 20, transcendentals=0
        ),
    )(*args)


def on_device(tokens, queries, kv_weight, out_grad):
    rows = tokens.shape[0]
    core = lax.axis_index("core")

    def swap(x):
        return lax.ppermute(x, "core", [(0, 1), (1, 0)])

    def theirs(x):
        return swap(lax.dynamic_slice_in_dim(x, (1 - core) * 512, 512, 1))

    place = lax.axis_index(("y", "x"))
    mine = lax.dynamic_slice_in_dim(kv_weight, place * 16, 16, 0).reshape(16, 2, 2, 512)
    mine = lax.dynamic_index_in_dim(mine, core, 2, keepdims=False).reshape(16, 1024)
    along_z = lax.all_to_all(jnp.broadcast_to(mine[None], (8, 16, 1024)), "z", 0, 0, tiled=True)
    a0, b0 = along_z[:, :, :512], along_z[:, :, 512:]
    first = [(shift(a0, "x", d), shift(b0, "y", d)) for d in (2, 1, 3)]
    (a2, b2), (a1, b1), (a3, b3) = first
    a = jnp.stack([a0, a1, a2, a3])
    b = jnp.stack([b0, b1, b2, b3])
    (p2, r2), (p1, r1), (p3, r3) = [(shift(a, "y", e), shift(b, "x", e)) for e in (2, 1, 3)]

    sib_tokens = swap(tokens)
    sib_q, sib_g = theirs(queries), theirs(out_grad)
    both, turned = call(
        turn_kernel,
        [((2 * rows, 2048), BF), ((16, HD, 2 * rows), BF)],
        tokens, sib_tokens,
    )
    half = ((2 * rows, 512), BF)
    whole = ((2 * rows, 1024), BF)
    states = ((8, HD, HD), BF)
    w, kv, state = call(
        key_value_kernel,
        [((8, 16, 16, 1024), BF), whole, states],
        both, a, p1, p2, p3, b, r1, r2, r3,
        in_specs=[VMEM] + [ANY] * 8,
        out_specs=[ANY, VMEM, VMEM],
        scratch=[
            pltpu.VMEM((8, 16, 16, 1024), BF),
            pltpu.SemaphoreType.DMA((32,)),
            pltpu.SemaphoreType.DMA((2,)),
        ],
        flops=2 * 512 * 2048 * 1024,
    )
    sib_w = swap(w)

    def exchange(x, later, ahead):
        x = lax.all_to_all(x, "z", 0, 0, tiled=True)
        (x,) = call(
            lambda i, _, o: sums_kernel(later, i, o), [states], x, ahead, in_specs=[VMEM, ANY]
        )
        return lax.all_to_all(x, "z", 0, 0, tiled=True)

    qu, qf, scores, local = call(
        local_kernel,
        [half, half, ((8, 256, 256), BF), ((2 * rows, 512), F32)],
        queries, sib_q, kv,
        flops=2 * 8 * 256 * 256 * 256,
    )
    before = exchange(state, False, local)
    out, grad_att, state = call(
        forward_kernel,
        [half, half, states],
        qf, out_grad, sib_g, local, before,
        flops=2 * 8 * 256 * 128 * 256,
    )
    dq, local = call(
        mixed_kernel,
        [half, ((2 * rows, 1024), F32)],
        qu, qf, kv, scores, grad_att, before,
        flops=2 * 8 * 256 * 256 * 640,
    )
    after = exchange(state, True, local)
    sent = ((4, 128, 512), BF)
    dkv, a2, b2, a1, b1, a3, b3 = call(
        backward_kernel,
        [whole] + [sent] * 6,
        kv, local, after, turned,
        in_specs=[VMEM] * 3 + [ANY],
        out_specs=[VMEM] + [ANY] * 6,
        scratch=[
            pltpu.VMEM((16, HD, 2 * rows), BF),
            pltpu.VMEM((6, 4, 128, 512), BF),
            pltpu.SemaphoreType.DMA(()),
            pltpu.SemaphoreType.DMA((6,)),
        ],
        flops=2 * 512 * 2048 * 1024,
    )
    wa, wb = {}, {}
    for d, to_x, to_y in ((2, a2, b2), (1, a1, b1), (3, a3, b3)):
        wa[d] = shift(to_x, "x", d)
        wb[d] = shift(to_y, "y", d)
    (back,) = call(pack_kernel, [((rows, 2048), BF)], dkv, dq, out, a2, in_specs=[VMEM] * 3 + [ANY])
    a0, b0 = call(
        own_kernel, [sent] * 2, turned, dkv, back, in_specs=[VMEM] * 2 + [ANY],
        flops=2 * 512 * 512 * 1024,
    )
    token_grad, output, query_grad = token_call(rows, dkv, swap(back), out, dq, w, sib_w)
    full = ((128, 512), F32)
    sent = ((128, 512), BF)
    parts = call(
        plane_kernel,
        [full, sent, sent, sent, full, sent, sent, sent],
        a0, wa[1], wa[2], wa[3], b0, wb[1], wb[2], wb[3], token_grad,
        in_specs=[ANY] * 9,
        scratch=[pltpu.VMEM((32, 128, 512), BF), pltpu.SemaphoreType.DMA((32,))],
    )
    wa, wb = {}, {}
    for d in (2, 1, 3):
        wa[d], wb[d] = shift(parts[d], "y", d), shift(parts[4 + d], "x", d)
    (column,) = call(
        column_kernel,
        [((16, 8, 1024), BF)],
        parts[0], wa[1], wa[2], wa[3], parts[4], wb[1], wb[2], wb[3],
    )
    column = lax.all_to_all(column, ("core", "z"), 0, 0, tiled=True)
    scale = 1.0 / math.sqrt(rows * lax.axis_size(("y", "x", "core", "z")))
    (weight_grad,) = call(lambda i, o: last_kernel(scale, i, o), [((8, 2048), F32)], column)
    return (output, token_grad, query_grad, weight_grad)


def solution(mesh):
    fine = Mesh(mesh.devices.reshape(4, 4, 2, 8), ("y", "x", "core", "z"))
    rows = P(("y", "x", "core", "z"), None)
    return jax.shard_map(
        on_device,
        mesh=fine,
        in_specs=(rows, rows, P("z", None), rows),
        out_specs=(rows, rows, rows, rows),
        check_vma=False,
    )
```

profile of v0, /device:TPU:0, one launch (start us, length us, event | category | flops | bytes accessed | tf_op | source)
XLA Modules:
  0.0 260.5 jit_solution(14473991807821416444)
XLA Ops:
  0.7 1.2 copy-done
  2.1 0.7 broadcast_in_dim.8
  2.9 6.8 %all-to-all-start = ((bf16[8,16,1024]{2,1,0:T(8,128)(2,1)}), bf16[8,16,1024]{2,1,0:T(8,128)(2,1)S(1)}, u32[]{:S(2)}, u32[]{:S(2)}) async-start(bf16[8,16,1024]{2,1,0:T(8,128)(2,1)} %broadcast_in_dim.8), calls=%async_computation | async-start | bytes 524288 | tf_op jit(solution)/shard_map/all_to_all | solution.py:316
  9.6 11.9 %all-to-all-done = bf16[8,16,1024]{2,1,0:T(8,128)(2,1)S(1)} async-done(((bf16[8,16,1024]{2,1,0:T(8,128)(2,1)}), bf16[8,16,1024]{2,1,0:T(8,128)(2,1)S(1)}, u32[]{:S(2)}, u32[]{:S(2)}) %all-to-all-start) | async-done | bytes 262176 | tf_op jit(solution)/shard_map/all_to_all | solution.py:316
  21.6 3.1 %collective-permute-start.2 = (bf16[8,16,512]{2,1,0:T(8,128)(2,1)S(1)}, bf16[8,16,512]{2,1,0:T(8,128)(2,1)S(1)}, u32[]{:S(2)}, u32[]{:S(2)}) collective-permute-start(bf16[8,16,512]{2,1,0:T(8,128)(2,1)S(1)} %get-tuple-element.75), channel_id=1, source_target_pairs={{0,32},{16,48},{32,0},{48,16},{1,33},{17,49},{33,1},{49,17},{2,34}... | collective-permute-start | bytes 393224 | tf_op jit(solution)/shard_map/ppermute | solution.py:47
  25.3 2.6 %collective-permute-start.3 = (bf16[8,16,512]{2,1,0:T(8,128)(2,1)S(1)}, bf16[8,16,512]{2,1,0:T(8,128)(2,1)S(1)}, u32[]{:S(2)}, u32[]{:S(2)}) collective-permute-start(bf16[8,16,512]{2,1,0:T(8,128)(2,1)S(1)} %get-tuple-element.75), channel_id=1, source_target_pairs={{0,48},{16,0},{32,16},{48,32},{1,49},{17,1},{33,17},{49,33},{2,50}... | collective-permute-start | bytes 393224 | tf_op jit(solution)/shard_map/ppermute | solution.py:47
  27.9 0.7 collective-permute-done.2
  28.7 2.2 collective-permute-done.1
  30.9 3.1 %collective-permute-start.6 = (bf16[4,8,16,512]{3,2,1,0:T(8,128)(2,1)S(1)}, bf16[4,8,16,512]{3,2,1,0:T(8,128)(2,1)S(1)}, u32[]{:S(2)}, u32[]{:S(2)}) collective-permute-start(bf16[4,8,16,512]{3,2,1,0:T(8,128)(2,1)S(1)} %pad_maximum_fusion.refs_0_), channel_id=1, source_target_pairs={{0,192},{64,0},{128,64},{192,128},{1,193},{65,1},{129,65},{193,129... | collective-permute-start | bytes 1572872 | tf_op jit(solution)/shard_map/ppermute | solution.py:47
  34.0 0.6 collective-permute-start.8
  34.7 1.0 collective-permute-start.7
  35.6 2.3 collective-permute-start.9
  37.9 2.7 %collective-permute-done.8 = bf16[8,16,512]{2,1,0:T(8,128)(2,1)S(1)} collective-permute-done((bf16[8,16,512]{2,1,0:T(8,128)(2,1)S(1)}, bf16[8,16,512]{2,1,0:T(8,128)(2,1)S(1)}, u32[]{:S(2)}, u32[]{:S(2)}) %collective-permute-start.8) | collective-permute-done | bytes 131104 | tf_op jit(solution)/shard_map/ppermute | solution.py:47
  41.1 1.3 collective-permute-done.7
  42.4 8.8 %collective-permute-start.4 = (bf16[4,8,16,512]{3,2,1,0:T(8,128)(2,1)S(1)}, bf16[4,8,16,512]{3,2,1,0:T(8,128)(2,1)}, u32[]{:S(2)}, u32[]{:S(2)}) collective-permute-start(bf16[4,8,16,512]{3,2,1,0:T(8,128)(2,1)S(1)} %pad_maximum_fusion.refs_0_), channel_id=1, source_target_pairs={{0,64},{64,128},{128,192},{192,0},{1,65},{65,129},{129,193},{193,1... | collective-permute-start | bytes 1572872 | tf_op jit(solution)/shard_map/ppermute | solution.py:47
  51.2 9.2 %collective-permute-done.9 = bf16[8,16,512]{2,1,0:T(8,128)(2,1)S(1)} collective-permute-done((bf16[8,16,512]{2,1,0:T(8,128)(2,1)S(1)}, bf16[8,16,512]{2,1,0:T(8,128)(2,1)S(1)}, u32[]{:S(2)}, u32[]{:S(2)}) %collective-permute-start.9) | collective-permute-done | bytes 131104 | tf_op jit(solution)/shard_map/ppermute | solution.py:47
  60.5 3.0 %collective-permute-start.12 = (bf16[4,8,16,512]{3,2,1,0:T(8,128)(2,1)S(1)}, bf16[4,8,16,512]{3,2,1,0:T(8,128)(2,1)}, u32[]{:S(2)}, u32[]{:S(2)}) collective-permute-start(bf16[4,8,16,512]{3,2,1,0:T(8,128)(2,1)S(1)} %pad_maximum_fusion.1.refs_4_), channel_id=1, source_target_pairs={{0,48},{16,0},{32,16},{48,32},{1,49},{17,1},{33,17},{49,33},{2,50}... | collective-permute-start | bytes 1572872 | tf_op jit(solution)/shard_map/ppermute | solution.py:47
  63.5 0.8 copy-done.21
  64.4 0.9 collective-permute-start.10
  65.3 4.2 %shard_map.75 = (bf16[512,2048]{1,0:T(8,128)(2,1)}, bf16[16,128,512]{2,1,0:T(8,128)(2,1)}) custom-call(bf16[256,2048]{1,0:T(8,128)(2,1)} %own.1, bf16[256,2048]{1,0:T(8,128)(2,1)} %copy-done.5), custom_call_target="tpu_custom_call" | custom-call | bytes 6291456 | tf_op jit(solution)/shard_map/pallas_call | solution.py:35
  69.5 6.3 %collective-permute-done.12.refs_7_ = bf16[4,8,16,512]{3,2,1,0:T(8,128)(2,1)} collective-permute-done((bf16[4,8,16,512]{3,2,1,0:T(8,128)(2,1)S(1)}, bf16[4,8,16,512]{3,2,1,0:T(8,128)(2,1)}, u32[]{:S(2)}, u32[]{:S(2)}) %collective-permute-start.12) | collective-permute-done | bytes 524320 | tf_op jit(solution)/shard_map/ppermute | solution.py:47
  75.8 4.1 %collective-permute-done.10.refs_5_ = bf16[4,8,16,512]{3,2,1,0:T(8,128)(2,1)} collective-permute-done((bf16[4,8,16,512]{3,2,1,0:T(8,128)(2,1)S(1)}, bf16[4,8,16,512]{3,2,1,0:T(8,128)(2,1)}, u32[]{:S(2)}, u32[]{:S(2)}) %collective-permute-start.10) | collective-permute-done | bytes 524320 | tf_op jit(solution)/shard_map/ppermute | solution.py:47
  79.9 8.1 %shard_map.76 = (bf16[8,16,16,1024]{3,2,1,0:T(8,128)(2,1)}, bf16[512,1024]{1,0:T(8,128)(2,1)}, bf16[8,128,128]{2,1,0:T(8,128)(2,1)}) custom-call(bf16[512,2048]{1,0:T(8,128)(2,1)} %get-tuple-element.38.tok, bf16[4,8,16,512]{3,2,1,0:T(8,128)(2,1)} %copy-done.11, bf16[4,8,16,512]{3,2,1,0:T(8,128)(2,1)} %collective-permute-done.4.refs_1_, ...), custom_call_target="tpu_custom_call" | custom-call | flops 2147483648 | bytes 11796480 | tf_op jit(solution)/shard_map/pallas_call | solution.py:35
  88.1 3.4 %all-to-all-start.1 = ((bf16[8,128,128]{2,1,0:T(8,128)(2,1)}), bf16[8,128,128]{2,1,0:T(8,128)(2,1)S(1)}, u32[]{:S(2)}, u32[]{:S(2)}) async-start(bf16[8,128,128]{2,1,0:T(8,128)(2,1)} %get-tuple-element.44), calls=%async_computation.1 | async-start | bytes 524288 | tf_op jit(solution)/shard_map/all_to_all | solution.py:350
  92.2 3.7 %collective-permute-done.13.q_sib = bf16[256,512]{1,0:T(8,128)(2,1)S(1)} collective-permute-done((bf16[256,512]{1,0:T(8,128)(2,1)S(1)}, bf16[256,512]{1,0:T(8,128)(2,1)S(1)}, u32[]{:S(2)}, u32[]{:S(2)}) %collective-permute-start.13) | collective-permute-done | bytes 262176 | tf_op jit(solution)/shard_map/ppermute | solution.py:308
  95.9 0.7 copy-done.14
  96.6 3.8 %shard_map.77 = (bf16[512,512]{1,0:T(8,128)(2,1)}, bf16[512,512]{1,0:T(8,128)(2,1)}, bf16[8,256,256]{2,1,0:T(8,128)(2,1)}, f32[512,512]{1,0:T(8,128)}) custom-call(bf16[256,1024]{1,0:T(8,128)(2,1)} %q_own.1, bf16[256,512]{1,0:T(8,128)(2,1)} %copy-done.14, bf16[512,1024]{1,0:T(8,128)(2,1)} %get-tuple-element.39.kv), custom_call_target="tpu_custom_call" | custom-call | flops 268435456 | bytes 4980736 | tf_op jit(solution)/shard_map/pallas_call | solution.py:35
  100.3 3.9 %all-to-all-done.1.i = bf16[8,128,128]{2,1,0:T(8,128)(2,1)S(1)} async-done(((bf16[8,128,128]{2,1,0:T(8,128)(2,1)}), bf16[8,128,128]{2,1,0:T(8,128)(2,1)S(1)}, u32[]{:S(2)}, u32[]{:S(2)}) %all-to-all-start.1) | async-done | bytes 262176 | tf_op jit(solution)/shard_map/all_to_all | solution.py:350
  104.3 0.7 copy-done.6
  105.0 1.7 shard_map.78
  106.7 3.4 %all-to-all-start.2 = ((bf16[8,128,128]{2,1,0:T(8,128)(2,1)}), bf16[8,128,128]{2,1,0:T(8,128)(2,1)S(1)}, u32[]{:S(2)}, u32[]{:S(2)}) async-start(bf16[8,128,128]{2,1,0:T(8,128)(2,1)} %shard_map.78), calls=%async_computation.2 | async-start | bytes 524288 | tf_op jit(solution)/shard_map/all_to_all | solution.py:354
  110.3 1.5 collective-permute-done.14.g_sib
  111.8 10.6 %all-to-all-done.2.before = bf16[8,128,128]{2,1,0:T(8,128)(2,1)S(1)} async-done(((bf16[8,128,128]{2,1,0:T(8,128)(2,1)}), bf16[8,128,128]{2,1,0:T(8,128)(2,1)S(1)}, u32[]{:S(2)}, u32[]{:S(2)}) %all-to-all-start.2) | async-done | bytes 262176 | tf_op jit(solution)/shard_map/all_to_all | solution.py:354
  122.4 0.7 copy-done.1
  123.1 3.8 %shard_map.79 = (bf16[512,512]{1,0:T(8,128)(2,1)}, bf16[512,512]{1,0:T(8,128)(2,1)}, bf16[8,128,128]{2,1,0:T(8,128)(2,1)}) custom-call(bf16[512,512]{1,0:T(8,128)(2,1)} %get-tuple-element.41.qf, bf16[256,1024]{1,0:T(8,128)(2,1)} %g_own.1, bf16[256,512]{1,0:T(8,128)(2,1)} %copy-done.13, f32[512,512]{1,0:T(8,128)} %get-tuple-element.43._.local, ...), custom_call_target="tpu_custom_call" | custom-call | flops 134217728 | bytes 3932160 | tf_op jit(solution)/shard_map/pallas_call | solution.py:35
  127.0 3.4 %all-to-all-start.3 = ((bf16[8,128,128]{2,1,0:T(8,128)(2,1)}), bf16[8,128,128]{2,1,0:T(8,128)(2,1)S(1)}, u32[]{:S(2)}, u32[]{:S(2)}) async-start(bf16[8,128,128]{2,1,0:T(8,128)(2,1)} %get-tuple-element.47), calls=%async_computation.3 | async-start | bytes 524288 | tf_op jit(solution)/shard_map/all_to_all | solution.py:350
  130.4 6.1 %shard_map.80 = (bf16[512,512]{1,0:T(8,128)(2,1)}, f32[512,1024]{1,0:T(8,128)}) custom-call(bf16[512,512]{1,0:T(8,128)(2,1)} %get-tuple-element.40.qu, bf16[512,512]{1,0:T(8,128)(2,1)} %get-tuple-element.41.qf, bf16[512,1024]{1,0:T(8,128)(2,1)} %get-tuple-element.39.kv, bf16[8,256,256]{2,1,0:T(8,128)(2,1)} %get-tuple-element.42.scores, ...), custom_call_target="tpu_custom_call" | custom-call | flops 671088640 | bytes 6553600 | tf_op jit(solution)/shard_map/pallas_call | solution.py:35
  136.4 6.1 %all-to-all-done.3.i = bf16[8,128,128]{2,1,0:T(8,128)(2,1)S(1)} async-done(((bf16[8,128,128]{2,1,0:T(8,128)(2,1)}), bf16[8,128,128]{2,1,0:T(8,128)(2,1)S(1)}, u32[]{:S(2)}, u32[]{:S(2)}) %all-to-all-start.3) | async-done | bytes 262176 | tf_op jit(solution)/shard_map/all_to_all | solution.py:350
  142.5 0.7 copy-done.4
  143.2 1.7 shard_map.81
  144.9 15.7 %all_to_all.30.after = bf16[8,128,128]{2,1,0:T(8,128)(2,1)} all-to-all(bf16[8,128,128]{2,1,0:T(8,128)(2,1)} %shard_map.81), channel_id=1, replica_groups=mesh['y'=4,'x'=4,'core'=2,'z'=8] {'z'}, dimensions={0} | all-to-all | bytes 524288 | tf_op jit(solution)/shard_map/all_to_all | solution.py:354
  160.7 7.1 %shard_map.82 = (bf16[512,1024]{1,0:T(8,128)(2,1)}, bf16[4,128,512]{2,1,0:T(8,128)(2,1)}, bf16[4,128,512]{2,1,0:T(8,128)(2,1)}, bf16[4,128,512]{2,1,0:T(8,128)(2...) custom-call(bf16[512,1024]{1,0:T(8,128)(2,1)} %get-tuple-element.39.kv, ...), custom_call_target="tpu_custom_call" | custom-call | flops 2147483648 | bytes 9699328 | tf_op jit(solution)/shard_map/pallas_call | solution.py:35
  167.8 2.6 %shard_map.83._ = bf16[256,2048]{1,0:T(8,128)(2,1)} custom-call(bf16[512,1024]{1,0:T(8,128)(2,1)} %get-tuple-element.49.dkv, bf16[512,512]{1,0:T(8,128)(2,1)} %get-tuple-element.50.dq, bf16[512,512]{1,0:T(8,128)(2,1)} %get-tuple-element.51.out.o, bf16[4,128,512]{2,1,0:T(8,128)(2,1)} %get-tuple-element.52._), custom_call_target="tpu_custom_call" | custom-call | bytes 3670016 | tf_op jit(solution)/shard_map/pallas_call | solution.py:35
  170.4 2.1 collective-permute-start.18
  172.5 1.2 collective-permute-start.19
  173.7 3.4 %shard_map.85 = (bf16[4,128,512]{2,1,0:T(8,128)(2,1)}, bf16[4,128,512]{2,1,0:T(8,128)(2,1)}) custom-call(bf16[16,128,512]{2,1,0:T(8,128)(2,1)} %get-tuple-element.48.turned_hbm.turned, bf16[512,1024]{1,0:T(8,128)(2,1)} %get-tuple-element.49.dkv, bf16[256,2048]{1,0:T(8,128)(2,1)} %shard_map.83._), custom_call_target="tpu_custom_call" | custom-call | flops 536870912 | bytes 5242880 | tf_op jit(solution)/shard_map/pallas_call | solution.py:35
  177.1 20.3 %collective-permute-done.17.refs_1_ = bf16[4,128,512]{2,1,0:T(8,128)(2,1)S(1)} collective-permute-done((bf16[4,128,512]{2,1,0:T(8,128)(2,1)}, bf16[4,128,512]{2,1,0:T(8,128)(2,1)S(1)}, u32[]{:S(2)}, u32[]{:S(2)}) %collective-permute-start.17) | collective-permute-done | bytes 524320 | tf_op jit(solution)/shard_map/ppermute | solution.py:47
  197.4 11.0 %collective-permute-start.21 = (bf16[4,128,512]{2,1,0:T(8,128)(2,1)}, bf16[4,128,512]{2,1,0:T(8,128)(2,1)}, u32[]{:S(2)}, u32[]{:S(2)}) collective-permute-start(bf16[4,128,512]{2,1,0:T(8,128)(2,1)} %get-tuple-element.62), channel_id=1, source_target_pairs={{0,128},{64,192},{128,0},{192,64},{1,129},{65,193},{129,1},{193,65... | collective-permute-start | bytes 1572872 | tf_op jit(solution)/shard_map/ppermute | solution.py:47
  208.4 9.8 %shard_map.84 = (bf16[256,2048]{1,0:T(8,128)(2,1)}, bf16[256,1024]{1,0:T(8,128)(2,1)}, bf16[256,1024]{1,0:T(8,128)(2,1)}) custom-call(bf16[512,1024]{1,0:T(8,128)(2,1)} %get-tuple-element.49.dkv, bf16[256,2048]{1,0:T(8,128)(2,1)} %collective-permute-done.15.got, bf16[512,512]{1,0:T(8,128)(2,1)} %get-tuple-element.51.out.o, ...), custom_call_target="tpu_custom_call" | custom-call | flops 8589934592 | bytes 12582912 | tf_op jit(solution)/shard_map/pallas_call | solution.py:291
  218.2 5.5 %collective-permute-done.20.refs_5_ = bf16[4,128,512]{2,1,0:T(8,128)(2,1)} collective-permute-done((bf16[4,128,512]{2,1,0:T(8,128)(2,1)}, bf16[4,128,512]{2,1,0:T(8,128)(2,1)}, u32[]{:S(2)}, u32[]{:S(2)}) %collective-permute-start.20) | collective-permute-done | bytes 524320 | tf_op jit(solution)/shard_map/ppermute | solution.py:47
  223.7 0.7 collective-permute-done.22.refs_7_
  224.3 0.8 copy-done.9
  225.1 3.6 %shard_map.86 = (f32[128,512]{1,0:T(8,128)}, bf16[128,512]{1,0:T(8,128)(2,1)}, bf16[128,512]{1,0:T(8,128)(2,1)}, bf16[128,512]{1,0:T(8,128)(2,1)}, f32[128,512]{...) custom-call(bf16[4,128,512]{2,1,0:T(8,128)(2,1)} %get-tuple-element.57.refs_0_, ...), custom_call_target="tpu_custom_call" | custom-call | bytes 6553600 | tf_op jit(solution)/shard_map/pallas_call | solution.py:35
  229.0 3.6 %collective-permute-start.24 = (bf16[128,512]{1,0:T(8,128)(2,1)}, bf16[128,512]{1,0:T(8,128)(2,1)S(1)}, u32[]{:S(2)}, u32[]{:S(2)}) collective-permute-start(bf16[128,512]{1,0:T(8,128)(2,1)} %get-tuple-element.66), channel_id=1, source_target_pairs={{0,128},{64,192},{128,0},{192,64},{1,129},{65,193},{129,1},{193,65... | collective-permute-start | bytes 393224 | tf_op jit(solution)/shard_map/ppermute | solution.py:47
  232.7 1.0 collective-permute-start.27
  233.7 1.6 collective-permute-done.23.refs_1_
  235.2 0.8 collective-permute-start.28
  236.0 1.2 collective-permute-done.24.refs_2_
  237.2 0.6 collective-permute-done.25.refs_3_
  237.9 2.6 %collective-permute-done.26.refs_5_ = bf16[128,512]{1,0:T(8,128)(2,1)S(1)} collective-permute-done((bf16[128,512]{1,0:T(8,128)(2,1)}, bf16[128,512]{1,0:T(8,128)(2,1)S(1)}, u32[]{:S(2)}, u32[]{:S(2)}) %collective-permute-start.26) | collective-permute-done | bytes 131104 | tf_op jit(solution)/shard_map/ppermute | solution.py:47
  240.5 0.9 collective-permute-done.28.refs_7_
  242.0 2.1 shard_map.87
  244.2 14.7 %all_to_all.31.i = bf16[16,8,1024]{2,1,0:T(8,128)(2,1)} all-to-all(bf16[16,8,1024]{2,1,0:T(8,128)(2,1)} %shard_map.87), channel_id=1, replica_groups=mesh['y'=4,'x'=4,'core'=2,'z'=8] {'core','z'}, dimensions={0} | all-to-all | bytes 524288 | tf_op jit(solution)/shard_map/all_to_all | solution.py:418
  258.8 1.6 shard_map.88
  (72 shorter events, 3.5 us)
Async XLA Ops:
  0.6 1.2 copy-start
  2.9 18.6 %all-to-all-start = ((bf16[8,16,1024]{2,1,0:T(8,128)(2,1)}), bf16[8,16,1024]{2,1,0:T(8,128)(2,1)S(1)}, u32[]{:S(2)}, u32[]{:S(2)}) async-start(bf16[8,16,1024]{2,1,0:T(8,128)(2,1)} %broadcast_in_dim.8), calls=%async_computation | async-start | bytes 524288 | tf_op jit(solution)/shard_map/all_to_all | solution.py:316
  9.6 53.9 %collective-permute-start = (bf16[256,2048]{1,0:T(8,128)(2,1)}, bf16[256,2048]{1,0:T(8,128)(2,1)S(1)}, u32[]{:S(2)}, u32[]{:S(2)}) collective-permute-start(bf16[256,2048]{1,0:T(8,128)(2,1)} %own.1), channel_id=1, source_target_pairs={{0,8},{8,0},{1,9},{9,1},{2,10},{10,2},{3,11},{11,3},{4,12},{12,4},... | collective-permute-start | bytes 3145736 | tf_op jit(solution)/shard_map/ppermute | solution.py:308
  21.6 7.1 %collective-permute-start.2 = (bf16[8,16,512]{2,1,0:T(8,128)(2,1)S(1)}, bf16[8,16,512]{2,1,0:T(8,128)(2,1)S(1)}, u32[]{:S(2)}, u32[]{:S(2)}) collective-permute-start(bf16[8,16,512]{2,1,0:T(8,128)(2,1)S(1)} %get-tuple-element.75), channel_id=1, source_target_pairs={{0,32},{16,48},{32,0},{48,16},{1,33},{17,49},{33,1},{49,17},{2,34}... | collective-permute-start | bytes 393224 | tf_op jit(solution)/shard_map/ppermute | solution.py:47
  24.7 6.2 %collective-permute-start.1 = (bf16[8,16,512]{2,1,0:T(8,128)(2,1)S(1)}, bf16[8,16,512]{2,1,0:T(8,128)(2,1)S(1)}, u32[]{:S(2)}, u32[]{:S(2)}) collective-permute-start(bf16[8,16,512]{2,1,0:T(8,128)(2,1)S(1)} %get-tuple-element.75), channel_id=1, source_target_pairs={{0,16},{16,32},{32,48},{48,0},{1,17},{17,33},{33,49},{49,1},{2,18}... | collective-permute-start | bytes 393224 | tf_op jit(solution)/shard_map/ppermute | solution.py:47
  25.3 5.6 %collective-permute-start.3 = (bf16[8,16,512]{2,1,0:T(8,128)(2,1)S(1)}, bf16[8,16,512]{2,1,0:T(8,128)(2,1)S(1)}, u32[]{:S(2)}, u32[]{:S(2)}) collective-permute-start(bf16[8,16,512]{2,1,0:T(8,128)(2,1)S(1)} %get-tuple-element.75), channel_id=1, source_target_pairs={{0,48},{16,0},{32,16},{48,32},{1,49},{17,1},{33,17},{49,33},{2,50}... | collective-permute-start | bytes 393224 | tf_op jit(solution)/shard_map/ppermute | solution.py:47
  30.9 49.0 %copy-start.11 = (bf16[4,8,16,512]{3,2,1,0:T(8,128)(2,1)}, bf16[4,8,16,512]{3,2,1,0:T(8,128)(2,1)S(1)}, u32[]{:S(2)}) copy-start(bf16[4,8,16,512]{3,2,1,0:T(8,128)(2,1)S(1)} %pad_maximum_fusion.refs_0_) | copy-start | bytes 1572868
  30.9 32.6 %collective-permute-start.6 = (bf16[4,8,16,512]{3,2,1,0:T(8,128)(2,1)S(1)}, bf16[4,8,16,512]{3,2,1,0:T(8,128)(2,1)S(1)}, u32[]{:S(2)}, u32[]{:S(2)}) collective-permute-start(bf16[4,8,16,512]{3,2,1,0:T(8,128)(2,1)S(1)} %pad_maximum_fusion.refs_0_), channel_id=1, source_target_pairs={{0,192},{64,0},{128,64},{192,128},{1,193},{65,1},{129,65},{193,129... | collective-permute-start | bytes 1572872 | tf_op jit(solution)/shard_map/ppermute | solution.py:47
  34.0 6.6 %collective-permute-start.8 = (bf16[8,16,512]{2,1,0:T(8,128)(2,1)S(1)}, bf16[8,16,512]{2,1,0:T(8,128)(2,1)S(1)}, u32[]{:S(2)}, u32[]{:S(2)}) collective-permute-start(bf16[8,16,512]{2,1,0:T(8,128)(2,1)S(1)} %get-tuple-element.74), channel_id=1, source_target_pairs={{0,128},{64,192},{128,0},{192,64},{1,129},{65,193},{129,1},{193,65... | collective-permute-start | bytes 393224 | tf_op jit(solution)/shard_map/ppermute | solution.py:47
  34.7 7.7 %collective-permute-start.7 = (bf16[8,16,512]{2,1,0:T(8,128)(2,1)S(1)}, bf16[8,16,512]{2,1,0:T(8,128)(2,1)S(1)}, u32[]{:S(2)}, u32[]{:S(2)}) collective-permute-start(bf16[8,16,512]{2,1,0:T(8,128)(2,1)S(1)} %get-tuple-element.74), channel_id=1, source_target_pairs={{0,64},{64,128},{128,192},{192,0},{1,65},{65,129},{129,193},{193,1... | collective-permute-start | bytes 393224 | tf_op jit(solution)/shard_map/ppermute | solution.py:47
  35.6 24.7 %collective-permute-start.9 = (bf16[8,16,512]{2,1,0:T(8,128)(2,1)S(1)}, bf16[8,16,512]{2,1,0:T(8,128)(2,1)S(1)}, u32[]{:S(2)}, u32[]{:S(2)}) collective-permute-start(bf16[8,16,512]{2,1,0:T(8,128)(2,1)S(1)} %get-tuple-element.74), channel_id=1, source_target_pairs={{0,192},{64,0},{128,64},{192,128},{1,193},{65,1},{129,65},{193,129... | collective-permute-start | bytes 393224 | tf_op jit(solution)/shard_map/ppermute | solution.py:47
  40.6 28.9 %collective-permute-start.5 = (bf16[4,8,16,512]{3,2,1,0:T(8,128)(2,1)S(1)}, bf16[4,8,16,512]{3,2,1,0:T(8,128)(2,1)}, u32[]{:S(2)}, u32[]{:S(2)}) collective-permute-start(bf16[4,8,16,512]{3,2,1,0:T(8,128)(2,1)S(1)} %pad_maximum_fusion.refs_0_), channel_id=1, source_target_pairs={{0,128},{64,192},{128,0},{192,64},{1,129},{65,193},{129,1},{193,65... | collective-permute-start | bytes 1572872 | tf_op jit(solution)/shard_map/ppermute | solution.py:47
  42.4 27.1 %collective-permute-start.4 = (bf16[4,8,16,512]{3,2,1,0:T(8,128)(2,1)S(1)}, bf16[4,8,16,512]{3,2,1,0:T(8,128)(2,1)}, u32[]{:S(2)}, u32[]{:S(2)}) collective-permute-start(bf16[4,8,16,512]{3,2,1,0:T(8,128)(2,1)S(1)} %pad_maximum_fusion.refs_0_), channel_id=1, source_target_pairs={{0,64},{64,128},{128,192},{192,0},{1,65},{65,129},{129,193},{193,1... | collective-permute-start | bytes 1572872 | tf_op jit(solution)/shard_map/ppermute | solution.py:47
  60.5 19.5 %copy-start.12 = (bf16[4,8,16,512]{3,2,1,0:T(8,128)(2,1)}, bf16[4,8,16,512]{3,2,1,0:T(8,128)(2,1)S(1)}, u32[]{:S(2)}) copy-start(bf16[4,8,16,512]{3,2,1,0:T(8,128)(2,1)S(1)} %pad_maximum_fusion.1.refs_4_) | copy-start | bytes 1572868
  60.5 15.3 %collective-permute-start.12 = (bf16[4,8,16,512]{3,2,1,0:T(8,128)(2,1)S(1)}, bf16[4,8,16,512]{3,2,1,0:T(8,128)(2,1)}, u32[]{:S(2)}, u32[]{:S(2)}) collective-permute-start(bf16[4,8,16,512]{3,2,1,0:T(8,128)(2,1)S(1)} %pad_maximum_fusion.1.refs_4_), channel_id=1, source_target_pairs={{0,48},{16,0},{32,16},{48,32},{1,49},{17,1},{33,17},{49,33},{2,50}... | collective-permute-start | bytes 1572872 | tf_op jit(solution)/shard_map/ppermute | solution.py:47
  63.5 1.8 copy-start.5
  63.5 12.3 %collective-permute-start.11 = (bf16[4,8,16,512]{3,2,1,0:T(8,128)(2,1)S(1)}, bf16[4,8,16,512]{3,2,1,0:T(8,128)(2,1)}, u32[]{:S(2)}, u32[]{:S(2)}) collective-permute-start(bf16[4,8,16,512]{3,2,1,0:T(8,128)(2,1)S(1)} %pad_maximum_fusion.1.refs_4_), channel_id=1, source_target_pairs={{0,32},{16,48},{32,0},{48,16},{1,33},{17,49},{33,1},{49,17},{2,34}... | collective-permute-start | bytes 1572872 | tf_op jit(solution)/shard_map/ppermute | solution.py:47
  63.5 0.8 copy-start.21
  64.4 15.5 %collective-permute-start.10 = (bf16[4,8,16,512]{3,2,1,0:T(8,128)(2,1)S(1)}, bf16[4,8,16,512]{3,2,1,0:T(8,128)(2,1)}, u32[]{:S(2)}, u32[]{:S(2)}) collective-permute-start(bf16[4,8,16,512]{3,2,1,0:T(8,128)(2,1)S(1)} %pad_maximum_fusion.1.refs_4_), channel_id=1, source_target_pairs={{0,16},{16,32},{32,48},{48,0},{1,17},{17,33},{33,49},{49,1},{2,18}... | collective-permute-start | bytes 1572872 | tf_op jit(solution)/shard_map/ppermute | solution.py:47
  79.9 11.7 %copy-start.2 = (bf16[256,1024]{1,0:T(8,128)(2,1)S(1)}, bf16[256,1024]{1,0:T(8,128)(2,1)}, u32[]{:S(2)}) copy-start(bf16[256,1024]{1,0:T(8,128)(2,1)} %q_own.1) | copy-start | bytes 1572868
  88.0 120.4 %collective-permute-start.16 = (bf16[8,16,16,1024]{3,2,1,0:T(8,128)(2,1)}, bf16[8,16,16,1024]{3,2,1,0:T(8,128)(2,1)}, u32[]{:S(2)}, u32[]{:S(2)}) collective-permute-start(bf16[8,16,16,1024]{3,2,1,0:T(8,128)(2,1)} %get-tuple-element.53.w), channel_id=1, source_target_pairs={{0,8},{8,0},{1,9},{9,1},{2,10},{10,2},{3,11},{11,3},{4,12},{12,4},... | collective-permute-start | bytes 12582920 | tf_op jit(solution)/shard_map/ppermute | solution.py:308
  88.1 16.1 %all-to-all-start.1 = ((bf16[8,128,128]{2,1,0:T(8,128)(2,1)}), bf16[8,128,128]{2,1,0:T(8,128)(2,1)S(1)}, u32[]{:S(2)}, u32[]{:S(2)}) async-start(bf16[8,128,128]{2,1,0:T(8,128)(2,1)} %get-tuple-element.44), calls=%async_computation.1 | async-start | bytes 524288 | tf_op jit(solution)/shard_map/all_to_all | solution.py:350
  91.6 18.5 %copy-start.3 = (bf16[256,1024]{1,0:T(8,128)(2,1)S(1)}, bf16[256,1024]{1,0:T(8,128)(2,1)}, u32[]{:S(2)}) copy-start(bf16[256,1024]{1,0:T(8,128)(2,1)} %g_own.1) | copy-start | bytes 1572868
  91.6 4.2 %collective-permute-start.13 = (bf16[256,512]{1,0:T(8,128)(2,1)S(1)}, bf16[256,512]{1,0:T(8,128)(2,1)S(1)}, u32[]{:S(2)}, u32[]{:S(2)}) collective-permute-start(bf16[256,512]{1,0:T(8,128)(2,1)S(1)} %constant_dynamic-slice_fusion.1), channel_id=1, source_target_pairs={{0,8},{8,0},{1,9},{9,1},{2,10},{10,2},{3,11},{11,3},{4,12},{12,4},... | collective-permute-start | bytes 786440 | tf_op jit(solution)/shard_map/ppermute | solution.py:308
  95.9 0.7 copy-start.14
  104.3 0.7 copy-start.6
  106.7 15.7 %all-to-all-start.2 = ((bf16[8,128,128]{2,1,0:T(8,128)(2,1)}), bf16[8,128,128]{2,1,0:T(8,128)(2,1)S(1)}, u32[]{:S(2)}, u32[]{:S(2)}) async-start(bf16[8,128,128]{2,1,0:T(8,128)(2,1)} %shard_map.78), calls=%async_computation.2 | async-start | bytes 524288 | tf_op jit(solution)/shard_map/all_to_all | solution.py:354
  110.2 1.6 collective-permute-start.14
  111.8 10.6 %copy-start.13 = (bf16[256,512]{1,0:T(8,128)(2,1)}, bf16[256,512]{1,0:T(8,128)(2,1)S(1)}, u32[]{:S(2)}) copy-start(bf16[256,512]{1,0:T(8,128)(2,1)S(1)} %collective-permute-done.14.g_sib) | copy-start | bytes 786436
  122.4 0.7 copy-start.1
  127.0 15.6 %all-to-all-start.3 = ((bf16[8,128,128]{2,1,0:T(8,128)(2,1)}), bf16[8,128,128]{2,1,0:T(8,128)(2,1)S(1)}, u32[]{:S(2)}, u32[]{:S(2)}) async-start(bf16[8,128,128]{2,1,0:T(8,128)(2,1)} %get-tuple-element.47), calls=%async_computation.3 | async-start | bytes 524288 | tf_op jit(solution)/shard_map/all_to_all | solution.py:350
  142.5 0.7 copy-start.4
  167.8 2.6 %copy-start.7 = (bf16[4,128,512]{2,1,0:T(8,128)(2,1)S(1)}, bf16[4,128,512]{2,1,0:T(8,128)(2,1)}, u32[]{:S(2)}) copy-start(bf16[4,128,512]{2,1,0:T(8,128)(2,1)} %get-tuple-element.52._) | copy-start | bytes 1572868
  170.4 27.0 %collective-permute-start.15 = (bf16[256,2048]{1,0:T(8,128)(2,1)}, bf16[256,2048]{1,0:T(8,128)(2,1)}, u32[]{:S(2)}, u32[]{:S(2)}) collective-permute-start(bf16[256,2048]{1,0:T(8,128)(2,1)} %shard_map.83._), channel_id=1, source_target_pairs={{0,8},{8,0},{1,9},{9,1},{2,10},{10,2},{3,11},{11,3},{4,12},{12,4},... | collective-permute-start | bytes 3145736 | tf_op jit(solution)/shard_map/ppermute | solution.py:308
  170.4 27.0 %collective-permute-start.17 = (bf16[4,128,512]{2,1,0:T(8,128)(2,1)}, bf16[4,128,512]{2,1,0:T(8,128)(2,1)S(1)}, u32[]{:S(2)}, u32[]{:S(2)}) collective-permute-start(bf16[4,128,512]{2,1,0:T(8,128)(2,1)} %get-tuple-element.58), channel_id=1, source_target_pairs={{0,16},{16,32},{32,48},{48,0},{1,17},{17,33},{33,49},{49,1},{2,18}... | collective-permute-start | bytes 1572872 | tf_op jit(solution)/shard_map/ppermute | solution.py:47
  170.4 53.9 %collective-permute-start.18 = (bf16[4,128,512]{2,1,0:T(8,128)(2,1)S(1)}, bf16[4,128,512]{2,1,0:T(8,128)(2,1)S(1)}, u32[]{:S(2)}, u32[]{:S(2)}) collective-permute-start(bf16[4,128,512]{2,1,0:T(8,128)(2,1)S(1)} %copy-done.7), channel_id=1, source_target_pairs={{0,32},{16,48},{32,0},{48,16},{1,33},{17,49},{33,1},{49,17},{2,34}... | collective-permute-start | bytes 1572872 | tf_op jit(solution)/shard_map/ppermute | solution.py:47
  172.5 45.7 %collective-permute-start.19 = (bf16[4,128,512]{2,1,0:T(8,128)(2,1)}, bf16[4,128,512]{2,1,0:T(8,128)(2,1)S(1)}, u32[]{:S(2)}, u32[]{:S(2)}) collective-permute-start(bf16[4,128,512]{2,1,0:T(8,128)(2,1)} %get-tuple-element.59), channel_id=1, source_target_pairs={{0,48},{16,0},{32,16},{48,32},{1,49},{17,1},{33,17},{49,33},{2,50}... | collective-permute-start | bytes 1572872 | tf_op jit(solution)/shard_map/ppermute | solution.py:47
  197.4 20.7 %copy-start.8 = (bf16[4,128,512]{2,1,0:T(8,128)(2,1)}, bf16[4,128,512]{2,1,0:T(8,128)(2,1)S(1)}, u32[]{:S(2)}) copy-start(bf16[4,128,512]{2,1,0:T(8,128)(2,1)S(1)} %collective-permute-done.17.refs_1_) | copy-start | bytes 1572868
  197.4 26.2 %collective-permute-start.20 = (bf16[4,128,512]{2,1,0:T(8,128)(2,1)}, bf16[4,128,512]{2,1,0:T(8,128)(2,1)}, u32[]{:S(2)}, u32[]{:S(2)}) collective-permute-start(bf16[4,128,512]{2,1,0:T(8,128)(2,1)} %get-tuple-element.61), channel_id=1, source_target_pairs={{0,64},{64,128},{128,192},{192,0},{1,65},{65,129},{129,193},{193,1... | collective-permute-start | bytes 1572872 | tf_op jit(solution)/shard_map/ppermute | solution.py:47
  197.4 26.2 %collective-permute-start.21 = (bf16[4,128,512]{2,1,0:T(8,128)(2,1)}, bf16[4,128,512]{2,1,0:T(8,128)(2,1)}, u32[]{:S(2)}, u32[]{:S(2)}) collective-permute-start(bf16[4,128,512]{2,1,0:T(8,128)(2,1)} %get-tuple-element.62), channel_id=1, source_target_pairs={{0,128},{64,192},{128,0},{192,64},{1,129},{65,193},{129,1},{193,65... | collective-permute-start | bytes 1572872 | tf_op jit(solution)/shard_map/ppermute | solution.py:47
  208.4 15.9 %collective-permute-start.22 = (bf16[4,128,512]{2,1,0:T(8,128)(2,1)}, bf16[4,128,512]{2,1,0:T(8,128)(2,1)}, u32[]{:S(2)}, u32[]{:S(2)}) collective-permute-start(bf16[4,128,512]{2,1,0:T(8,128)(2,1)} %get-tuple-element.63), channel_id=1, source_target_pairs={{0,192},{64,0},{128,64},{192,128},{1,193},{65,1},{129,65},{193,129... | collective-permute-start | bytes 1572872 | tf_op jit(solution)/shard_map/ppermute | solution.py:47
  218.2 6.2 %copy-start.10 = (bf16[4,128,512]{2,1,0:T(8,128)(2,1)}, bf16[4,128,512]{2,1,0:T(8,128)(2,1)S(1)}, u32[]{:S(2)}) copy-start(bf16[4,128,512]{2,1,0:T(8,128)(2,1)S(1)} %collective-permute-done.19.refs_3_) | copy-start | bytes 1572868
  224.3 0.8 copy-start.9
  228.8 6.5 %collective-permute-start.23 = (bf16[128,512]{1,0:T(8,128)(2,1)}, bf16[128,512]{1,0:T(8,128)(2,1)S(1)}, u32[]{:S(2)}, u32[]{:S(2)}) collective-permute-start(bf16[128,512]{1,0:T(8,128)(2,1)} %get-tuple-element.65), channel_id=1, source_target_pairs={{0,64},{64,128},{128,192},{192,0},{1,65},{65,129},{129,193},{193,1... | collective-permute-start | bytes 393224 | tf_op jit(solution)/shard_map/ppermute | solution.py:47
  229.0 8.2 %collective-permute-start.24 = (bf16[128,512]{1,0:T(8,128)(2,1)}, bf16[128,512]{1,0:T(8,128)(2,1)S(1)}, u32[]{:S(2)}, u32[]{:S(2)}) collective-permute-start(bf16[128,512]{1,0:T(8,128)(2,1)} %get-tuple-element.66), channel_id=1, source_target_pairs={{0,128},{64,192},{128,0},{192,64},{1,129},{65,193},{129,1},{193,65... | collective-permute-start | bytes 393224 | tf_op jit(solution)/shard_map/ppermute | solution.py:47
  232.7 5.2 %collective-permute-start.25 = (bf16[128,512]{1,0:T(8,128)(2,1)}, bf16[128,512]{1,0:T(8,128)(2,1)S(1)}, u32[]{:S(2)}, u32[]{:S(2)}) collective-permute-start(bf16[128,512]{1,0:T(8,128)(2,1)} %get-tuple-element.67), channel_id=1, source_target_pairs={{0,192},{64,0},{128,64},{192,128},{1,193},{65,1},{129,65},{193,129... | collective-permute-start | bytes 393224 | tf_op jit(solution)/shard_map/ppermute | solution.py:47
  232.7 7.8 %collective-permute-start.26 = (bf16[128,512]{1,0:T(8,128)(2,1)}, bf16[128,512]{1,0:T(8,128)(2,1)S(1)}, u32[]{:S(2)}, u32[]{:S(2)}) collective-permute-start(bf16[128,512]{1,0:T(8,128)(2,1)} %get-tuple-element.69), channel_id=1, source_target_pairs={{0,16},{16,32},{32,48},{48,0},{1,17},{17,33},{33,49},{49,1},{2,18}... | collective-permute-start | bytes 393224 | tf_op jit(solution)/shard_map/ppermute | solution.py:47
  232.7 7.8 %collective-permute-start.27 = (bf16[128,512]{1,0:T(8,128)(2,1)}, bf16[128,512]{1,0:T(8,128)(2,1)S(1)}, u32[]{:S(2)}, u32[]{:S(2)}) collective-permute-start(bf16[128,512]{1,0:T(8,128)(2,1)} %get-tuple-element.70), channel_id=1, source_target_pairs={{0,32},{16,48},{32,0},{48,16},{1,33},{17,49},{33,1},{49,17},{2,34}... | collective-permute-start | bytes 393224 | tf_op jit(solution)/shard_map/ppermute | solution.py:47
  235.2 6.2 %copy-start.15 = (bf16[128,512]{1,0:T(8,128)(2,1)}, bf16[128,512]{1,0:T(8,128)(2,1)S(1)}, u32[]{:S(2)}) copy-start(bf16[128,512]{1,0:T(8,128)(2,1)S(1)} %collective-permute-done.23.refs_1_) | copy-start | bytes 393220
  235.2 6.2 %collective-permute-start.28 = (bf16[128,512]{1,0:T(8,128)(2,1)}, bf16[128,512]{1,0:T(8,128)(2,1)S(1)}, u32[]{:S(2)}, u32[]{:S(2)}) collective-permute-start(bf16[128,512]{1,0:T(8,128)(2,1)} %get-tuple-element.71), channel_id=1, source_target_pairs={{0,48},{16,0},{32,16},{48,32},{1,49},{17,1},{33,17},{49,33},{2,50}... | collective-permute-start | bytes 393224 | tf_op jit(solution)/shard_map/ppermute | solution.py:47
  237.2 4.2 %copy-start.16 = (bf16[128,512]{1,0:T(8,128)(2,1)}, bf16[128,512]{1,0:T(8,128)(2,1)S(1)}, u32[]{:S(2)}) copy-start(bf16[128,512]{1,0:T(8,128)(2,1)S(1)} %collective-permute-done.24.refs_2_) | copy-start | bytes 393220
  237.9 3.5 %copy-start.17 = (bf16[128,512]{1,0:T(8,128)(2,1)}, bf16[128,512]{1,0:T(8,128)(2,1)S(1)}, u32[]{:S(2)}) copy-start(bf16[128,512]{1,0:T(8,128)(2,1)S(1)} %collective-permute-done.25.refs_3_) | copy-start | bytes 393220
  240.5 0.9 copy-start.18
  240.5 0.9 copy-start.19
  241.4 0.7 copy-start.20
where the time goes:
time: 264 us; the launch traced here: 260 us
  waiting for transfers between devices  97.6 us (37%)
  starting transfers between devices  64.3 us (24%)
  Pallas kernels  59.7 us (23%)
  blocking collectives  30.4 us (12%)
  local copies, waits for them, and re-layouts  7.45 us (3%)
    ppermute x24, waiting for transfers between devices, shift(): return lax.ppermute(x, axis, [(i, (i + step) % size) for i in range(size)])  59.9 us
    pallas_call x13, Pallas kernels, call(): pl.pallas_call(body, out_shape=[jax.ShapeDtypeStruct(s, d) for s, d in ou...  49.9 us
    ppermute x24, starting transfers between devices, shift(): return lax.ppermute(x, axis, [(i, (i + step) % size) for i in range(size)])  46.5 us
    all_to_all x1, blocking collectives, exchange(): return lax.all_to_all(x, 'z', 0, 0, tiled=True)  15.7 us
    all_to_all x1, blocking collectives, on_device(): column = lax.all_to_all(column, ('core', 'z'), 0, 0, tiled=True)  14.7 us
    all_to_all x1, waiting for transfers between devices, on_device(): lax.all_to_all(jnp.broadcast_to(mine[None], (8, 16, 1024)), 'z', 0, 0, ti...  11.9 us
    all_to_all x1, waiting for transfers between devices, exchange(): return lax.all_to_all(x, 'z', 0, 0, tiled=True)  10.6 us
    all_to_all x2, waiting for transfers between devices, exchange(): x = lax.all_to_all(x, 'z', 0, 0, tiled=True)  10.1 us
  transfers between devices with their start and end apart: 33, of which 21 were waited for; matrix products, arithmetic and copies ran while one was open for 0% of the time, Pallas kernels for 17%

commit v1 on v0

--- a/solution.py
+++ b/solution.py
@@ -50,14 +50,51 @@
 def turn_kernel(own, sib, both, turned):
     both[:256] = own[...]
     both[256:] = sib[...]
-    for n in range(16):
-        at = slice(n * HD, n * HD + HD)
+
+    def step(n, _):
+        at = pl.ds(pl.multiple_of(n * HD, HD), HD)
         turned[n, :, :256] = own[:, at].T
         turned[n, :, 256:] = sib[:, at].T
-
-
-def key_value_kernel(tok, *refs):
-    pieces, (w_out, kv, state, w_ref, sems, out_sems) = refs[:8], refs[8:]
+        return 0
+
+    lax.fori_loop(0, 16, step, 0)
+
+
+def project(tok, w_ref, out):
+    def tile(n, _):
+        at = pl.ds(pl.multiple_of(n * 256, 256), 256)
+        if len(w_ref.shape) == 4:
+            w = w_ref[:, :, :, at].reshape(2048, 256)
+        else:
+            w = w_ref[:, :, at].reshape(2048, 256)
+        out[:, at] = dot(tok[...], w, 1, 0).astype(BF)
+        return 0
+
+    lax.fori_loop(0, 2, tile, 0)
+
+
+def key_kernel(tok, *refs):
+    shards, (w_out, key, w_ref, sems, out_sem) = refs[:9], refs[9:]
+    z = lax.axis_index("z")
+    copies = []
+    for n, step in enumerate((0, -1, 1, -2, 2, -3, 3)):
+        to = w_ref.at[lax.rem(z + step + 8, 8)]
+        copies.append(pltpu.make_async_copy(shards[n], to, sems.at[n]))
+    for n in range(2):
+        to = w_ref.at[lax.rem(z + 4, 8), pl.ds(n * 128, 128)]
+        copies.append(pltpu.make_async_copy(shards[7 + n], to, sems.at[7 + n]))
+    for c in copies:
+        c.start()
+    for c in copies:
+        c.wait()
+    store = pltpu.make_async_copy(w_ref, w_out, out_sem)
+    store.start()
+    project(tok, w_ref, key)
+    store.wait()
+
+
+def value_kernel(tok, key, *refs):
+    pieces, (w_out, val, state, w_ref, sems, out_sem) = refs[:8], refs[8:]
     y, x = lax.axis_index("y"), lax.axis_index("x")
     copies = []
     for half in range(2):
@@ -68,39 +105,24 @@
                 copies.append(
                     pltpu.make_async_copy(
                         pieces[half * 4 + e].at[d],
-                        w_ref.at[:, place, :, pl.ds(half * 512, 512)],
+                        w_ref.at[:, place, :, pl.ds(half * 256, 256)],
                         sems.at[len(copies)],
                     )
                 )
     for c in copies:
         c.start()
-    stored = []
-    for half in range(2):
-        for c in copies[half * 16 : half * 16 + 16]:
-            c.wait()
-        at = pl.ds(half * 512, 512)
-        stored.append(
-            pltpu.make_async_copy(
-                w_ref.at[:, :, :, at], w_out.at[:, :, :, at], out_sems.at[half]
-            )
-        )
-        stored[-1].start()
-
-        def tile(n, _):
-            at = pl.ds(pl.multiple_of(n * 256, 256), 256)
-            w = w_ref[:, :, :, at].reshape(2048, 256)
-            kv[:, at] = dot(tok[...], w, 1, 0).astype(BF)
-            return 0
-
-        lax.fori_loop(half * 2, half * 2 + 2, tile, 0)
-    for s in range(2):
-        rows = slice(s * 256, s * 256 + 256)
-        for h in range(4):
-            k = feature(kv[rows, h * HD : (h + 1) * HD].astype(F32)).astype(BF)
-            v = kv[rows, 512 + h * HD : 512 + (h + 1) * HD]
-            state[s * 4 + h] = dot(k, v, 0, 0).astype(BF)
-    for c in stored:
+    for c in copies:
         c.wait()
+    project(tok, w_ref, val)
+    store = pltpu.make_async_copy(w_ref, w_out, out_sem)
+    store.start()
+
+    def body(n, rows, at):
+        k = feature(key[rows, at].astype(F32)).astype(BF)
+        state[n] = dot(k, val[rows, at], 0, 0).astype(BF)
+
+    each_spot(body)
+    store.wait()
 
 
 def sums_kernel(later, states, out):
@@ -118,62 +140,70 @@
     return lax.broadcasted_iota(jnp.int32, shape, 0) >= lax.broadcasted_iota(jnp.int32, shape, 1)
 
 
-def spots():
-    for s in range(2):
-        for h in range(4):
-            rows = slice(s * 256, s * 256 + 256)
-            yield (
-                s * 4 + h,
-                rows,
-                slice(h * HD, (h + 1) * HD),
-                slice(512 + h * HD, 512 + (h + 1) * HD),
-            )
-
-
-def local_kernel(q_own, q_sib, kv, qu, qf, scores, local):
+def each_spot(body):
+    def step(h, _):
+        for s in range(2):
+            at = pl.ds(pl.multiple_of(h * HD, HD), HD)
+            body(s * 4 + h, slice(s * 256, s * 256 + 256), at)
+        return 0
+
+    lax.fori_loop(0, 4, step, 0)
+
+
+def local_kernel(q_own, q_sib, key, val, qu, qf, scores, local):
     mask = causal()
     at = lax.axis_index("core") * 512
     qu[:256] = q_own[:, pl.ds(pl.multiple_of(at, 512), 512)]
     qu[256:] = q_sib[...]
-    for n, rows, at, vat in spots():
+
+    def body(n, rows, at):
         q = feature(qu[rows, at].astype(F32)).astype(BF)
         qf[rows, at] = q
-        k = feature(kv[rows, at].astype(F32)).astype(BF)
+        k = feature(key[rows, at].astype(F32)).astype(BF)
         score = jnp.where(mask, dot(q, k, 1, 1), 0.0).astype(BF)
         scores[n] = score
-        local[rows, at] = dot(score, kv[rows, vat], 1, 0)
+        local[rows, at] = dot(score, val[rows, at], 1, 0)
+
+    each_spot(body)
 
 
 def forward_kernel(qf, g_own, g_sib, local, before, out, grad_att, state):
     core = lax.axis_index("core")
-    for n, rows, at, _ in spots():
-        q = qf[rows, at]
-        attended = local[rows, at] + dot(q, before[n], 1, 0)
-        if n < 4:
-            g = g_own[:, pl.ds(pl.multiple_of(core * 512 + n * HD, HD), HD)].astype(F32)
-        else:
-            g = g_sib[:, at].astype(F32)
-        power = jnp.mean(attended * attended, axis=-1, keepdims=True) + EPSILON
-        inverse = lax.rsqrt(power)
-        normed = attended * inverse
-        along = jnp.mean(g * normed, axis=-1, keepdims=True)
-        grad = ((g - normed * along) * inverse).astype(BF)
-        out[rows, at] = normed.astype(BF)
-        grad_att[rows, at] = grad
-        state[n] = dot(q, grad, 0, 0).astype(BF)
-
-
-def mixed_kernel(qu, qf, kv, scores, grad_att, before, dq, local):
+
+    def step(h, _):
+        at = pl.ds(pl.multiple_of(h * HD, HD), HD)
+        mine = pl.ds(pl.multiple_of(core * 512 + h * HD, HD), HD)
+        for s, (g_ref, g_at) in enumerate(((g_own, mine), (g_sib, at))):
+            n, rows = s * 4 + h, slice(s * 256, s * 256 + 256)
+            q, g = qf[rows, at], g_ref[:, g_at].astype(F32)
+            attended = local[rows, at] + dot(q, before[n], 1, 0)
+            power = jnp.mean(attended * attended, axis=-1, keepdims=True) + EPSILON
+            inverse = lax.rsqrt(power)
+            normed = attended * inverse
+            along = jnp.mean(g * normed, axis=-1, keepdims=True)
+            grad = ((g - normed * along) * inverse).astype(BF)
+            out[rows, at] = normed.astype(BF)
+            grad_att[rows, at] = grad
+            state[n] = dot(q, grad, 0, 0).astype(BF)
+        return 0
+
+    lax.fori_loop(0, 4, step, 0)
+
+
+def mixed_kernel(qu, qf, key, val, scores, grad_att, before, dq, local_k, local_v):
     mask = causal()
-    for n, rows, at, vat in spots():
+
+    def body(n, rows, at):
         u, q = qu[rows, at].astype(F32), qf[rows, at]
-        k = feature(kv[rows, at].astype(F32)).astype(BF)
+        k = feature(key[rows, at].astype(F32)).astype(BF)
         a = grad_att[rows, at]
-        mixed = jnp.where(mask, dot(a, kv[rows, vat], 1, 1), 0.0).astype(BF)
+        mixed = jnp.where(mask, dot(a, val[rows, at], 1, 1), 0.0).astype(BF)
         grad_q = dot(mixed, k, 1, 0) + dot(a, before[n], 1, 1)
         dq[rows, at] = (grad_q * slope(u)).astype(BF)
-        local[rows, at] = dot(mixed, q, 0, 0)
-        local[rows, vat] = dot(scores[n], a, 0, 0)
+        local_k[rows, at] = dot(mixed, q, 0, 0)
+        local_v[rows, at] = dot(scores[n], a, 0, 0)
+
+    each_spot(body)
 
 
 def chunk(half, d, turned, dkv):
@@ -190,17 +220,21 @@
 STEPS = (2, 1, 3)
 
 
-def backward_kernel(kv, local, after, turned_hbm, dkv, *refs):
+def backward_kernel(key, val, local_k, local_v, after, turned_hbm, dkv, *refs):
     outs, (turned, held, sem, sems) = refs[:6], refs[6:]
     load = pltpu.make_async_copy(turned_hbm, turned, sem)
     load.start()
-    for n, rows, at, vat in spots():
-        u = kv[rows, at].astype(F32)
-        k, v = feature(u).astype(BF), kv[rows, vat]
-        grad_k = local[rows, at] + dot(v, after[n], 1, 1)
-        grad_v = local[rows, vat] + dot(k, after[n], 1, 0)
+
+    def body(n, rows, at):
+        u = key[rows, at].astype(F32)
+        k, v = feature(u).astype(BF), val[rows, at]
+        vat = pl.ds(pl.multiple_of(512 + at.start, HD), HD)
+        grad_k = local_k[rows, at] + dot(v, after[n], 1, 1)
+        grad_v = local_v[rows, at] + dot(k, after[n], 1, 0)
         dkv[rows, at] = (grad_k * slope(u)).astype(BF)
         dkv[rows, vat] = grad_v.astype(BF)
+
+    each_spot(body)
     load.wait()
     stores = []
     for i, d in enumerate(STEPS):
@@ -249,11 +283,18 @@
 
 def column_kernel(*refs):
     out = refs[-1]
-    for half in range(2):
-        total = refs[half * 4][...]
-        for r in refs[half * 4 + 1 : half * 4 + 4]:
-            total = total + r[...].astype(F32)
-        out[:, :, half * 512 : half * 512 + 512] = total.reshape(16, 8, 512).astype(BF)
+
+    def step(n, _):
+        rows = pl.ds(pl.multiple_of(n * 64, 64), 64)
+        for half in range(2):
+            total = refs[half * 4][rows]
+            for r in refs[half * 4 + 1 : half * 4 + 4]:
+                total = total + r[rows].astype(F32)
+            at = slice(half * 512, half * 512 + 512)
+            out[pl.ds(n * 8, 8), :, at] = total.reshape(8, 8, 512).astype(BF)
+        return 0
+
+    lax.fori_loop(0, 2, step, 0)
 
 
 def last_kernel(scale, parts, out):
@@ -267,9 +308,10 @@
             out[:, at : at + 512] = total[:, half * 512 : half * 512 + 512]
 
 
-def token_kernel(dkv, got, o, dq, w, w_sib, out, o_out, dq_out):
-    total = dot(dkv[:256], w[0].reshape(256, 1024), 1, 1)
-    total += dot(got[:, :1024], w_sib[0].reshape(256, 1024), 1, 1)
+def token_kernel(dkv, got, o, dq, wk, wk_sib, wv, wv_sib, out, o_out, dq_out):
+    total = dot(dkv[:256, :512], wk[0], 1, 1) + dot(got[:, :512], wk_sib[0], 1, 1)
+    total += dot(dkv[:256, 512:], wv[0].reshape(128, 512), 1, 1)
+    total += dot(got[:, 512:1024], wv_sib[0].reshape(128, 512), 1, 1)
     out[...] = total.astype(BF)
 
     @pl.when(pl.program_id(0) == 0)
@@ -287,13 +329,14 @@
     def fixed(shape):
         return pl.BlockSpec(shape, lambda n: (0,) * len(shape))
 
-    tile = pl.BlockSpec((1, 16, 16, 1024), lambda n: (n, 0, 0, 0))
+    tile_k = pl.BlockSpec((1, 128, 512), lambda n: (n // 2, n % 2, 0))
+    tile_v = pl.BlockSpec((1, 8, 16, 512), lambda n: (n // 2, n % 2, 0, 0))
     return pl.pallas_call(
         token_kernel,
-        grid=(8,),
+        grid=(16,),
         out_shape=[jax.ShapeDtypeStruct((rows, n), BF) for n in (2048, 1024, 1024)],
-        in_specs=[fixed(a.shape) for a in args[:4]] + [tile] * 2,
-        out_specs=[pl.BlockSpec((rows, 256), lambda n: (0, n))] + [fixed((rows, 1024))] * 2,
+        in_specs=[fixed(a.shape) for a in args[:4]] + [tile_k] * 2 + [tile_v] * 2,
+        out_specs=[pl.BlockSpec((rows, 128), lambda n: (0, n))] + [fixed((rows, 1024))] * 2,
         cost_estimate=pl.CostEstimate(
             flops=4 * 2 * rows * 2048 * 2048, bytes_accessed=12 << 20, transcendentals=0
         ),
@@ -310,13 +353,17 @@
     def theirs(x):
         return swap(lax.dynamic_slice_in_dim(x, (1 - core) * 512, 512, 1))
 
+    shard = lax.dynamic_slice_in_dim(kv_weight, core * 512, 512, 1)
+    shards, left, right = [shard], shard, shard
+    for _ in range(3):
+        left, right = shift(left, "z", 1), shift(right, "z", -1)
+        shards += [left, right]
+    shards += [shift(left[:128], "z", 1), shift(right[128:], "z", -1)]
     place = lax.axis_index(("y", "x"))
-    mine = lax.dynamic_slice_in_dim(kv_weight, place * 16, 16, 0).reshape(16, 2, 2, 512)
-    mine = lax.dynamic_index_in_dim(mine, core, 2, keepdims=False).reshape(16, 1024)
-    along_z = lax.all_to_all(jnp.broadcast_to(mine[None], (8, 16, 1024)), "z", 0, 0, tiled=True)
-    a0, b0 = along_z[:, :, :512], along_z[:, :, 512:]
-    first = [(shift(a0, "x", d), shift(b0, "y", d)) for d in (2, 1, 3)]
-    (a2, b2), (a1, b1), (a3, b3) = first
+    mine = lax.dynamic_slice(kv_weight, (place * 16, 1024 + core * 512), (16, 512))
+    along_z = lax.all_to_all(jnp.broadcast_to(mine[None], (8, 16, 512)), "z", 0, 0, tiled=True)
+    a0, b0 = along_z[:, :, :256], along_z[:, :, 256:]
+    (a2, b2), (a1, b1), (a3, b3) = [(shift(a0, "x", d), shift(b0, "y", d)) for d in (2, 1, 3)]
     a = jnp.stack([a0, a1, a2, a3])
     b = jnp.stack([b0, b1, b2, b3])
     (p2, r2), (p1, r1), (p3, r3) = [(shift(a, "y", e), shift(b, "x", e)) for e in (2, 1, 3)]
@@ -331,20 +378,32 @@
     half = ((2 * rows, 512), BF)
     whole = ((2 * rows, 1024), BF)
     states = ((8, HD, HD), BF)
-    w, kv, state = call(
-        key_value_kernel,
-        [((8, 16, 16, 1024), BF), whole, states],
-        both, a, p1, p2, p3, b, r1, r2, r3,
-        in_specs=[VMEM] + [ANY] * 8,
+    w_key, key = call(
+        key_kernel,
+        [((8, 256, 512), BF), half],
+        both, *shards,
+        in_specs=[VMEM] + [ANY] * 9,
+        out_specs=[ANY, VMEM],
+        scratch=[
+            pltpu.VMEM((8, 256, 512), BF),
+            pltpu.SemaphoreType.DMA((9,)),
+            pltpu.SemaphoreType.DMA(()),
+        ],
+        flops=2 * 512 * 2048 * 512,
+    )
+    w_val, val, state = call(
+        value_kernel,
+        [((8, 16, 16, 512), BF), half, states],
+        both, key, a, p1, p2, p3, b, r1, r2, r3,
+        in_specs=[VMEM] * 2 + [ANY] * 8,
         out_specs=[ANY, VMEM, VMEM],
         scratch=[
-            pltpu.VMEM((8, 16, 16, 1024), BF),
+            pltpu.VMEM((8, 16, 16, 512), BF),
             pltpu.SemaphoreType.DMA((32,)),
-            pltpu.SemaphoreType.DMA((2,)),
+            pltpu.SemaphoreType.DMA(()),
         ],
-        flops=2 * 512 * 2048 * 1024,
-    )
-    sib_w = swap(w)
+        flops=2 * 512 * 2048 * 512,
+    )
 
     def exchange(x, later, ahead):
         x = lax.all_to_all(x, "z", 0, 0, tiled=True)
@@ -356,7 +415,7 @@
     qu, qf, scores, local = call(
         local_kernel,
         [half, half, ((8, 256, 256), BF), ((2 * rows, 512), F32)],
-        queries, sib_q, kv,
+        queries, sib_q, key, val,
         flops=2 * 8 * 256 * 256 * 256,
     )
     before = exchange(state, False, local)
@@ -366,19 +425,19 @@
         qf, out_grad, sib_g, local, before,
         flops=2 * 8 * 256 * 128 * 256,
     )
-    dq, local = call(
+    dq, local_k, local_v = call(
         mixed_kernel,
-        [half, ((2 * rows, 1024), F32)],
-        qu, qf, kv, scores, grad_att, before,
+        [half] + [((2 * rows, 512), F32)] * 2,
+        qu, qf, key, val, scores, grad_att, before,
         flops=2 * 8 * 256 * 256 * 640,
     )
-    after = exchange(state, True, local)
+    after = exchange(state, True, local_v)
     sent = ((4, 128, 512), BF)
     dkv, a2, b2, a1, b1, a3, b3 = call(
         backward_kernel,
         [whole] + [sent] * 6,
-        kv, local, after, turned,
-        in_specs=[VMEM] * 3 + [ANY],
+        key, val, local_k, local_v, after, turned,
+        in_specs=[VMEM] * 5 + [ANY],
         out_specs=[VMEM] + [ANY] * 6,
         scratch=[
             pltpu.VMEM((16, HD, 2 * rows), BF),
@@ -397,7 +456,9 @@
         own_kernel, [sent] * 2, turned, dkv, back, in_specs=[VMEM] * 2 + [ANY],
         flops=2 * 512 * 512 * 1024,
     )
-    token_grad, output, query_grad = token_call(rows, dkv, swap(back), out, dq, w, sib_w)
+    token_grad, output, query_grad = token_call(
+        rows, dkv, swap(back), out, dq, w_key, swap(w_key), w_val, swap(w_val)
+    )
     full = ((128, 512), F32)
     sent = ((128, 512), BF)
     parts = call(

time: 264 us -> 249 us (0.943)
  waiting for transfers between devices: 97.6 us -> 63.8 us
  Pallas kernels: 59.7 us -> 72.6 us
  starting transfers between devices: 64.3 us -> 70.7 us
    ppermute x24 -> x32, waiting for transfers between devices: 59.9 us -> 36.6 us  [shift(): return lax.ppermute(x, axis, [(i, (i + step) % size) for i in range(size)])]
    pallas_call x13 -> x14, Pallas kernels: 49.9 us -> 57.5 us  [call(): pl.pallas_call(body, out_shape=[jax.ShapeDtypeStruct(s, d) for s, d in ou...]
    all_to_all x1, waiting for transfers between devices: 11.9 us -> 6.43 us  [on_device(): lax.all_to_all(jnp.broadcast_to(mine[None], (8, 16, 512)), 'z', 0, 0, til...]
    pallas_call x1, Pallas kernels: 9.76 us -> 15.1 us  [token_call(): pl.pallas_call(token_kernel, grid=(16,), out_shape=[jax.ShapeDtypeStruct(...]
    ppermute x24 -> x32, starting transfers between devices: 46.5 us -> 51.6 us  [shift(): return lax.ppermute(x, axis, [(i, (i + step) % size) for i in range(size)])]
    all_to_all x2, waiting for transfers between devices: 10.1 us -> 7.17 us  [exchange(): x = lax.all_to_all(x, 'z', 0, 0, tiled=True)]
    unnamed x45 -> x66, local copies, waits for them, and re-layouts: 6.35 us -> 4.44 us
  transfers between devices with their start and end apart: 33 -> 42, of which waited for: 21 -> 15; matrix products, arithmetic and copies ran while one was open for 0% -> 1% of each run, Pallas kernels for 17% -> 21%
where the time goes in v1:
time: 249 us; the launch traced here: 245 us
  Pallas kernels  72.6 us (29%)
  starting transfers between devices  70.7 us (28%)
  waiting for transfers between devices  63.8 us (26%)
  blocking collectives  29.8 us (12%)
  local copies, waits for them, and re-layouts  6.89 us (3%)
    pallas_call x14, Pallas kernels, call(): pl.pallas_call(body, out_shape=[jax.ShapeDtypeStruct(s, d) for s, d in ou...  57.5 us
    ppermute x32, starting transfers between devices, shift(): return lax.ppermute(x, axis, [(i, (i + step) % size) for i in range(size)])  51.6 us
    ppermute x32, waiting for transfers between devices, shift(): return lax.ppermute(x, axis, [(i, (i + step) % size) for i in range(size)])  36.6 us
    all_to_all x1, blocking collectives, exchange(): return lax.all_to_all(x, 'z', 0, 0, tiled=True)  15.2 us
    pallas_call x1, Pallas kernels, token_call(): pl.pallas_call(token_kernel, grid=(16,), out_shape=[jax.ShapeDtypeStruct(...  15.1 us
    all_to_all x1, blocking collectives, on_device(): column = lax.all_to_all(column, ('core', 'z'), 0, 0, tiled=True)  14.7 us
    all_to_all x1, waiting for transfers between devices, exchange(): return lax.all_to_all(x, 'z', 0, 0, tiled=True)  10.5 us
    all_to_all x2, starting transfers between devices, exchange(): x = lax.all_to_all(x, 'z', 0, 0, tiled=True)  8.46 us
  transfers between devices with their start and end apart: 42, of which 15 were waited for; matrix products, arithmetic and copies ran while one was open for 1% of the time, Pallas kernels for 21%

profile of v1, /device:TPU:0, one launch (start us, length us, event | category | flops | bytes accessed | tf_op | source)
XLA Modules:
  0.0 245.0 jit_solution(15494155487292885799)
XLA Ops:
  0.7 1.0 constant_dynamic-slice_fusion.2.refs_0_
  2.0 4.0 %collective-permute-start.2 = (bf16[256,512]{1,0:T(8,128)(2,1)S(1)}, bf16[256,512]{1,0:T(8,128)(2,1)S(1)}, u32[]{:S(2)}, u32[]{:S(2)}) collective-permute-start(bf16[256,512]{1,0:T(8,128)(2,1)S(1)} %constant_dynamic-slice_fusion.2.refs_0_), channel_id=1, source_target_pairs={{0,7},{1,0},{2,1},{3,2},{4,3},{5,4},{6,5},{7,6},{8,15},{9,8},{10,9... | collective-permute-start | bytes 786440 | tf_op jit(solution)/shard_map/ppermute | solution.py:47
  6.0 0.7 dynamic_slice.13
  7.4 5.8 %all-to-all-start = ((bf16[8,16,512]{2,1,0:T(8,128)(2,1)}), bf16[8,16,512]{2,1,0:T(8,128)(2,1)S(1)}, u32[]{:S(2)}, u32[]{:S(2)}) async-start(bf16[8,16,512]{2,1,0:T(8,128)(2,1)} %broadcast_in_dim.2), calls=%async_computation | async-start | bytes 262144 | tf_op jit(solution)/shard_map/all_to_all | solution.py:364
  13.2 2.1 collective-permute-start.3
  15.3 1.3 collective-permute-start.4
  16.6 6.4 %all-to-all-done = bf16[8,16,512]{2,1,0:T(8,128)(2,1)S(1)} async-done(((bf16[8,16,512]{2,1,0:T(8,128)(2,1)}), bf16[8,16,512]{2,1,0:T(8,128)(2,1)S(1)}, u32[]{:S(2)}, u32[]{:S(2)}) %all-to-all-start) | async-done | bytes 131104 | tf_op jit(solution)/shard_map/all_to_all | solution.py:364
  23.1 1.6 collective-permute-start.9
  25.3 3.0 %collective-permute-start.10 = (bf16[8,16,256]{2,1,0:T(8,128)(2,1)S(1)}, bf16[8,16,256]{2,1,0:T(8,128)(2,1)S(1)}, u32[]{:S(2)}, u32[]{:S(2)}) collective-permute-start(bf16[8,16,256]{2,1,0:T(8,128)(2,1)S(1)} %get-tuple-element.81), channel_id=1, source_target_pairs={{0,32},{16,48},{32,0},{48,16},{1,33},{17,49},{33,1},{49,17},{2,34}... | collective-permute-start | bytes 196616 | tf_op jit(solution)/shard_map/ppermute | solution.py:47
  28.3 3.2 %collective-permute-start.6 = (bf16[256,512]{1,0:T(8,128)(2,1)S(1)}, bf16[256,512]{1,0:T(8,128)(2,1)S(1)}, u32[]{:S(2)}, u32[]{:S(2)}) collective-permute-start(bf16[256,512]{1,0:T(8,128)(2,1)S(1)} %collective-permute-done.4.refs_4_), channel_id=1, source_target_pairs={{0,7},{1,0},{2,1},{3,2},{4,3},{5,4},{6,5},{7,6},{8,15},{9,8},{10,9... | collective-permute-start | bytes 786440 | tf_op jit(solution)/shard_map/ppermute | solution.py:47
  31.5 1.1 collective-permute-start.11
  32.7 3.1 %collective-permute-done.11 = bf16[8,16,256]{2,1,0:T(8,128)(2,1)S(1)} collective-permute-done((bf16[8,16,256]{2,1,0:T(8,128)(2,1)S(1)}, bf16[8,16,256]{2,1,0:T(8,128)(2,1)S(1)}, u32[]{:S(2)}, u32[]{:S(2)}) %collective-permute-start.11) | collective-permute-done | bytes 65568 | tf_op jit(solution)/shard_map/ppermute | solution.py:47
  35.9 1.7 collective-permute-start.12
  37.5 1.6 collective-permute-start.15
  39.1 1.5 collective-permute-start.16
  40.6 2.4 collective-permute-start.17
  43.1 1.9 collective-permute-done.15
  44.9 1.9 collective-permute-done.16
  46.8 1.4 collective-permute-start.8
  48.2 2.6 %collective-permute-start.13 = (bf16[4,8,16,256]{3,2,1,0:T(8,128)(2,1)S(1)}, bf16[4,8,16,256]{3,2,1,0:T(8,128)(2,1)}, u32[]{:S(2)}, u32[]{:S(2)}) collective-permute-start(bf16[4,8,16,256]{3,2,1,0:T(8,128)(2,1)S(1)} %pad_maximum_fusion.refs_0_), channel_id=1, source_target_pairs={{0,128},{64,192},{128,0},{192,64},{1,129},{65,193},{129,1},{193,65... | collective-permute-start | bytes 786440 | tf_op jit(solution)/shard_map/ppermute | solution.py:47
  51.9 3.2 %collective-permute-start.19 = (bf16[4,8,16,256]{3,2,1,0:T(8,128)(2,1)S(1)}, bf16[4,8,16,256]{3,2,1,0:T(8,128)(2,1)}, u32[]{:S(2)}, u32[]{:S(2)}) collective-permute-start(bf16[4,8,16,256]{3,2,1,0:T(8,128)(2,1)S(1)} %pad_maximum_fusion.1.refs_4_), channel_id=1, source_target_pairs={{0,32},{16,48},{32,0},{48,16},{1,33},{17,49},{33,1},{49,17},{2,34}... | collective-permute-start | bytes 786440 | tf_op jit(solution)/shard_map/ppermute | solution.py:47
  55.3 0.9 copy-done.6
  56.1 5.3 %shard_map.75 = (bf16[512,2048]{1,0:T(8,128)(2,1)}, bf16[16,128,512]{2,1,0:T(8,128)(2,1)}) custom-call(bf16[256,2048]{1,0:T(8,128)(2,1)} %own.1, bf16[256,2048]{1,0:T(8,128)(2,1)} %copy-done.6), custom_call_target="tpu_custom_call" | custom-call | bytes 6291456 | tf_op jit(solution)/shard_map/pallas_call | solution.py:35
  61.5 5.4 %shard_map.76 = (bf16[8,256,512]{2,1,0:T(8,128)(2,1)}, bf16[512,512]{1,0:T(8,128)(2,1)}) custom-call(bf16[512,2048]{1,0:T(8,128)(2,1)} %get-tuple-element.41.tok, bf16[256,512]{1,0:T(8,128)(2,1)} %copy-done.3, bf16[256,512]{1,0:T(8,128)(2,1)} %copy-done.17, bf16[256,512]{1,0:T(8,128)(2,1)} %copy-done.18, bf16[256,512]{1,0:T(8,128)(2,1)} %copy-done.19, ...), custom_call_target="tpu_custom_call" | custom-call | flops 1073741824 | bytes 6815744 | tf_op jit(solution)/shard_map/pallas_call | solution.py:35
  67.0 7.0 %shard_map.77 = (bf16[8,16,16,512]{3,2,1,0:T(8,128)(2,1)}, bf16[512,512]{1,0:T(8,128)(2,1)}, bf16[8,128,128]{2,1,0:T(8,128)(2,1)}) custom-call(bf16[512,2048]{1,0:T(8,128)(2,1)} %get-tuple-element.41.tok, bf16[512,512]{1,0:T(8,128)(2,1)} %get-tuple-element.42.key, bf16[4,8,16,256]{3,2,1,0:T(8,128)(2,1)} %copy-done.4, bf16[4,8,16,256]{3,2,1,0:T(8,128)(2,1)} %copy-done.21, ...), custom_call_target="tpu_custom_call" | custom-call | flops 1073741824 | bytes 7602176 | tf_op jit(solution)/shard_map/pallas_call | solution.py:35
  74.0 5.0 %all-to-all-start.1 = ((bf16[8,128,128]{2,1,0:T(8,128)(2,1)}), bf16[8,128,128]{2,1,0:T(8,128)(2,1)S(1)}, u32[]{:S(2)}, u32[]{:S(2)}) async-start(bf16[8,128,128]{2,1,0:T(8,128)(2,1)} %get-tuple-element.48), calls=%async_computation.1 | async-start | bytes 524288 | tf_op jit(solution)/shard_map/all_to_all | solution.py:409
  79.2 1.5 collective-permute-done.21.q_sib
  80.7 0.7 copy-done.23
  81.4 4.9 %shard_map.78 = (bf16[512,512]{1,0:T(8,128)(2,1)}, bf16[512,512]{1,0:T(8,128)(2,1)}, bf16[8,256,256]{2,1,0:T(8,128)(2,1)}, f32[512,512]{1,0:T(8,128)}) custom-call(bf16[256,1024]{1,0:T(8,128)(2,1)} %q_own.1, bf16[256,512]{1,0:T(8,128)(2,1)} %copy-done.23, bf16[512,512]{1,0:T(8,128)(2,1)} %get-tuple-element.42.key, bf16[512,512]{1,0:T(8,128)(2,1)} %get-tuple-element.43.val), custom_call_target="tpu_custom_call" | custom-call | flops 268435456 | bytes 4980736 | tf_op jit(solution)/shard_map/pallas_call | solution.py:35
  86.3 3.2 %all-to-all-done.1.i = bf16[8,128,128]{2,1,0:T(8,128)(2,1)S(1)} async-done(((bf16[8,128,128]{2,1,0:T(8,128)(2,1)}), bf16[8,128,128]{2,1,0:T(8,128)(2,1)S(1)}, u32[]{:S(2)}, u32[]{:S(2)}) %all-to-all-start.1) | async-done | bytes 262176 | tf_op jit(solution)/shard_map/all_to_all | solution.py:409
  89.5 0.7 copy-done.7
  90.2 1.7 shard_map.79
  91.9 4.0 %all-to-all-start.2 = ((bf16[8,128,128]{2,1,0:T(8,128)(2,1)}), bf16[8,128,128]{2,1,0:T(8,128)(2,1)S(1)}, u32[]{:S(2)}, u32[]{:S(2)}) async-start(bf16[8,128,128]{2,1,0:T(8,128)(2,1)} %shard_map.79), calls=%async_computation.2 | async-start | bytes 524288 | tf_op jit(solution)/shard_map/all_to_all | solution.py:413
  96.1 1.5 collective-permute-done.22.g_sib
  97.6 10.5 %all-to-all-done.2.before = bf16[8,128,128]{2,1,0:T(8,128)(2,1)S(1)} async-done(((bf16[8,128,128]{2,1,0:T(8,128)(2,1)}), bf16[8,128,128]{2,1,0:T(8,128)(2,1)S(1)}, u32[]{:S(2)}, u32[]{:S(2)}) %all-to-all-start.2) | async-done | bytes 262176 | tf_op jit(solution)/shard_map/all_to_all | solution.py:413
  108.8 4.6 %shard_map.80 = (bf16[512,512]{1,0:T(8,128)(2,1)}, bf16[512,512]{1,0:T(8,128)(2,1)}, bf16[8,128,128]{2,1,0:T(8,128)(2,1)}) custom-call(bf16[512,512]{1,0:T(8,128)(2,1)} %get-tuple-element.45.qf, bf16[256,1024]{1,0:T(8,128)(2,1)} %g_own.1, bf16[256,512]{1,0:T(8,128)(2,1)} %copy-done.22, f32[512,512]{1,0:T(8,128)} %get-tuple-element.47._.local, ...), custom_call_target="tpu_custom_call" | custom-call | flops 134217728 | bytes 3932160 | tf_op jit(solution)/shard_map/pallas_call | solution.py:35
  113.4 3.4 %all-to-all-start.3 = ((bf16[8,128,128]{2,1,0:T(8,128)(2,1)}), bf16[8,128,128]{2,1,0:T(8,128)(2,1)S(1)}, u32[]{:S(2)}, u32[]{:S(2)}) async-start(bf16[8,128,128]{2,1,0:T(8,128)(2,1)} %get-tuple-element.52), calls=%async_computation.3 | async-start | bytes 524288 | tf_op jit(solution)/shard_map/all_to_all | solution.py:409
  117.4 6.4 %shard_map.81 = (bf16[512,512]{1,0:T(8,128)(2,1)}, f32[512,512]{1,0:T(8,128)}, f32[512,512]{1,0:T(8,128)}) custom-call(bf16[512,512]{1,0:T(8,128)(2,1)} %get-tuple-element.44.qu, bf16[512,512]{1,0:T(8,128)(2,1)} %get-tuple-element.45.qf, bf16[512,512]{1,0:T(8,128)(2,1)} %get-tuple-element.42.key, bf16[512,512]{1,0:T(8,128)(2,1)} %get-tuple-element.43.val, ...), custom_call_target="tpu_custom_call" | custom-call | flops 671088640 | bytes 6553600 | tf_op jit(solution)/shard_map/pallas_call | solution.py:35
  123.8 4.0 %all-to-all-done.3.i = bf16[8,128,128]{2,1,0:T(8,128)(2,1)S(1)} async-done(((bf16[8,128,128]{2,1,0:T(8,128)(2,1)}), bf16[8,128,128]{2,1,0:T(8,128)(2,1)S(1)}, u32[]{:S(2)}, u32[]{:S(2)}) %all-to-all-start.3) | async-done | bytes 262176 | tf_op jit(solution)/shard_map/all_to_all | solution.py:409
  128.6 1.7 shard_map.82
  130.2 15.2 %all_to_all.30.after = bf16[8,128,128]{2,1,0:T(8,128)(2,1)} all-to-all(bf16[8,128,128]{2,1,0:T(8,128)(2,1)} %shard_map.82), channel_id=1, replica_groups=mesh['y'=4,'x'=4,'core'=2,'z'=8] {'z'}, dimensions={0} | all-to-all | bytes 524288 | tf_op jit(solution)/shard_map/all_to_all | solution.py:413
  145.4 7.2 %shard_map.83 = (bf16[512,1024]{1,0:T(8,128)(2,1)}, bf16[4,128,512]{2,1,0:T(8,128)(2,1)}, bf16[4,128,512]{2,1,0:T(8,128)(2,1)}, bf16[4,128,512]{2,1,0:T(8,128)(2...) custom-call(bf16[512,512]{1,0:T(8,128)(2,1)} %get-tuple-element.42.key, ...), custom_call_target="tpu_custom_call" | custom-call | flops 2147483648 | bytes 9699328 | tf_op jit(solution)/shard_map/pallas_call | solution.py:35
  152.6 2.6 %shard_map.84._ = bf16[256,2048]{1,0:T(8,128)(2,1)} custom-call(bf16[512,1024]{1,0:T(8,128)(2,1)} %get-tuple-element.54.dkv, bf16[512,512]{1,0:T(8,128)(2,1)} %get-tuple-element.55.dq, bf16[512,512]{1,0:T(8,128)(2,1)} %get-tuple-element.56.out.o, bf16[4,128,512]{2,1,0:T(8,128)(2,1)} %get-tuple-element.57._), custom_call_target="tpu_custom_call" | custom-call | bytes 3670016 | tf_op jit(solution)/shard_map/pallas_call | solution.py:35
  155.2 1.1 collective-permute-start.26
  157.0 3.4 %shard_map.86 = (bf16[4,128,512]{2,1,0:T(8,128)(2,1)}, bf16[4,128,512]{2,1,0:T(8,128)(2,1)}) custom-call(bf16[16,128,512]{2,1,0:T(8,128)(2,1)} %get-tuple-element.53.turned_hbm.turned, bf16[512,1024]{1,0:T(8,128)(2,1)} %get-tuple-element.54.dkv, bf16[256,2048]{1,0:T(8,128)(2,1)} %shard_map.84._), custom_call_target="tpu_custom_call" | custom-call | flops 536870912 | bytes 5242880 | tf_op jit(solution)/shard_map/pallas_call | solution.py:35
  160.3 2.2 collective-permute-start.28
  162.6 1.7 collective-permute-start.29
  164.2 17.8 %collective-permute-done.26.refs_1_ = bf16[4,128,512]{2,1,0:T(8,128)(2,1)S(1)} collective-permute-done((bf16[4,128,512]{2,1,0:T(8,128)(2,1)S(1)}, bf16[4,128,512]{2,1,0:T(8,128)(2,1)S(1)}, u32[]{:S(2)}, u32[]{:S(2)}) %collective-permute-start.26) | collective-permute-done | bytes 524320 | tf_op jit(solution)/shard_map/ppermute | solution.py:47
  182.0 2.4 collective-permute-start.30
  184.5 1.9 collective-permute-start.31
  186.4 15.1 %shard_map.85 = (bf16[256,2048]{1,0:T(8,128)(2,1)}, bf16[256,1024]{1,0:T(8,128)(2,1)}, bf16[256,1024]{1,0:T(8,128)(2,1)}) custom-call(bf16[512,1024]{1,0:T(8,128)(2,1)} %get-tuple-element.54.dkv, bf16[256,2048]{1,0:T(8,128)(2,1)} %collective-permute-done.23.got, bf16[512,512]{1,0:T(8,128)(2,1)} %get-tuple-element.56.out.o, ...), custom_call_target="tpu_custom_call" | custom-call | flops 8589934592 | bytes 12582912 | tf_op jit(solution)/shard_map/pallas_call | solution.py:334
  201.6 5.9 %collective-permute-done.31.refs_7_ = bf16[4,128,512]{2,1,0:T(8,128)(2,1)} collective-permute-done((bf16[4,128,512]{2,1,0:T(8,128)(2,1)}, bf16[4,128,512]{2,1,0:T(8,128)(2,1)}, u32[]{:S(2)}, u32[]{:S(2)}) %collective-permute-start.31) | collective-permute-done | bytes 524320 | tf_op jit(solution)/shard_map/ppermute | solution.py:47
  207.5 3.6 %shard_map.87 = (f32[128,512]{1,0:T(8,128)}, bf16[128,512]{1,0:T(8,128)(2,1)}, bf16[128,512]{1,0:T(8,128)(2,1)}, bf16[128,512]{1,0:T(8,128)(2,1)}, f32[128,512]{...) custom-call(bf16[4,128,512]{2,1,0:T(8,128)(2,1)} %get-tuple-element.63.refs_0_, ...), custom_call_target="tpu_custom_call" | custom-call | bytes 6553600 | tf_op jit(solution)/shard_map/pallas_call | solution.py:35
  211.1 1.8 collective-permute-start.32
  212.9 2.4 collective-permute-start.33
  215.3 1.9 collective-permute-start.34
  217.2 0.9 collective-permute-start.36
  218.1 2.5 %collective-permute-start.37 = (bf16[128,512]{1,0:T(8,128)(2,1)}, bf16[128,512]{1,0:T(8,128)(2,1)S(1)}, u32[]{:S(2)}, u32[]{:S(2)}) collective-permute-start(bf16[128,512]{1,0:T(8,128)(2,1)} %get-tuple-element.77), channel_id=1, source_target_pairs={{0,48},{16,0},{32,16},{48,32},{1,49},{17,1},{33,17},{49,33},{2,50}... | collective-permute-start | bytes 393224 | tf_op jit(solution)/shard_map/ppermute | solution.py:47
  220.6 1.1 collective-permute-done.33.refs_2_
  221.7 3.3 %collective-permute-done.35.refs_5_ = bf16[128,512]{1,0:T(8,128)(2,1)S(1)} collective-permute-done((bf16[128,512]{1,0:T(8,128)(2,1)}, bf16[128,512]{1,0:T(8,128)(2,1)S(1)}, u32[]{:S(2)}, u32[]{:S(2)}) %collective-permute-start.35) | collective-permute-done | bytes 131104 | tf_op jit(solution)/shard_map/ppermute | solution.py:47
  225.0 0.9 collective-permute-done.37.refs_7_
  226.6 2.1 shard_map.88
  228.7 14.7 %all_to_all.31.i = bf16[16,8,1024]{2,1,0:T(8,128)(2,1)} all-to-all(bf16[16,8,1024]{2,1,0:T(8,128)(2,1)} %shard_map.88), channel_id=1, replica_groups=mesh['y'=4,'x'=4,'core'=2,'z'=8] {'core','z'}, dimensions={0} | all-to-all | bytes 524288 | tf_op jit(solution)/shard_map/all_to_all | solution.py:479
  243.4 1.6 shard_map.89
  (113 shorter events, 6.5 us)
Async XLA Ops:
  0.6 54.5 %collective-permute-start = (bf16[256,2048]{1,0:T(8,128)(2,1)}, bf16[256,2048]{1,0:T(8,128)(2,1)S(1)}, u32[]{:S(2)}, u32[]{:S(2)}) collective-permute-start(bf16[256,2048]{1,0:T(8,128)(2,1)} %own.1), channel_id=1, source_target_pairs={{0,8},{8,0},{1,9},{9,1},{2,10},{10,2},{3,11},{11,3},{4,12},{12,4},... | collective-permute-start | bytes 3145736 | tf_op jit(solution)/shard_map/ppermute | solution.py:351
  1.7 59.7 %copy-start.3 = (bf16[256,512]{1,0:T(8,128)(2,1)}, bf16[256,512]{1,0:T(8,128)(2,1)S(1)}, u32[]{:S(2)}) copy-start(bf16[256,512]{1,0:T(8,128)(2,1)S(1)} %constant_dynamic-slice_fusion.2.refs_0_) | copy-start | bytes 786436
  1.7 11.5 %collective-permute-start.1 = (bf16[256,512]{1,0:T(8,128)(2,1)S(1)}, bf16[256,512]{1,0:T(8,128)(2,1)S(1)}, u32[]{:S(2)}, u32[]{:S(2)}) collective-permute-start(bf16[256,512]{1,0:T(8,128)(2,1)S(1)} %constant_dynamic-slice_fusion.2.refs_0_), channel_id=1, source_target_pairs={{0,1},{1,2},{2,3},{3,4},{4,5},{5,6},{6,7},{7,0},{8,9},{9,10},{10,1... | collective-permute-start | bytes 786440 | tf_op jit(solution)/shard_map/ppermute | solution.py:47
  2.0 13.3 %collective-permute-start.2 = (bf16[256,512]{1,0:T(8,128)(2,1)S(1)}, bf16[256,512]{1,0:T(8,128)(2,1)S(1)}, u32[]{:S(2)}, u32[]{:S(2)}) collective-permute-start(bf16[256,512]{1,0:T(8,128)(2,1)S(1)} %constant_dynamic-slice_fusion.2.refs_0_), channel_id=1, source_target_pairs={{0,7},{1,0},{2,1},{3,2},{4,3},{5,4},{6,5},{7,6},{8,15},{9,8},{10,9... | collective-permute-start | bytes 786440 | tf_op jit(solution)/shard_map/ppermute | solution.py:47
  7.4 15.6 %all-to-all-start = ((bf16[8,16,512]{2,1,0:T(8,128)(2,1)}), bf16[8,16,512]{2,1,0:T(8,128)(2,1)S(1)}, u32[]{:S(2)}, u32[]{:S(2)}) async-start(bf16[8,16,512]{2,1,0:T(8,128)(2,1)} %broadcast_in_dim.2), calls=%async_computation | async-start | bytes 262144 | tf_op jit(solution)/shard_map/all_to_all | solution.py:364
  13.2 48.2 %copy-start.17 = (bf16[256,512]{1,0:T(8,128)(2,1)}, bf16[256,512]{1,0:T(8,128)(2,1)S(1)}, u32[]{:S(2)}) copy-start(bf16[256,512]{1,0:T(8,128)(2,1)S(1)} %collective-permute-done.1.refs_1_) | copy-start | bytes 786436
  13.2 12.1 %collective-permute-start.3 = (bf16[256,512]{1,0:T(8,128)(2,1)S(1)}, bf16[256,512]{1,0:T(8,128)(2,1)S(1)}, u32[]{:S(2)}, u32[]{:S(2)}) collective-permute-start(bf16[256,512]{1,0:T(8,128)(2,1)S(1)} %collective-permute-done.1.refs_1_), channel_id=1, source_target_pairs={{0,1},{1,2},{2,3},{3,4},{4,5},{5,6},{6,7},{7,0},{8,9},{9,10},{10,1... | collective-permute-start | bytes 786440 | tf_op jit(solution)/shard_map/ppermute | solution.py:47
  15.3 46.1 %copy-start.18 = (bf16[256,512]{1,0:T(8,128)(2,1)}, bf16[256,512]{1,0:T(8,128)(2,1)S(1)}, u32[]{:S(2)}) copy-start(bf16[256,512]{1,0:T(8,128)(2,1)S(1)} %collective-permute-done.2.refs_2_) | copy-start | bytes 786436
  15.3 13.0 %collective-permute-start.4 = (bf16[256,512]{1,0:T(8,128)(2,1)S(1)}, bf16[256,512]{1,0:T(8,128)(2,1)S(1)}, u32[]{:S(2)}, u32[]{:S(2)}) collective-permute-start(bf16[256,512]{1,0:T(8,128)(2,1)S(1)} %collective-permute-done.2.refs_2_), channel_id=1, source_target_pairs={{0,7},{1,0},{2,1},{3,2},{4,3},{5,4},{6,5},{7,6},{8,15},{9,8},{10,9... | collective-permute-start | bytes 786440 | tf_op jit(solution)/shard_map/ppermute | solution.py:47
  23.1 8.5 %collective-permute-start.9 = (bf16[8,16,256]{2,1,0:T(8,128)(2,1)S(1)}, bf16[8,16,256]{2,1,0:T(8,128)(2,1)S(1)}, u32[]{:S(2)}, u32[]{:S(2)}) collective-permute-start(bf16[8,16,256]{2,1,0:T(8,128)(2,1)S(1)} %get-tuple-element.81), channel_id=1, source_target_pairs={{0,16},{16,32},{32,48},{48,0},{1,17},{17,33},{33,49},{49,1},{2,18}... | collective-permute-start | bytes 196616 | tf_op jit(solution)/shard_map/ppermute | solution.py:47
  25.3 36.2 %copy-start.19 = (bf16[256,512]{1,0:T(8,128)(2,1)}, bf16[256,512]{1,0:T(8,128)(2,1)S(1)}, u32[]{:S(2)}) copy-start(bf16[256,512]{1,0:T(8,128)(2,1)S(1)} %collective-permute-done.3.refs_3_) | copy-start | bytes 786436
  25.3 13.8 %collective-permute-start.5 = (bf16[256,512]{1,0:T(8,128)(2,1)S(1)}, bf16[256,512]{1,0:T(8,128)(2,1)S(1)}, u32[]{:S(2)}, u32[]{:S(2)}) collective-permute-start(bf16[256,512]{1,0:T(8,128)(2,1)S(1)} %collective-permute-done.3.refs_3_), channel_id=1, source_target_pairs={{0,1},{1,2},{2,3},{3,4},{4,5},{5,6},{6,7},{7,0},{8,9},{9,10},{10,1... | collective-permute-start | bytes 786440 | tf_op jit(solution)/shard_map/ppermute | solution.py:47
  25.3 7.4 %collective-permute-start.10 = (bf16[8,16,256]{2,1,0:T(8,128)(2,1)S(1)}, bf16[8,16,256]{2,1,0:T(8,128)(2,1)S(1)}, u32[]{:S(2)}, u32[]{:S(2)}) collective-permute-start(bf16[8,16,256]{2,1,0:T(8,128)(2,1)S(1)} %get-tuple-element.81), channel_id=1, source_target_pairs={{0,32},{16,48},{32,0},{48,16},{1,33},{17,49},{33,1},{49,17},{2,34}... | collective-permute-start | bytes 196616 | tf_op jit(solution)/shard_map/ppermute | solution.py:47
  28.3 33.1 %copy-start.20 = (bf16[256,512]{1,0:T(8,128)(2,1)}, bf16[256,512]{1,0:T(8,128)(2,1)S(1)}, u32[]{:S(2)}) copy-start(bf16[256,512]{1,0:T(8,128)(2,1)S(1)} %collective-permute-done.4.refs_4_) | copy-start | bytes 786436
  28.3 12.3 %collective-permute-start.6 = (bf16[256,512]{1,0:T(8,128)(2,1)S(1)}, bf16[256,512]{1,0:T(8,128)(2,1)S(1)}, u32[]{:S(2)}, u32[]{:S(2)}) collective-permute-start(bf16[256,512]{1,0:T(8,128)(2,1)S(1)} %collective-permute-done.4.refs_4_), channel_id=1, source_target_pairs={{0,7},{1,0},{2,1},{3,2},{4,3},{5,4},{6,5},{7,6},{8,15},{9,8},{10,9... | collective-permute-start | bytes 786440 | tf_op jit(solution)/shard_map/ppermute | solution.py:47
  31.5 4.3 %collective-permute-start.11 = (bf16[8,16,256]{2,1,0:T(8,128)(2,1)S(1)}, bf16[8,16,256]{2,1,0:T(8,128)(2,1)S(1)}, u32[]{:S(2)}, u32[]{:S(2)}) collective-permute-start(bf16[8,16,256]{2,1,0:T(8,128)(2,1)S(1)} %get-tuple-element.81), channel_id=1, source_target_pairs={{0,48},{16,0},{32,16},{48,32},{1,49},{17,1},{33,17},{49,33},{2,50}... | collective-permute-start | bytes 196616 | tf_op jit(solution)/shard_map/ppermute | solution.py:47
  35.8 31.0 %copy-start.4 = (bf16[4,8,16,256]{3,2,1,0:T(8,128)(2,1)}, bf16[4,8,16,256]{3,2,1,0:T(8,128)(2,1)S(1)}, u32[]{:S(2)}) copy-start(bf16[4,8,16,256]{3,2,1,0:T(8,128)(2,1)S(1)} %pad_maximum_fusion.refs_0_) | copy-start | bytes 786436
  35.9 15.0 %collective-permute-start.12 = (bf16[4,8,16,256]{3,2,1,0:T(8,128)(2,1)S(1)}, bf16[4,8,16,256]{3,2,1,0:T(8,128)(2,1)S(1)}, u32[]{:S(2)}, u32[]{:S(2)}) collective-permute-start(bf16[4,8,16,256]{3,2,1,0:T(8,128)(2,1)S(1)} %pad_maximum_fusion.refs_0_), channel_id=1, source_target_pairs={{0,64},{64,128},{128,192},{192,0},{1,65},{65,129},{129,193},{193,1... | collective-permute-start | bytes 786440 | tf_op jit(solution)/shard_map/ppermute | solution.py:47
  37.5 7.4 %collective-permute-start.15 = (bf16[8,16,256]{2,1,0:T(8,128)(2,1)S(1)}, bf16[8,16,256]{2,1,0:T(8,128)(2,1)S(1)}, u32[]{:S(2)}, u32[]{:S(2)}) collective-permute-start(bf16[8,16,256]{2,1,0:T(8,128)(2,1)S(1)} %get-tuple-element.80), channel_id=1, source_target_pairs={{0,64},{64,128},{128,192},{192,0},{1,65},{65,129},{129,193},{193,1... | collective-permute-start | bytes 196616 | tf_op jit(solution)/shard_map/ppermute | solution.py:47
  39.1 22.4 %copy-start.9 = (bf16[256,512]{1,0:T(8,128)(2,1)}, bf16[256,512]{1,0:T(8,128)(2,1)S(1)}, u32[]{:S(2)}) copy-start(bf16[256,512]{1,0:T(8,128)(2,1)S(1)} %collective-permute-done.5.refs_5_) | copy-start | bytes 786436
  39.1 7.7 %collective-permute-start.16 = (bf16[8,16,256]{2,1,0:T(8,128)(2,1)S(1)}, bf16[8,16,256]{2,1,0:T(8,128)(2,1)S(1)}, u32[]{:S(2)}, u32[]{:S(2)}) collective-permute-start(bf16[8,16,256]{2,1,0:T(8,128)(2,1)S(1)} %get-tuple-element.80), channel_id=1, source_target_pairs={{0,128},{64,192},{128,0},{192,64},{1,129},{65,193},{129,1},{193,65... | collective-permute-start | bytes 196616 | tf_op jit(solution)/shard_map/ppermute | solution.py:47
  40.6 20.8 %copy-start.10 = (bf16[256,512]{1,0:T(8,128)(2,1)}, bf16[256,512]{1,0:T(8,128)(2,1)S(1)}, u32[]{:S(2)}) copy-start(bf16[256,512]{1,0:T(8,128)(2,1)S(1)} %collective-permute-done.6.refs_6_) | copy-start | bytes 786436
  40.6 7.5 %collective-permute-start.17 = (bf16[8,16,256]{2,1,0:T(8,128)(2,1)S(1)}, bf16[8,16,256]{2,1,0:T(8,128)(2,1)S(1)}, u32[]{:S(2)}, u32[]{:S(2)}) collective-permute-start(bf16[8,16,256]{2,1,0:T(8,128)(2,1)S(1)} %get-tuple-element.80), channel_id=1, source_target_pairs={{0,192},{64,0},{128,64},{192,128},{1,193},{65,1},{129,65},{193,129... | collective-permute-start | bytes 196616 | tf_op jit(solution)/shard_map/ppermute | solution.py:47
  44.9 6.4 %collective-permute-start.7 = (bf16[128,512]{1,0:T(8,128)(2,1)S(1)}, bf16[128,512]{1,0:T(8,128)(2,1)S(1)}, u32[]{:S(2)}, u32[]{:S(2)}) collective-permute-start(bf16[128,512]{1,0:T(8,128)(2,1)S(1)} %slice.16), channel_id=1, source_target_pairs={{0,1},{1,2},{2,3},{3,4},{4,5},{5,6},{6,7},{7,0},{8,9},{9,10},{10,1... | collective-permute-start | bytes 393224 | tf_op jit(solution)/shard_map/ppermute | solution.py:47
  46.8 5.1 %collective-permute-start.8 = (bf16[128,512]{1,0:T(8,128)(2,1)S(1)}, bf16[128,512]{1,0:T(8,128)(2,1)S(1)}, u32[]{:S(2)}, u32[]{:S(2)}) collective-permute-start(bf16[128,512]{1,0:T(8,128)(2,1)S(1)} %slice.17), channel_id=1, source_target_pairs={{0,7},{1,0},{2,1},{3,2},{4,3},{5,4},{6,5},{7,6},{8,15},{9,8},{10,9... | collective-permute-start | bytes 393224 | tf_op jit(solution)/shard_map/ppermute | solution.py:47
  48.2 18.7 %collective-permute-start.13 = (bf16[4,8,16,256]{3,2,1,0:T(8,128)(2,1)S(1)}, bf16[4,8,16,256]{3,2,1,0:T(8,128)(2,1)}, u32[]{:S(2)}, u32[]{:S(2)}) collective-permute-start(bf16[4,8,16,256]{3,2,1,0:T(8,128)(2,1)S(1)} %pad_maximum_fusion.refs_0_), channel_id=1, source_target_pairs={{0,128},{64,192},{128,0},{192,64},{1,129},{65,193},{129,1},{193,65... | collective-permute-start | bytes 786440 | tf_op jit(solution)/shard_map/ppermute | solution.py:47
  50.9 16.1 %copy-start.5 = (bf16[4,8,16,256]{3,2,1,0:T(8,128)(2,1)}, bf16[4,8,16,256]{3,2,1,0:T(8,128)(2,1)S(1)}, u32[]{:S(2)}) copy-start(bf16[4,8,16,256]{3,2,1,0:T(8,128)(2,1)S(1)} %pad_maximum_fusion.1.refs_4_) | copy-start | bytes 786436
  50.9 4.3 %copy-start.21 = (bf16[4,8,16,256]{3,2,1,0:T(8,128)(2,1)}, bf16[4,8,16,256]{3,2,1,0:T(8,128)(2,1)S(1)}, u32[]{:S(2)}) copy-start(bf16[4,8,16,256]{3,2,1,0:T(8,128)(2,1)S(1)} %collective-permute-done.12.refs_1_) | copy-start | bytes 786436
  50.9 16.0 %collective-permute-start.14 = (bf16[4,8,16,256]{3,2,1,0:T(8,128)(2,1)S(1)}, bf16[4,8,16,256]{3,2,1,0:T(8,128)(2,1)}, u32[]{:S(2)}, u32[]{:S(2)}) collective-permute-start(bf16[4,8,16,256]{3,2,1,0:T(8,128)(2,1)S(1)} %pad_maximum_fusion.refs_0_), channel_id=1, source_target_pairs={{0,192},{64,0},{128,64},{192,128},{1,193},{65,1},{129,65},{193,129... | collective-permute-start | bytes 786440 | tf_op jit(solution)/shard_map/ppermute | solution.py:47
  51.3 10.1 %copy-start.24 = (bf16[128,512]{1,0:T(8,128)(2,1)}, bf16[128,512]{1,0:T(8,128)(2,1)S(1)}, u32[]{:S(2)}) copy-start(bf16[128,512]{1,0:T(8,128)(2,1)S(1)} %collective-permute-done.7.refs_7_) | copy-start | bytes 393220
  51.3 15.6 %collective-permute-start.18 = (bf16[4,8,16,256]{3,2,1,0:T(8,128)(2,1)S(1)}, bf16[4,8,16,256]{3,2,1,0:T(8,128)(2,1)}, u32[]{:S(2)}, u32[]{:S(2)}) collective-permute-start(bf16[4,8,16,256]{3,2,1,0:T(8,128)(2,1)S(1)} %pad_maximum_fusion.1.refs_4_), channel_id=1, source_target_pairs={{0,16},{16,32},{32,48},{48,0},{1,17},{17,33},{33,49},{49,1},{2,18}... | collective-permute-start | bytes 786440 | tf_op jit(solution)/shard_map/ppermute | solution.py:47
  51.9 15.0 %collective-permute-start.19 = (bf16[4,8,16,256]{3,2,1,0:T(8,128)(2,1)S(1)}, bf16[4,8,16,256]{3,2,1,0:T(8,128)(2,1)}, u32[]{:S(2)}, u32[]{:S(2)}) collective-permute-start(bf16[4,8,16,256]{3,2,1,0:T(8,128)(2,1)S(1)} %pad_maximum_fusion.1.refs_4_), channel_id=1, source_target_pairs={{0,32},{16,48},{32,0},{48,16},{1,33},{17,49},{33,1},{49,17},{2,34}... | collective-permute-start | bytes 786440 | tf_op jit(solution)/shard_map/ppermute | solution.py:47
  55.2 11.8 %collective-permute-start.20 = (bf16[4,8,16,256]{3,2,1,0:T(8,128)(2,1)S(1)}, bf16[4,8,16,256]{3,2,1,0:T(8,128)(2,1)}, u32[]{:S(2)}, u32[]{:S(2)}) collective-permute-start(bf16[4,8,16,256]{3,2,1,0:T(8,128)(2,1)S(1)} %pad_maximum_fusion.1.refs_4_), channel_id=1, source_target_pairs={{0,48},{16,0},{32,16},{48,32},{1,49},{17,1},{33,17},{49,33},{2,50}... | collective-permute-start | bytes 786440 | tf_op jit(solution)/shard_map/ppermute | solution.py:47
  67.0 12.1 %copy-start.1 = (bf16[256,1024]{1,0:T(8,128)(2,1)S(1)}, bf16[256,1024]{1,0:T(8,128)(2,1)}, u32[]{:S(2)}) copy-start(bf16[256,1024]{1,0:T(8,128)(2,1)} %q_own.1) | copy-start | bytes 1572868
  74.0 15.5 %all-to-all-start.1 = ((bf16[8,128,128]{2,1,0:T(8,128)(2,1)}), bf16[8,128,128]{2,1,0:T(8,128)(2,1)S(1)}, u32[]{:S(2)}, u32[]{:S(2)}) async-start(bf16[8,128,128]{2,1,0:T(8,128)(2,1)} %get-tuple-element.48), calls=%async_computation.1 | async-start | bytes 524288 | tf_op jit(solution)/shard_map/all_to_all | solution.py:409
  79.1 16.9 %copy-start.2 = (bf16[256,1024]{1,0:T(8,128)(2,1)S(1)}, bf16[256,1024]{1,0:T(8,128)(2,1)}, u32[]{:S(2)}) copy-start(bf16[256,1024]{1,0:T(8,128)(2,1)} %g_own.1) | copy-start | bytes 1572868
  79.1 1.6 collective-permute-start.21
  91.9 16.2 %all-to-all-start.2 = ((bf16[8,128,128]{2,1,0:T(8,128)(2,1)}), bf16[8,128,128]{2,1,0:T(8,128)(2,1)S(1)}, u32[]{:S(2)}, u32[]{:S(2)}) async-start(bf16[8,128,128]{2,1,0:T(8,128)(2,1)} %shard_map.79), calls=%async_computation.2 | async-start | bytes 524288 | tf_op jit(solution)/shard_map/all_to_all | solution.py:413
  96.0 1.6 collective-permute-start.22
  97.6 10.5 %copy-start.22 = (bf16[256,512]{1,0:T(8,128)(2,1)}, bf16[256,512]{1,0:T(8,128)(2,1)S(1)}, u32[]{:S(2)}) copy-start(bf16[256,512]{1,0:T(8,128)(2,1)S(1)} %collective-permute-done.22.g_sib) | copy-start | bytes 786436
  113.4 14.4 %all-to-all-start.3 = ((bf16[8,128,128]{2,1,0:T(8,128)(2,1)}), bf16[8,128,128]{2,1,0:T(8,128)(2,1)S(1)}, u32[]{:S(2)}, u32[]{:S(2)}) async-start(bf16[8,128,128]{2,1,0:T(8,128)(2,1)} %get-tuple-element.52), calls=%async_computation.3 | async-start | bytes 524288 | tf_op jit(solution)/shard_map/all_to_all | solution.py:409
  116.8 43.5 %collective-permute-start.25 = (bf16[8,16,16,512]{3,2,1,0:T(8,128)(2,1)}, bf16[8,16,16,512]{3,2,1,0:T(8,128)(2,1)}, u32[]{:S(2)}, u32[]{:S(2)}) collective-permute-start(bf16[8,16,16,512]{3,2,1,0:T(8,128)(2,1)} %get-tuple-element.59.wv), channel_id=1, source_target_pairs={{0,8},{8,0},{1,9},{9,1},{2,10},{10,2},{3,11},{11,3},{4,12},{12,4},... | collective-permute-start | bytes 6291464 | tf_op jit(solution)/shard_map/ppermute | solution.py:351
  116.9 45.6 %collective-permute-start.24 = (bf16[8,256,512]{2,1,0:T(8,128)(2,1)}, bf16[8,256,512]{2,1,0:T(8,128)(2,1)}, u32[]{:S(2)}, u32[]{:S(2)}) collective-permute-start(bf16[8,256,512]{2,1,0:T(8,128)(2,1)} %get-tuple-element.58.wk), channel_id=1, source_target_pairs={{0,8},{8,0},{1,9},{9,1},{2,10},{10,2},{3,11},{11,3},{4,12},{12,4},... | collective-permute-start | bytes 6291464 | tf_op jit(solution)/shard_map/ppermute | solution.py:351
  155.2 29.2 %collective-permute-start.23 = (bf16[256,2048]{1,0:T(8,128)(2,1)}, bf16[256,2048]{1,0:T(8,128)(2,1)}, u32[]{:S(2)}, u32[]{:S(2)}) collective-permute-start(bf16[256,2048]{1,0:T(8,128)(2,1)} %shard_map.84._), channel_id=1, source_target_pairs={{0,8},{8,0},{1,9},{9,1},{2,10},{10,2},{3,11},{11,3},{4,12},{12,4},... | collective-permute-start | bytes 3145736 | tf_op jit(solution)/shard_map/ppermute | solution.py:351
  155.2 26.8 %collective-permute-start.26 = (bf16[4,128,512]{2,1,0:T(8,128)(2,1)S(1)}, bf16[4,128,512]{2,1,0:T(8,128)(2,1)S(1)}, u32[]{:S(2)}, u32[]{:S(2)}) collective-permute-start(bf16[4,128,512]{2,1,0:T(8,128)(2,1)S(1)} %copy-done.32), channel_id=1, source_target_pairs={{0,16},{16,32},{32,48},{48,0},{1,17},{17,33},{33,49},{49,1},{2,18}... | collective-permute-start | bytes 1572872 | tf_op jit(solution)/shard_map/ppermute | solution.py:47
  156.4 45.1 %collective-permute-start.27 = (bf16[4,128,512]{2,1,0:T(8,128)(2,1)S(1)}, bf16[4,128,512]{2,1,0:T(8,128)(2,1)S(1)}, u32[]{:S(2)}, u32[]{:S(2)}) collective-permute-start(bf16[4,128,512]{2,1,0:T(8,128)(2,1)S(1)} %copy-done.13), channel_id=1, source_target_pairs={{0,32},{16,48},{32,0},{48,16},{1,33},{17,49},{33,1},{49,17},{2,34}... | collective-permute-start | bytes 1572872 | tf_op jit(solution)/shard_map/ppermute | solution.py:47
  160.3 41.2 %collective-permute-start.28 = (bf16[4,128,512]{2,1,0:T(8,128)(2,1)}, bf16[4,128,512]{2,1,0:T(8,128)(2,1)S(1)}, u32[]{:S(2)}, u32[]{:S(2)}) collective-permute-start(bf16[4,128,512]{2,1,0:T(8,128)(2,1)} %get-tuple-element.65), channel_id=1, source_target_pairs={{0,48},{16,0},{32,16},{48,32},{1,49},{17,1},{33,17},{49,33},{2,50}... | collective-permute-start | bytes 1572872 | tf_op jit(solution)/shard_map/ppermute | solution.py:47
  162.6 39.0 %collective-permute-start.29 = (bf16[4,128,512]{2,1,0:T(8,128)(2,1)}, bf16[4,128,512]{2,1,0:T(8,128)(2,1)S(1)}, u32[]{:S(2)}, u32[]{:S(2)}) collective-permute-start(bf16[4,128,512]{2,1,0:T(8,128)(2,1)} %get-tuple-element.67), channel_id=1, source_target_pairs={{0,64},{64,128},{128,192},{192,0},{1,65},{65,129},{129,193},{193,1... | collective-permute-start | bytes 1572872 | tf_op jit(solution)/shard_map/ppermute | solution.py:47
  182.0 19.4 %copy-start.11 = (bf16[4,128,512]{2,1,0:T(8,128)(2,1)}, bf16[4,128,512]{2,1,0:T(8,128)(2,1)S(1)}, u32[]{:S(2)}) copy-start(bf16[4,128,512]{2,1,0:T(8,128)(2,1)S(1)} %collective-permute-done.26.refs_1_) | copy-start | bytes 1572868
  182.0 19.5 %collective-permute-start.30 = (bf16[4,128,512]{2,1,0:T(8,128)(2,1)}, bf16[4,128,512]{2,1,0:T(8,128)(2,1)S(1)}, u32[]{:S(2)}, u32[]{:S(2)}) collective-permute-start(bf16[4,128,512]{2,1,0:T(8,128)(2,1)} %get-tuple-element.68), channel_id=1, source_target_pairs={{0,128},{64,192},{128,0},{192,64},{1,129},{65,193},{129,1},{193,65... | collective-permute-start | bytes 1572872 | tf_op jit(solution)/shard_map/ppermute | solution.py:47
  184.5 23.0 %collective-permute-start.31 = (bf16[4,128,512]{2,1,0:T(8,128)(2,1)}, bf16[4,128,512]{2,1,0:T(8,128)(2,1)}, u32[]{:S(2)}, u32[]{:S(2)}) collective-permute-start(bf16[4,128,512]{2,1,0:T(8,128)(2,1)} %get-tuple-element.69), channel_id=1, source_target_pairs={{0,192},{64,0},{128,64},{192,128},{1,193},{65,1},{129,65},{193,129... | collective-permute-start | bytes 1572872 | tf_op jit(solution)/shard_map/ppermute | solution.py:47
  201.5 6.0 %copy-start.12 = (bf16[4,128,512]{2,1,0:T(8,128)(2,1)}, bf16[4,128,512]{2,1,0:T(8,128)(2,1)S(1)}, u32[]{:S(2)}) copy-start(bf16[4,128,512]{2,1,0:T(8,128)(2,1)S(1)} %collective-permute-done.27.refs_2_) | copy-start | bytes 1572868
  201.5 6.0 %copy-start.14 = (bf16[4,128,512]{2,1,0:T(8,128)(2,1)}, bf16[4,128,512]{2,1,0:T(8,128)(2,1)S(1)}, u32[]{:S(2)}) copy-start(bf16[4,128,512]{2,1,0:T(8,128)(2,1)S(1)} %collective-permute-done.28.refs_3_) | copy-start | bytes 1572868
  201.5 6.0 %copy-start.15 = (bf16[4,128,512]{2,1,0:T(8,128)(2,1)}, bf16[4,128,512]{2,1,0:T(8,128)(2,1)S(1)}, u32[]{:S(2)}) copy-start(bf16[4,128,512]{2,1,0:T(8,128)(2,1)S(1)} %collective-permute-done.29.refs_5_) | copy-start | bytes 1572868
  201.5 5.9 %copy-start.16 = (bf16[4,128,512]{2,1,0:T(8,128)(2,1)}, bf16[4,128,512]{2,1,0:T(8,128)(2,1)S(1)}, u32[]{:S(2)}) copy-start(bf16[4,128,512]{2,1,0:T(8,128)(2,1)S(1)} %collective-permute-done.30.refs_6_) | copy-start | bytes 1572868
  211.1 7.0 %collective-permute-start.32 = (bf16[128,512]{1,0:T(8,128)(2,1)}, bf16[128,512]{1,0:T(8,128)(2,1)S(1)}, u32[]{:S(2)}, u32[]{:S(2)}) collective-permute-start(bf16[128,512]{1,0:T(8,128)(2,1)} %get-tuple-element.71), channel_id=1, source_target_pairs={{0,64},{64,128},{128,192},{192,0},{1,65},{65,129},{129,193},{193,1... | collective-permute-start | bytes 393224 | tf_op jit(solution)/shard_map/ppermute | solution.py:47
  212.9 8.8 %collective-permute-start.33 = (bf16[128,512]{1,0:T(8,128)(2,1)}, bf16[128,512]{1,0:T(8,128)(2,1)S(1)}, u32[]{:S(2)}, u32[]{:S(2)}) collective-permute-start(bf16[128,512]{1,0:T(8,128)(2,1)} %get-tuple-element.72), channel_id=1, source_target_pairs={{0,128},{64,192},{128,0},{192,64},{1,129},{65,193},{129,1},{193,65... | collective-permute-start | bytes 393224 | tf_op jit(solution)/shard_map/ppermute | solution.py:47
  215.3 6.4 %collective-permute-start.34 = (bf16[128,512]{1,0:T(8,128)(2,1)}, bf16[128,512]{1,0:T(8,128)(2,1)S(1)}, u32[]{:S(2)}, u32[]{:S(2)}) collective-permute-start(bf16[128,512]{1,0:T(8,128)(2,1)} %get-tuple-element.73), channel_id=1, source_target_pairs={{0,192},{64,0},{128,64},{192,128},{1,193},{65,1},{129,65},{193,129... | collective-permute-start | bytes 393224 | tf_op jit(solution)/shard_map/ppermute | solution.py:47
  217.2 7.8 %collective-permute-start.35 = (bf16[128,512]{1,0:T(8,128)(2,1)}, bf16[128,512]{1,0:T(8,128)(2,1)S(1)}, u32[]{:S(2)}, u32[]{:S(2)}) collective-permute-start(bf16[128,512]{1,0:T(8,128)(2,1)} %get-tuple-element.75), channel_id=1, source_target_pairs={{0,16},{16,32},{32,48},{48,0},{1,17},{17,33},{33,49},{49,1},{2,18}... | collective-permute-start | bytes 393224 | tf_op jit(solution)/shard_map/ppermute | solution.py:47
  217.2 7.8 %collective-permute-start.36 = (bf16[128,512]{1,0:T(8,128)(2,1)}, bf16[128,512]{1,0:T(8,128)(2,1)S(1)}, u32[]{:S(2)}, u32[]{:S(2)}) collective-permute-start(bf16[128,512]{1,0:T(8,128)(2,1)} %get-tuple-element.76), channel_id=1, source_target_pairs={{0,32},{16,48},{32,0},{48,16},{1,33},{17,49},{33,1},{49,17},{2,34}... | collective-permute-start | bytes 393224 | tf_op jit(solution)/shard_map/ppermute | solution.py:47
  218.1 7.8 %copy-start.26 = (bf16[128,512]{1,0:T(8,128)(2,1)}, bf16[128,512]{1,0:T(8,128)(2,1)S(1)}, u32[]{:S(2)}) copy-start(bf16[128,512]{1,0:T(8,128)(2,1)S(1)} %collective-permute-done.32.refs_1_) | copy-start | bytes 393220
  218.1 7.8 %collective-permute-start.37 = (bf16[128,512]{1,0:T(8,128)(2,1)}, bf16[128,512]{1,0:T(8,128)(2,1)S(1)}, u32[]{:S(2)}, u32[]{:S(2)}) collective-permute-start(bf16[128,512]{1,0:T(8,128)(2,1)} %get-tuple-element.77), channel_id=1, source_target_pairs={{0,48},{16,0},{32,16},{48,32},{1,49},{17,1},{33,17},{49,33},{2,50}... | collective-permute-start | bytes 393224 | tf_op jit(solution)/shard_map/ppermute | solution.py:47
  221.7 4.2 %copy-start.27 = (bf16[128,512]{1,0:T(8,128)(2,1)}, bf16[128,512]{1,0:T(8,128)(2,1)S(1)}, u32[]{:S(2)}) copy-start(bf16[128,512]{1,0:T(8,128)(2,1)S(1)} %collective-permute-done.33.refs_2_) | copy-start | bytes 393220
  221.7 4.2 %copy-start.28 = (bf16[128,512]{1,0:T(8,128)(2,1)}, bf16[128,512]{1,0:T(8,128)(2,1)S(1)}, u32[]{:S(2)}) copy-start(bf16[128,512]{1,0:T(8,128)(2,1)S(1)} %collective-permute-done.34.refs_3_) | copy-start | bytes 393220
  (11 other events, 16.0 us)

commit v2 on v1

--- a/solution.py
+++ b/solution.py
@@ -74,15 +74,12 @@
 
 
 def key_kernel(tok, *refs):
-    shards, (w_out, key, w_ref, sems, out_sem) = refs[:9], refs[9:]
+    shards, (w_out, key, w_ref, sems, out_sem) = refs[:8], refs[8:]
     z = lax.axis_index("z")
     copies = []
-    for n, step in enumerate((0, -1, 1, -2, 2, -3, 3)):
+    for n, step in enumerate((0, -1, 1, -2, 2, -3, 3, 4)):
         to = w_ref.at[lax.rem(z + step + 8, 8)]
         copies.append(pltpu.make_async_copy(shards[n], to, sems.at[n]))
-    for n in range(2):
-        to = w_ref.at[lax.rem(z + 4, 8), pl.ds(n * 128, 128)]
-        copies.append(pltpu.make_async_copy(shards[7 + n], to, sems.at[7 + n]))
     for c in copies:
         c.start()
     for c in copies:
@@ -248,8 +245,15 @@
 
 
 def own_kernel(turned, dkv, _, a_ref, b_ref):
-    a_ref[...] = chunk(0, 0, turned, dkv)
-    b_ref[...] = chunk(1, 0, turned, dkv)
+    y, x = lax.axis_index("y"), lax.axis_index("x")
+
+    def step(n, _):
+        for to, chip, half in ((a_ref, n * 4 + x, 0), (b_ref, y * 4 + n, 1)):
+            part = dot(turned[chip], dkv[:, half * 512 : half * 512 + 512], 1, 0)
+            to[n] = part.astype(BF)
+        return 0
+
+    lax.fori_loop(0, 4, step, 0)
 
 
 def pack_kernel(dkv, dq, out, _, back):
@@ -310,8 +314,8 @@
 
 def token_kernel(dkv, got, o, dq, wk, wk_sib, wv, wv_sib, out, o_out, dq_out):
     total = dot(dkv[:256, :512], wk[0], 1, 1) + dot(got[:, :512], wk_sib[0], 1, 1)
-    total += dot(dkv[:256, 512:], wv[0].reshape(128, 512), 1, 1)
-    total += dot(got[:, 512:1024], wv_sib[0].reshape(128, 512), 1, 1)
+    total += dot(dkv[:256, 512:], wv[0].reshape(256, 512), 1, 1)
+    total += dot(got[:, 512:1024], wv_sib[0].reshape(256, 512), 1, 1)
     out[...] = total.astype(BF)
 
     @pl.when(pl.program_id(0) == 0)
@@ -329,14 +333,14 @@
     def fixed(shape):
         return pl.BlockSpec(shape, lambda n: (0,) * len(shape))
 
-    tile_k = pl.BlockSpec((1, 128, 512), lambda n: (n // 2, n % 2, 0))
-    tile_v = pl.BlockSpec((1, 8, 16, 512), lambda n: (n // 2, n % 2, 0, 0))
+    tile_k = pl.BlockSpec((1, 256, 512), lambda n: (n, 0, 0))
+    tile_v = pl.BlockSpec((1, 16, 16, 512), lambda n: (n, 0, 0, 0))
     return pl.pallas_call(
         token_kernel,
-        grid=(16,),
+        grid=(8,),
         out_shape=[jax.ShapeDtypeStruct((rows, n), BF) for n in (2048, 1024, 1024)],
         in_specs=[fixed(a.shape) for a in args[:4]] + [tile_k] * 2 + [tile_v] * 2,
-        out_specs=[pl.BlockSpec((rows, 128), lambda n: (0, n))] + [fixed((rows, 1024))] * 2,
+        out_specs=[pl.BlockSpec((rows, 256), lambda n: (0, n))] + [fixed((rows, 1024))] * 2,
         cost_estimate=pl.CostEstimate(
             flops=4 * 2 * rows * 2048 * 2048, bytes_accessed=12 << 20, transcendentals=0
         ),
@@ -358,10 +362,11 @@
     for _ in range(3):
         left, right = shift(left, "z", 1), shift(right, "z", -1)
         shards += [left, right]
-    shards += [shift(left[:128], "z", 1), shift(right[128:], "z", -1)]
+    shards.append(shift(left, "z", 1))
     place = lax.axis_index(("y", "x"))
     mine = lax.dynamic_slice(kv_weight, (place * 16, 1024 + core * 512), (16, 512))
-    along_z = lax.all_to_all(jnp.broadcast_to(mine[None], (8, 16, 512)), "z", 0, 0, tiled=True)
+    mine = jnp.broadcast_to(mine[None], (8, 16, 512))
+    along_z = lax.all_to_all(mine, "z", 0, 0, tiled=True)
     a0, b0 = along_z[:, :, :256], along_z[:, :, 256:]
     (a2, b2), (a1, b1), (a3, b3) = [(shift(a0, "x", d), shift(b0, "y", d)) for d in (2, 1, 3)]
     a = jnp.stack([a0, a1, a2, a3])
@@ -382,11 +387,11 @@
         key_kernel,
         [((8, 256, 512), BF), half],
         both, *shards,
-        in_specs=[VMEM] + [ANY] * 9,
+        in_specs=[VMEM] + [ANY] * 8,
         out_specs=[ANY, VMEM],
         scratch=[
             pltpu.VMEM((8, 256, 512), BF),
-            pltpu.SemaphoreType.DMA((9,)),
+            pltpu.SemaphoreType.DMA((8,)),
             pltpu.SemaphoreType.DMA(()),
         ],
         flops=2 * 512 * 2048 * 512,

time: 249 us -> 253 us (1.016)
  waiting for transfers between devices: 63.8 us -> 76.4 us
  Pallas kernels: 72.6 us -> 68 us
  starting transfers between devices: 70.7 us -> 67.7 us
    ppermute x32 -> x31, waiting for transfers between devices: 36.6 us -> 49.3 us  [shift(): return lax.ppermute(x, axis, [(i, (i + step) % size) for i in range(size)])]
    pallas_call x1, Pallas kernels: 15.1 us -> 9.79 us  [token_call(): pl.pallas_call(token_kernel, grid=(8,), out_shape=[jax.ShapeDtypeStruct((...]
    ppermute x32 -> x31, starting transfers between devices: 51.6 us -> 50 us  [shift(): return lax.ppermute(x, axis, [(i, (i + step) % size) for i in range(size)])]
  transfers between devices with their start and end apart: 42 -> 41, of which waited for: 15 -> 18; matrix products, arithmetic and copies ran while one was open for 1% -> 1% of each run, Pallas kernels for 21% -> 19%
where the time goes in v2:
time: 253 us; the launch traced here: 250 us
  waiting for transfers between devices  76.4 us (30%)
  Pallas kernels  68 us (27%)
  starting transfers between devices  67.7 us (27%)
  blocking collectives  29.9 us (12%)
  local copies, waits for them, and re-layouts  6.64 us (3%)
    pallas_call x14, Pallas kernels, call(): pl.pallas_call(body, out_shape=[jax.ShapeDtypeStruct(s, d) for s, d in ou...  58.2 us
    ppermute x31, starting transfers between devices, shift(): return lax.ppermute(x, axis, [(i, (i + step) % size) for i in range(size)])  50 us
    ppermute x31, waiting for transfers between devices, shift(): return lax.ppermute(x, axis, [(i, (i + step) % size) for i in range(size)])  49.3 us
    all_to_all x1, blocking collectives, exchange(): return lax.all_to_all(x, 'z', 0, 0, tiled=True)  15.2 us
    all_to_all x1, blocking collectives, on_device(): column = lax.all_to_all(column, ('core', 'z'), 0, 0, tiled=True)  14.7 us
    all_to_all x1, waiting for transfers between devices, exchange(): return lax.all_to_all(x, 'z', 0, 0, tiled=True)  10.5 us
    pallas_call x1, Pallas kernels, token_call(): pl.pallas_call(token_kernel, grid=(8,), out_shape=[jax.ShapeDtypeStruct((...  9.79 us
    all_to_all x2, waiting for transfers between devices, exchange(): x = lax.all_to_all(x, 'z', 0, 0, tiled=True)  7.07 us
  transfers between devices with their start and end apart: 41, of which 18 were waited for; matrix products, arithmetic and copies ran while one was open for 1% of the time, Pallas kernels for 19%

profile of v2, /device:TPU:0, one launch (start us, length us, event | category | flops | bytes accessed | tf_op | source)
XLA Modules:
  0.0 249.7 jit_solution(9707331008549740841)
XLA Ops:
  0.6 1.0 constant_dynamic-slice_fusion.2.refs_0_
  1.9 4.1 %collective-permute-start.2 = (bf16[256,512]{1,0:T(8,128)(2,1)S(1)}, bf16[256,512]{1,0:T(8,128)(2,1)S(1)}, u32[]{:S(2)}, u32[]{:S(2)}) collective-permute-start(bf16[256,512]{1,0:T(8,128)(2,1)S(1)} %constant_dynamic-slice_fusion.2.refs_0_), channel_id=1, source_target_pairs={{0,7},{1,0},{2,1},{3,2},{4,3},{5,4},{6,5},{7,6},{8,15},{9,8},{10,9... | collective-permute-start | bytes 786440 | tf_op jit(solution)/shard_map/ppermute | solution.py:47
  6.0 6.1 %collective-permute-done.1.refs_1_ = bf16[256,512]{1,0:T(8,128)(2,1)S(1)} collective-permute-done((bf16[256,512]{1,0:T(8,128)(2,1)S(1)}, bf16[256,512]{1,0:T(8,128)(2,1)S(1)}, u32[]{:S(2)}, u32[]{:S(2)}) %collective-permute-start.1) | collective-permute-done | bytes 262176 | tf_op jit(solution)/shard_map/ppermute | solution.py:47
  12.2 0.7 dynamic_slice.13
  13.5 6.1 %all-to-all-start = ((bf16[8,16,512]{2,1,0:T(8,128)(2,1)}), bf16[8,16,512]{2,1,0:T(8,128)(2,1)S(1)}, u32[]{:S(2)}, u32[]{:S(2)}) async-start(bf16[8,16,512]{2,1,0:T(8,128)(2,1)} %broadcast_in_dim.2), calls=%async_computation | async-start | bytes 262144 | tf_op jit(solution)/shard_map/all_to_all | solution.py:369
  19.7 3.3 %collective-permute-start.4 = (bf16[256,512]{1,0:T(8,128)(2,1)S(1)}, bf16[256,512]{1,0:T(8,128)(2,1)S(1)}, u32[]{:S(2)}, u32[]{:S(2)}) collective-permute-start(bf16[256,512]{1,0:T(8,128)(2,1)S(1)} %collective-permute-done.2.refs_2_), channel_id=1, source_target_pairs={{0,7},{1,0},{2,1},{3,2},{4,3},{5,4},{6,5},{7,6},{8,15},{9,8},{10,9... | collective-permute-start | bytes 786440 | tf_op jit(solution)/shard_map/ppermute | solution.py:47
  23.0 6.5 %all-to-all-done = bf16[8,16,512]{2,1,0:T(8,128)(2,1)S(1)} async-done(((bf16[8,16,512]{2,1,0:T(8,128)(2,1)}), bf16[8,16,512]{2,1,0:T(8,128)(2,1)S(1)}, u32[]{:S(2)}, u32[]{:S(2)}) %all-to-all-start) | async-done | bytes 131104 | tf_op jit(solution)/shard_map/all_to_all | solution.py:369
  29.5 1.6 collective-permute-start.8
  31.1 2.7 %collective-permute-start.9 = (bf16[8,16,256]{2,1,0:T(8,128)(2,1)S(1)}, bf16[8,16,256]{2,1,0:T(8,128)(2,1)S(1)}, u32[]{:S(2)}, u32[]{:S(2)}) collective-permute-start(bf16[8,16,256]{2,1,0:T(8,128)(2,1)S(1)} %get-tuple-element.81), channel_id=1, source_target_pairs={{0,32},{16,48},{32,0},{48,16},{1,33},{17,49},{33,1},{49,17},{2,34}... | collective-permute-start | bytes 196616 | tf_op jit(solution)/shard_map/ppermute | solution.py:47
  33.8 1.3 collective-permute-done.8
  35.1 1.5 collective-permute-start.10
  36.8 1.6 collective-permute-start.14
  38.4 0.9 collective-permute-done.10
  39.4 1.7 collective-permute-start.11
  41.5 1.6 collective-permute-start.7
  43.1 2.9 %collective-permute-start.15 = (bf16[8,16,256]{2,1,0:T(8,128)(2,1)S(1)}, bf16[8,16,256]{2,1,0:T(8,128)(2,1)S(1)}, u32[]{:S(2)}, u32[]{:S(2)}) collective-permute-start(bf16[8,16,256]{2,1,0:T(8,128)(2,1)S(1)} %get-tuple-element.80), channel_id=1, source_target_pairs={{0,128},{64,192},{128,0},{192,64},{1,129},{65,193},{129,1},{193,65... | collective-permute-start | bytes 196616 | tf_op jit(solution)/shard_map/ppermute | solution.py:47
  45.9 3.0 %collective-permute-done.15 = bf16[8,16,256]{2,1,0:T(8,128)(2,1)S(1)} collective-permute-done((bf16[8,16,256]{2,1,0:T(8,128)(2,1)S(1)}, bf16[8,16,256]{2,1,0:T(8,128)(2,1)S(1)}, u32[]{:S(2)}, u32[]{:S(2)}) %collective-permute-start.15) | collective-permute-done | bytes 65568 | tf_op jit(solution)/shard_map/ppermute | solution.py:47
  48.9 1.6 collective-permute-start.16
  50.5 3.4 %collective-permute-done.16 = bf16[8,16,256]{2,1,0:T(8,128)(2,1)S(1)} collective-permute-done((bf16[8,16,256]{2,1,0:T(8,128)(2,1)S(1)}, bf16[8,16,256]{2,1,0:T(8,128)(2,1)S(1)}, u32[]{:S(2)}, u32[]{:S(2)}) %collective-permute-start.16) | collective-permute-done | bytes 65568 | tf_op jit(solution)/shard_map/ppermute | solution.py:47
  53.9 2.8 %collective-permute-start.12 = (bf16[4,8,16,256]{3,2,1,0:T(8,128)(2,1)S(1)}, bf16[4,8,16,256]{3,2,1,0:T(8,128)(2,1)}, u32[]{:S(2)}, u32[]{:S(2)}) collective-permute-start(bf16[4,8,16,256]{3,2,1,0:T(8,128)(2,1)S(1)} %pad_maximum_fusion.refs_0_), channel_id=1, source_target_pairs={{0,128},{64,192},{128,0},{192,64},{1,129},{65,193},{129,1},{193,65... | collective-permute-start | bytes 786440 | tf_op jit(solution)/shard_map/ppermute | solution.py:47
  56.7 1.6 collective-permute-start.13
  58.7 3.9 %collective-permute-start.18 = (bf16[4,8,16,256]{3,2,1,0:T(8,128)(2,1)S(1)}, bf16[4,8,16,256]{3,2,1,0:T(8,128)(2,1)}, u32[]{:S(2)}, u32[]{:S(2)}) collective-permute-start(bf16[4,8,16,256]{3,2,1,0:T(8,128)(2,1)S(1)} %pad_maximum_fusion.1.refs_4_), channel_id=1, source_target_pairs={{0,32},{16,48},{32,0},{48,16},{1,33},{17,49},{33,1},{49,17},{2,34}... | collective-permute-start | bytes 786440 | tf_op jit(solution)/shard_map/ppermute | solution.py:47
  63.6 5.2 %shard_map.75 = (bf16[512,2048]{1,0:T(8,128)(2,1)}, bf16[16,128,512]{2,1,0:T(8,128)(2,1)}) custom-call(bf16[256,2048]{1,0:T(8,128)(2,1)} %own.1, bf16[256,2048]{1,0:T(8,128)(2,1)} %copy-done.6), custom_call_target="tpu_custom_call" | custom-call | bytes 6291456 | tf_op jit(solution)/shard_map/pallas_call | solution.py:35
  68.9 5.4 %shard_map.76 = (bf16[8,256,512]{2,1,0:T(8,128)(2,1)}, bf16[512,512]{1,0:T(8,128)(2,1)}) custom-call(bf16[512,2048]{1,0:T(8,128)(2,1)} %get-tuple-element.41.tok, bf16[256,512]{1,0:T(8,128)(2,1)} %copy-done.3, bf16[256,512]{1,0:T(8,128)(2,1)} %copy-done.15, bf16[256,512]{1,0:T(8,128)(2,1)} %copy-done.16, bf16[256,512]{1,0:T(8,128)(2,1)} %copy-done.17, ...), custom_call_target="tpu_custom_call" | custom-call | flops 1073741824 | bytes 6815744 | tf_op jit(solution)/shard_map/pallas_call | solution.py:35
  74.4 7.0 %shard_map.77 = (bf16[8,16,16,512]{3,2,1,0:T(8,128)(2,1)}, bf16[512,512]{1,0:T(8,128)(2,1)}, bf16[8,128,128]{2,1,0:T(8,128)(2,1)}) custom-call(bf16[512,2048]{1,0:T(8,128)(2,1)} %get-tuple-element.41.tok, bf16[512,512]{1,0:T(8,128)(2,1)} %get-tuple-element.42.key, bf16[4,8,16,256]{3,2,1,0:T(8,128)(2,1)} %copy-done.4, bf16[4,8,16,256]{3,2,1,0:T(8,128)(2,1)} %copy-done.20, ...), custom_call_target="tpu_custom_call" | custom-call | flops 1073741824 | bytes 7602176 | tf_op jit(solution)/shard_map/pallas_call | solution.py:35
  81.4 3.4 %all-to-all-start.1 = ((bf16[8,128,128]{2,1,0:T(8,128)(2,1)}), bf16[8,128,128]{2,1,0:T(8,128)(2,1)S(1)}, u32[]{:S(2)}, u32[]{:S(2)}) async-start(bf16[8,128,128]{2,1,0:T(8,128)(2,1)} %get-tuple-element.48), calls=%async_computation.1 | async-start | bytes 524288 | tf_op jit(solution)/shard_map/all_to_all | solution.py:414
  85.0 1.5 collective-permute-done.20.q_sib
  86.5 0.7 copy-done.24
  87.2 4.9 %shard_map.78 = (bf16[512,512]{1,0:T(8,128)(2,1)}, bf16[512,512]{1,0:T(8,128)(2,1)}, bf16[8,256,256]{2,1,0:T(8,128)(2,1)}, f32[512,512]{1,0:T(8,128)}) custom-call(bf16[256,1024]{1,0:T(8,128)(2,1)} %q_own.1, bf16[256,512]{1,0:T(8,128)(2,1)} %copy-done.24, bf16[512,512]{1,0:T(8,128)(2,1)} %get-tuple-element.42.key, bf16[512,512]{1,0:T(8,128)(2,1)} %get-tuple-element.43.val), custom_call_target="tpu_custom_call" | custom-call | flops 268435456 | bytes 4980736 | tf_op jit(solution)/shard_map/pallas_call | solution.py:35
  92.1 3.1 %all-to-all-done.1.i = bf16[8,128,128]{2,1,0:T(8,128)(2,1)S(1)} async-done(((bf16[8,128,128]{2,1,0:T(8,128)(2,1)}), bf16[8,128,128]{2,1,0:T(8,128)(2,1)S(1)}, u32[]{:S(2)}, u32[]{:S(2)}) %all-to-all-start.1) | async-done | bytes 262176 | tf_op jit(solution)/shard_map/all_to_all | solution.py:414
  95.2 0.7 copy-done.7
  95.9 1.7 shard_map.79
  97.6 4.0 %all-to-all-start.2 = ((bf16[8,128,128]{2,1,0:T(8,128)(2,1)}), bf16[8,128,128]{2,1,0:T(8,128)(2,1)S(1)}, u32[]{:S(2)}, u32[]{:S(2)}) async-start(bf16[8,128,128]{2,1,0:T(8,128)(2,1)} %shard_map.79), calls=%async_computation.2 | async-start | bytes 524288 | tf_op jit(solution)/shard_map/all_to_all | solution.py:418
  101.8 1.5 collective-permute-done.21.g_sib
  103.3 10.5 %all-to-all-done.2.before = bf16[8,128,128]{2,1,0:T(8,128)(2,1)S(1)} async-done(((bf16[8,128,128]{2,1,0:T(8,128)(2,1)}), bf16[8,128,128]{2,1,0:T(8,128)(2,1)S(1)}, u32[]{:S(2)}, u32[]{:S(2)}) %all-to-all-start.2) | async-done | bytes 262176 | tf_op jit(solution)/shard_map/all_to_all | solution.py:418
  113.8 0.7 copy-done
  114.5 4.6 %shard_map.80 = (bf16[512,512]{1,0:T(8,128)(2,1)}, bf16[512,512]{1,0:T(8,128)(2,1)}, bf16[8,128,128]{2,1,0:T(8,128)(2,1)}) custom-call(bf16[512,512]{1,0:T(8,128)(2,1)} %get-tuple-element.45.qf, bf16[256,1024]{1,0:T(8,128)(2,1)} %g_own.1, bf16[256,512]{1,0:T(8,128)(2,1)} %copy-done.23, f32[512,512]{1,0:T(8,128)} %get-tuple-element.47._.local, ...), custom_call_target="tpu_custom_call" | custom-call | flops 134217728 | bytes 3932160 | tf_op jit(solution)/shard_map/pallas_call | solution.py:35
  119.1 3.4 %all-to-all-start.3 = ((bf16[8,128,128]{2,1,0:T(8,128)(2,1)}), bf16[8,128,128]{2,1,0:T(8,128)(2,1)S(1)}, u32[]{:S(2)}, u32[]{:S(2)}) async-start(bf16[8,128,128]{2,1,0:T(8,128)(2,1)} %get-tuple-element.52), calls=%async_computation.3 | async-start | bytes 524288 | tf_op jit(solution)/shard_map/all_to_all | solution.py:414
  123.1 6.4 %shard_map.81 = (bf16[512,512]{1,0:T(8,128)(2,1)}, f32[512,512]{1,0:T(8,128)}, f32[512,512]{1,0:T(8,128)}) custom-call(bf16[512,512]{1,0:T(8,128)(2,1)} %get-tuple-element.44.qu, bf16[512,512]{1,0:T(8,128)(2,1)} %get-tuple-element.45.qf, bf16[512,512]{1,0:T(8,128)(2,1)} %get-tuple-element.42.key, bf16[512,512]{1,0:T(8,128)(2,1)} %get-tuple-element.43.val, ...), custom_call_target="tpu_custom_call" | custom-call | flops 671088640 | bytes 6553600 | tf_op jit(solution)/shard_map/pallas_call | solution.py:35
  129.6 4.0 %all-to-all-done.3.i = bf16[8,128,128]{2,1,0:T(8,128)(2,1)S(1)} async-done(((bf16[8,128,128]{2,1,0:T(8,128)(2,1)}), bf16[8,128,128]{2,1,0:T(8,128)(2,1)S(1)}, u32[]{:S(2)}, u32[]{:S(2)}) %all-to-all-start.3) | async-done | bytes 262176 | tf_op jit(solution)/shard_map/all_to_all | solution.py:414
  134.3 1.7 shard_map.82
  135.9 15.2 %all_to_all.30.after = bf16[8,128,128]{2,1,0:T(8,128)(2,1)} all-to-all(bf16[8,128,128]{2,1,0:T(8,128)(2,1)} %shard_map.82), channel_id=1, replica_groups=mesh['y'=4,'x'=4,'core'=2,'z'=8] {'z'}, dimensions={0} | all-to-all | bytes 524288 | tf_op jit(solution)/shard_map/all_to_all | solution.py:418
  151.1 7.1 %shard_map.83 = (bf16[512,1024]{1,0:T(8,128)(2,1)}, bf16[4,128,512]{2,1,0:T(8,128)(2,1)}, bf16[4,128,512]{2,1,0:T(8,128)(2,1)}, bf16[4,128,512]{2,1,0:T(8,128)(2...) custom-call(bf16[512,512]{1,0:T(8,128)(2,1)} %get-tuple-element.42.key, ...), custom_call_target="tpu_custom_call" | custom-call | flops 2147483648 | bytes 9699328 | tf_op jit(solution)/shard_map/pallas_call | solution.py:35
  158.3 2.6 %shard_map.84._ = bf16[256,2048]{1,0:T(8,128)(2,1)} custom-call(bf16[512,1024]{1,0:T(8,128)(2,1)} %get-tuple-element.54.dkv, bf16[512,512]{1,0:T(8,128)(2,1)} %get-tuple-element.55.dq, bf16[512,512]{1,0:T(8,128)(2,1)} %get-tuple-element.56.out.o, bf16[4,128,512]{2,1,0:T(8,128)(2,1)} %get-tuple-element.57._), custom_call_target="tpu_custom_call" | custom-call | bytes 3670016 | tf_op jit(solution)/shard_map/pallas_call | solution.py:35
  160.9 1.1 collective-permute-start.25
  162.7 4.0 %shard_map.86 = (bf16[4,128,512]{2,1,0:T(8,128)(2,1)}, bf16[4,128,512]{2,1,0:T(8,128)(2,1)}) custom-call(bf16[16,128,512]{2,1,0:T(8,128)(2,1)} %get-tuple-element.53.turned_hbm.turned, bf16[512,1024]{1,0:T(8,128)(2,1)} %get-tuple-element.54.dkv, bf16[256,2048]{1,0:T(8,128)(2,1)} %shard_map.84._), custom_call_target="tpu_custom_call" | custom-call | flops 536870912 | bytes 5242880 | tf_op jit(solution)/shard_map/pallas_call | solution.py:35
  166.8 2.2 collective-permute-start.27
  169.6 18.1 %collective-permute-done.25.refs_1_ = bf16[4,128,512]{2,1,0:T(8,128)(2,1)S(1)} collective-permute-done((bf16[4,128,512]{2,1,0:T(8,128)(2,1)S(1)}, bf16[4,128,512]{2,1,0:T(8,128)(2,1)S(1)}, u32[]{:S(2)}, u32[]{:S(2)}) %collective-permute-start.25) | collective-permute-done | bytes 524320 | tf_op jit(solution)/shard_map/ppermute | solution.py:47
  187.7 1.6 collective-permute-start.29
  189.3 1.8 collective-permute-start.30
  191.1 9.8 %shard_map.85 = (bf16[256,2048]{1,0:T(8,128)(2,1)}, bf16[256,1024]{1,0:T(8,128)(2,1)}, bf16[256,1024]{1,0:T(8,128)(2,1)}) custom-call(bf16[512,1024]{1,0:T(8,128)(2,1)} %get-tuple-element.54.dkv, bf16[256,2048]{1,0:T(8,128)(2,1)} %collective-permute-done.22.got, bf16[512,512]{1,0:T(8,128)(2,1)} %get-tuple-element.56.out.o, ...), custom_call_target="tpu_custom_call" | custom-call | flops 8589934592 | bytes 12582912 | tf_op jit(solution)/shard_map/pallas_call | solution.py:338
  201.0 2.0 collective-permute-done.29.refs_6_
  202.9 8.8 %collective-permute-done.30.refs_7_ = bf16[4,128,512]{2,1,0:T(8,128)(2,1)} collective-permute-done((bf16[4,128,512]{2,1,0:T(8,128)(2,1)}, bf16[4,128,512]{2,1,0:T(8,128)(2,1)}, u32[]{:S(2)}, u32[]{:S(2)}) %collective-permute-start.30) | collective-permute-done | bytes 524320 | tf_op jit(solution)/shard_map/ppermute | solution.py:47
  211.8 3.6 %shard_map.87 = (f32[128,512]{1,0:T(8,128)}, bf16[128,512]{1,0:T(8,128)(2,1)}, bf16[128,512]{1,0:T(8,128)(2,1)}, bf16[128,512]{1,0:T(8,128)(2,1)}, f32[128,512]{...) custom-call(bf16[4,128,512]{2,1,0:T(8,128)(2,1)} %get-tuple-element.63.refs_0_, ...), custom_call_target="tpu_custom_call" | custom-call | bytes 6553600 | tf_op jit(solution)/shard_map/pallas_call | solution.py:35
  215.4 2.6 %collective-permute-start.31 = (bf16[128,512]{1,0:T(8,128)(2,1)}, bf16[128,512]{1,0:T(8,128)(2,1)S(1)}, u32[]{:S(2)}, u32[]{:S(2)}) collective-permute-start(bf16[128,512]{1,0:T(8,128)(2,1)} %get-tuple-element.71), channel_id=1, source_target_pairs={{0,64},{64,128},{128,192},{192,0},{1,65},{65,129},{129,193},{193,1... | collective-permute-start | bytes 393224 | tf_op jit(solution)/shard_map/ppermute | solution.py:47
  218.0 1.6 collective-permute-start.32
  219.6 2.4 collective-permute-start.33
  221.9 0.9 collective-permute-start.35
  222.8 2.5 collective-permute-start.36
  226.0 3.8 %collective-permute-done.34.refs_5_ = bf16[128,512]{1,0:T(8,128)(2,1)S(1)} collective-permute-done((bf16[128,512]{1,0:T(8,128)(2,1)}, bf16[128,512]{1,0:T(8,128)(2,1)S(1)}, u32[]{:S(2)}, u32[]{:S(2)}) %collective-permute-start.34) | collective-permute-done | bytes 131104 | tf_op jit(solution)/shard_map/ppermute | solution.py:47
  229.7 0.9 collective-permute-done.36.refs_7_
  231.3 2.1 shard_map.88
  233.4 14.7 %all_to_all.31.i = bf16[16,8,1024]{2,1,0:T(8,128)(2,1)} all-to-all(bf16[16,8,1024]{2,1,0:T(8,128)(2,1)} %shard_map.88), channel_id=1, replica_groups=mesh['y'=4,'x'=4,'core'=2,'z'=8] {'core','z'}, dimensions={0} | all-to-all | bytes 524288 | tf_op jit(solution)/shard_map/all_to_all | solution.py:484
  248.1 1.6 shard_map.89
  (107 shorter events, 7.3 us)
Async XLA Ops:
  1.6 67.2 %copy-start.3 = (bf16[256,512]{1,0:T(8,128)(2,1)}, bf16[256,512]{1,0:T(8,128)(2,1)S(1)}, u32[]{:S(2)}) copy-start(bf16[256,512]{1,0:T(8,128)(2,1)S(1)} %constant_dynamic-slice_fusion.2.refs_0_) | copy-start | bytes 786436
  1.6 10.5 %collective-permute-start.1 = (bf16[256,512]{1,0:T(8,128)(2,1)S(1)}, bf16[256,512]{1,0:T(8,128)(2,1)S(1)}, u32[]{:S(2)}, u32[]{:S(2)}) collective-permute-start(bf16[256,512]{1,0:T(8,128)(2,1)S(1)} %constant_dynamic-slice_fusion.2.refs_0_), channel_id=1, source_target_pairs={{0,1},{1,2},{2,3},{3,4},{4,5},{5,6},{6,7},{7,0},{8,9},{9,10},{10,1... | collective-permute-start | bytes 786440 | tf_op jit(solution)/shard_map/ppermute | solution.py:47
  1.9 60.7 %collective-permute-start = (bf16[256,2048]{1,0:T(8,128)(2,1)}, bf16[256,2048]{1,0:T(8,128)(2,1)S(1)}, u32[]{:S(2)}, u32[]{:S(2)}) collective-permute-start(bf16[256,2048]{1,0:T(8,128)(2,1)} %own.1), channel_id=1, source_target_pairs={{0,8},{8,0},{1,9},{9,1},{2,10},{10,2},{3,11},{11,3},{4,12},{12,4},... | collective-permute-start | bytes 3145736 | tf_op jit(solution)/shard_map/ppermute | solution.py:355
  1.9 17.8 %collective-permute-start.2 = (bf16[256,512]{1,0:T(8,128)(2,1)S(1)}, bf16[256,512]{1,0:T(8,128)(2,1)S(1)}, u32[]{:S(2)}, u32[]{:S(2)}) collective-permute-start(bf16[256,512]{1,0:T(8,128)(2,1)S(1)} %constant_dynamic-slice_fusion.2.refs_0_), channel_id=1, source_target_pairs={{0,7},{1,0},{2,1},{3,2},{4,3},{5,4},{6,5},{7,6},{8,15},{9,8},{10,9... | collective-permute-start | bytes 786440 | tf_op jit(solution)/shard_map/ppermute | solution.py:47
  12.2 56.7 %copy-start.15 = (bf16[256,512]{1,0:T(8,128)(2,1)}, bf16[256,512]{1,0:T(8,128)(2,1)S(1)}, u32[]{:S(2)}) copy-start(bf16[256,512]{1,0:T(8,128)(2,1)S(1)} %collective-permute-done.1.refs_1_) | copy-start | bytes 786436
  12.2 10.8 %collective-permute-start.3 = (bf16[256,512]{1,0:T(8,128)(2,1)S(1)}, bf16[256,512]{1,0:T(8,128)(2,1)S(1)}, u32[]{:S(2)}, u32[]{:S(2)}) collective-permute-start(bf16[256,512]{1,0:T(8,128)(2,1)S(1)} %collective-permute-done.1.refs_1_), channel_id=1, source_target_pairs={{0,1},{1,2},{2,3},{3,4},{4,5},{5,6},{6,7},{7,0},{8,9},{9,10},{10,1... | collective-permute-start | bytes 786440 | tf_op jit(solution)/shard_map/ppermute | solution.py:47
  13.5 15.9 %all-to-all-start = ((bf16[8,16,512]{2,1,0:T(8,128)(2,1)}), bf16[8,16,512]{2,1,0:T(8,128)(2,1)S(1)}, u32[]{:S(2)}, u32[]{:S(2)}) async-start(bf16[8,16,512]{2,1,0:T(8,128)(2,1)} %broadcast_in_dim.2), calls=%async_computation | async-start | bytes 262144 | tf_op jit(solution)/shard_map/all_to_all | solution.py:369
  19.7 49.1 %copy-start.16 = (bf16[256,512]{1,0:T(8,128)(2,1)}, bf16[256,512]{1,0:T(8,128)(2,1)S(1)}, u32[]{:S(2)}) copy-start(bf16[256,512]{1,0:T(8,128)(2,1)S(1)} %collective-permute-done.2.refs_2_) | copy-start | bytes 786436
  19.7 21.3 %collective-permute-start.4 = (bf16[256,512]{1,0:T(8,128)(2,1)S(1)}, bf16[256,512]{1,0:T(8,128)(2,1)S(1)}, u32[]{:S(2)}, u32[]{:S(2)}) collective-permute-start(bf16[256,512]{1,0:T(8,128)(2,1)S(1)} %collective-permute-done.2.refs_2_), channel_id=1, source_target_pairs={{0,7},{1,0},{2,1},{3,2},{4,3},{5,4},{6,5},{7,6},{8,15},{9,8},{10,9... | collective-permute-start | bytes 786440 | tf_op jit(solution)/shard_map/ppermute | solution.py:47
  23.0 45.8 %copy-start.17 = (bf16[256,512]{1,0:T(8,128)(2,1)}, bf16[256,512]{1,0:T(8,128)(2,1)S(1)}, u32[]{:S(2)}) copy-start(bf16[256,512]{1,0:T(8,128)(2,1)S(1)} %collective-permute-done.3.refs_3_) | copy-start | bytes 786436
  23.0 18.5 %collective-permute-start.5 = (bf16[256,512]{1,0:T(8,128)(2,1)S(1)}, bf16[256,512]{1,0:T(8,128)(2,1)S(1)}, u32[]{:S(2)}, u32[]{:S(2)}) collective-permute-start(bf16[256,512]{1,0:T(8,128)(2,1)S(1)} %collective-permute-done.3.refs_3_), channel_id=1, source_target_pairs={{0,1},{1,2},{2,3},{3,4},{4,5},{5,6},{6,7},{7,0},{8,9},{9,10},{10,1... | collective-permute-start | bytes 786440 | tf_op jit(solution)/shard_map/ppermute | solution.py:47
  29.5 5.6 %collective-permute-start.8 = (bf16[8,16,256]{2,1,0:T(8,128)(2,1)S(1)}, bf16[8,16,256]{2,1,0:T(8,128)(2,1)S(1)}, u32[]{:S(2)}, u32[]{:S(2)}) collective-permute-start(bf16[8,16,256]{2,1,0:T(8,128)(2,1)S(1)} %get-tuple-element.81), channel_id=1, source_target_pairs={{0,16},{16,32},{32,48},{48,0},{1,17},{17,33},{33,49},{49,1},{2,18}... | collective-permute-start | bytes 196616 | tf_op jit(solution)/shard_map/ppermute | solution.py:47
  31.1 5.8 %collective-permute-start.9 = (bf16[8,16,256]{2,1,0:T(8,128)(2,1)S(1)}, bf16[8,16,256]{2,1,0:T(8,128)(2,1)S(1)}, u32[]{:S(2)}, u32[]{:S(2)}) collective-permute-start(bf16[8,16,256]{2,1,0:T(8,128)(2,1)S(1)} %get-tuple-element.81), channel_id=1, source_target_pairs={{0,32},{16,48},{32,0},{48,16},{1,33},{17,49},{33,1},{49,17},{2,34}... | collective-permute-start | bytes 196616 | tf_op jit(solution)/shard_map/ppermute | solution.py:47
  35.1 4.3 %collective-permute-start.10 = (bf16[8,16,256]{2,1,0:T(8,128)(2,1)S(1)}, bf16[8,16,256]{2,1,0:T(8,128)(2,1)S(1)}, u32[]{:S(2)}, u32[]{:S(2)}) collective-permute-start(bf16[8,16,256]{2,1,0:T(8,128)(2,1)S(1)} %get-tuple-element.81), channel_id=1, source_target_pairs={{0,48},{16,0},{32,16},{48,32},{1,49},{17,1},{33,17},{49,33},{2,50}... | collective-permute-start | bytes 196616 | tf_op jit(solution)/shard_map/ppermute | solution.py:47
  36.8 6.2 %collective-permute-start.14 = (bf16[8,16,256]{2,1,0:T(8,128)(2,1)S(1)}, bf16[8,16,256]{2,1,0:T(8,128)(2,1)S(1)}, u32[]{:S(2)}, u32[]{:S(2)}) collective-permute-start(bf16[8,16,256]{2,1,0:T(8,128)(2,1)S(1)} %get-tuple-element.80), channel_id=1, source_target_pairs={{0,64},{64,128},{128,192},{192,0},{1,65},{65,129},{129,193},{193,1... | collective-permute-start | bytes 196616 | tf_op jit(solution)/shard_map/ppermute | solution.py:47
  39.4 34.9 %copy-start.4 = (bf16[4,8,16,256]{3,2,1,0:T(8,128)(2,1)}, bf16[4,8,16,256]{3,2,1,0:T(8,128)(2,1)S(1)}, u32[]{:S(2)}) copy-start(bf16[4,8,16,256]{3,2,1,0:T(8,128)(2,1)S(1)} %pad_maximum_fusion.refs_0_) | copy-start | bytes 786436
  39.4 17.4 %collective-permute-start.11 = (bf16[4,8,16,256]{3,2,1,0:T(8,128)(2,1)S(1)}, bf16[4,8,16,256]{3,2,1,0:T(8,128)(2,1)S(1)}, u32[]{:S(2)}, u32[]{:S(2)}) collective-permute-start(bf16[4,8,16,256]{3,2,1,0:T(8,128)(2,1)S(1)} %pad_maximum_fusion.refs_0_), channel_id=1, source_target_pairs={{0,64},{64,128},{128,192},{192,0},{1,65},{65,129},{129,193},{193,1... | collective-permute-start | bytes 786440 | tf_op jit(solution)/shard_map/ppermute | solution.py:47
  41.0 27.8 %copy-start.18 = (bf16[256,512]{1,0:T(8,128)(2,1)}, bf16[256,512]{1,0:T(8,128)(2,1)S(1)}, u32[]{:S(2)}) copy-start(bf16[256,512]{1,0:T(8,128)(2,1)S(1)} %collective-permute-done.4.refs_4_) | copy-start | bytes 786436
  41.0 17.3 %collective-permute-start.6 = (bf16[256,512]{1,0:T(8,128)(2,1)S(1)}, bf16[256,512]{1,0:T(8,128)(2,1)S(1)}, u32[]{:S(2)}, u32[]{:S(2)}) collective-permute-start(bf16[256,512]{1,0:T(8,128)(2,1)S(1)} %collective-permute-done.4.refs_4_), channel_id=1, source_target_pairs={{0,7},{1,0},{2,1},{3,2},{4,3},{5,4},{6,5},{7,6},{8,15},{9,8},{10,9... | collective-permute-start | bytes 786440 | tf_op jit(solution)/shard_map/ppermute | solution.py:47
  41.5 27.4 %copy-start.19 = (bf16[256,512]{1,0:T(8,128)(2,1)}, bf16[256,512]{1,0:T(8,128)(2,1)S(1)}, u32[]{:S(2)}) copy-start(bf16[256,512]{1,0:T(8,128)(2,1)S(1)} %collective-permute-done.5.refs_5_) | copy-start | bytes 786436
  41.5 17.2 %collective-permute-start.7 = (bf16[256,512]{1,0:T(8,128)(2,1)S(1)}, bf16[256,512]{1,0:T(8,128)(2,1)S(1)}, u32[]{:S(2)}, u32[]{:S(2)}) collective-permute-start(bf16[256,512]{1,0:T(8,128)(2,1)S(1)} %collective-permute-done.5.refs_5_), channel_id=1, source_target_pairs={{0,1},{1,2},{2,3},{3,4},{4,5},{5,6},{6,7},{7,0},{8,9},{9,10},{10,1... | collective-permute-start | bytes 786440 | tf_op jit(solution)/shard_map/ppermute | solution.py:47
  43.1 5.9 %collective-permute-start.15 = (bf16[8,16,256]{2,1,0:T(8,128)(2,1)S(1)}, bf16[8,16,256]{2,1,0:T(8,128)(2,1)S(1)}, u32[]{:S(2)}, u32[]{:S(2)}) collective-permute-start(bf16[8,16,256]{2,1,0:T(8,128)(2,1)S(1)} %get-tuple-element.80), channel_id=1, source_target_pairs={{0,128},{64,192},{128,0},{192,64},{1,129},{65,193},{129,1},{193,65... | collective-permute-start | bytes 196616 | tf_op jit(solution)/shard_map/ppermute | solution.py:47
  48.9 5.0 %collective-permute-start.16 = (bf16[8,16,256]{2,1,0:T(8,128)(2,1)S(1)}, bf16[8,16,256]{2,1,0:T(8,128)(2,1)S(1)}, u32[]{:S(2)}, u32[]{:S(2)}) collective-permute-start(bf16[8,16,256]{2,1,0:T(8,128)(2,1)S(1)} %get-tuple-element.80), channel_id=1, source_target_pairs={{0,192},{64,0},{128,64},{192,128},{1,193},{65,1},{129,65},{193,129... | collective-permute-start | bytes 196616 | tf_op jit(solution)/shard_map/ppermute | solution.py:47
  53.9 20.4 %collective-permute-start.12 = (bf16[4,8,16,256]{3,2,1,0:T(8,128)(2,1)S(1)}, bf16[4,8,16,256]{3,2,1,0:T(8,128)(2,1)}, u32[]{:S(2)}, u32[]{:S(2)}) collective-permute-start(bf16[4,8,16,256]{3,2,1,0:T(8,128)(2,1)S(1)} %pad_maximum_fusion.refs_0_), channel_id=1, source_target_pairs={{0,128},{64,192},{128,0},{192,64},{1,129},{65,193},{129,1},{193,65... | collective-permute-start | bytes 786440 | tf_op jit(solution)/shard_map/ppermute | solution.py:47
  56.7 17.6 %copy-start.5 = (bf16[4,8,16,256]{3,2,1,0:T(8,128)(2,1)}, bf16[4,8,16,256]{3,2,1,0:T(8,128)(2,1)S(1)}, u32[]{:S(2)}) copy-start(bf16[4,8,16,256]{3,2,1,0:T(8,128)(2,1)S(1)} %pad_maximum_fusion.1.refs_4_) | copy-start | bytes 786436
  56.7 17.6 %copy-start.20 = (bf16[4,8,16,256]{3,2,1,0:T(8,128)(2,1)}, bf16[4,8,16,256]{3,2,1,0:T(8,128)(2,1)S(1)}, u32[]{:S(2)}) copy-start(bf16[4,8,16,256]{3,2,1,0:T(8,128)(2,1)S(1)} %collective-permute-done.11.refs_1_) | copy-start | bytes 786436
  56.7 17.6 %collective-permute-start.13 = (bf16[4,8,16,256]{3,2,1,0:T(8,128)(2,1)S(1)}, bf16[4,8,16,256]{3,2,1,0:T(8,128)(2,1)}, u32[]{:S(2)}, u32[]{:S(2)}) collective-permute-start(bf16[4,8,16,256]{3,2,1,0:T(8,128)(2,1)S(1)} %pad_maximum_fusion.refs_0_), channel_id=1, source_target_pairs={{0,192},{64,0},{128,64},{192,128},{1,193},{65,1},{129,65},{193,129... | collective-permute-start | bytes 786440 | tf_op jit(solution)/shard_map/ppermute | solution.py:47
  58.4 4.2 %copy-start.21 = (bf16[256,512]{1,0:T(8,128)(2,1)}, bf16[256,512]{1,0:T(8,128)(2,1)S(1)}, u32[]{:S(2)}) copy-start(bf16[256,512]{1,0:T(8,128)(2,1)S(1)} %collective-permute-done.6.refs_6_) | copy-start | bytes 786436
  58.4 16.0 %collective-permute-start.17 = (bf16[4,8,16,256]{3,2,1,0:T(8,128)(2,1)S(1)}, bf16[4,8,16,256]{3,2,1,0:T(8,128)(2,1)}, u32[]{:S(2)}, u32[]{:S(2)}) collective-permute-start(bf16[4,8,16,256]{3,2,1,0:T(8,128)(2,1)S(1)} %pad_maximum_fusion.1.refs_4_), channel_id=1, source_target_pairs={{0,16},{16,32},{32,48},{48,0},{1,17},{17,33},{33,49},{49,1},{2,18}... | collective-permute-start | bytes 786440 | tf_op jit(solution)/shard_map/ppermute | solution.py:47
  58.7 3.9 %copy-start.22 = (bf16[256,512]{1,0:T(8,128)(2,1)}, bf16[256,512]{1,0:T(8,128)(2,1)S(1)}, u32[]{:S(2)}) copy-start(bf16[256,512]{1,0:T(8,128)(2,1)S(1)} %collective-permute-done.7.refs_7_) | copy-start | bytes 786436
  58.7 15.7 %collective-permute-start.18 = (bf16[4,8,16,256]{3,2,1,0:T(8,128)(2,1)S(1)}, bf16[4,8,16,256]{3,2,1,0:T(8,128)(2,1)}, u32[]{:S(2)}, u32[]{:S(2)}) collective-permute-start(bf16[4,8,16,256]{3,2,1,0:T(8,128)(2,1)S(1)} %pad_maximum_fusion.1.refs_4_), channel_id=1, source_target_pairs={{0,32},{16,48},{32,0},{48,16},{1,33},{17,49},{33,1},{49,17},{2,34}... | collective-permute-start | bytes 786440 | tf_op jit(solution)/shard_map/ppermute | solution.py:47
  62.6 11.7 %collective-permute-start.19 = (bf16[4,8,16,256]{3,2,1,0:T(8,128)(2,1)S(1)}, bf16[4,8,16,256]{3,2,1,0:T(8,128)(2,1)}, u32[]{:S(2)}, u32[]{:S(2)}) collective-permute-start(bf16[4,8,16,256]{3,2,1,0:T(8,128)(2,1)S(1)} %pad_maximum_fusion.1.refs_4_), channel_id=1, source_target_pairs={{0,48},{16,0},{32,16},{48,32},{1,49},{17,1},{33,17},{49,33},{2,50}... | collective-permute-start | bytes 786440 | tf_op jit(solution)/shard_map/ppermute | solution.py:47
  74.4 10.5 %copy-start.1 = (bf16[256,1024]{1,0:T(8,128)(2,1)S(1)}, bf16[256,1024]{1,0:T(8,128)(2,1)}, u32[]{:S(2)}) copy-start(bf16[256,1024]{1,0:T(8,128)(2,1)} %q_own.1) | copy-start | bytes 1572868
  81.4 13.8 %all-to-all-start.1 = ((bf16[8,128,128]{2,1,0:T(8,128)(2,1)}), bf16[8,128,128]{2,1,0:T(8,128)(2,1)S(1)}, u32[]{:S(2)}, u32[]{:S(2)}) async-start(bf16[8,128,128]{2,1,0:T(8,128)(2,1)} %get-tuple-element.48), calls=%async_computation.1 | async-start | bytes 524288 | tf_op jit(solution)/shard_map/all_to_all | solution.py:414
  84.9 16.8 %copy-start.2 = (bf16[256,1024]{1,0:T(8,128)(2,1)S(1)}, bf16[256,1024]{1,0:T(8,128)(2,1)}, u32[]{:S(2)}) copy-start(bf16[256,1024]{1,0:T(8,128)(2,1)} %g_own.1) | copy-start | bytes 1572868
  84.9 1.6 collective-permute-start.20
  97.6 16.2 %all-to-all-start.2 = ((bf16[8,128,128]{2,1,0:T(8,128)(2,1)}), bf16[8,128,128]{2,1,0:T(8,128)(2,1)S(1)}, u32[]{:S(2)}, u32[]{:S(2)}) async-start(bf16[8,128,128]{2,1,0:T(8,128)(2,1)} %shard_map.79), calls=%async_computation.2 | async-start | bytes 524288 | tf_op jit(solution)/shard_map/all_to_all | solution.py:418
  101.7 1.6 collective-permute-start.21
  103.3 10.5 %copy-start.23 = (bf16[256,512]{1,0:T(8,128)(2,1)}, bf16[256,512]{1,0:T(8,128)(2,1)S(1)}, u32[]{:S(2)}) copy-start(bf16[256,512]{1,0:T(8,128)(2,1)S(1)} %collective-permute-done.21.g_sib) | copy-start | bytes 786436
  119.1 14.4 %all-to-all-start.3 = ((bf16[8,128,128]{2,1,0:T(8,128)(2,1)}), bf16[8,128,128]{2,1,0:T(8,128)(2,1)S(1)}, u32[]{:S(2)}, u32[]{:S(2)}) async-start(bf16[8,128,128]{2,1,0:T(8,128)(2,1)} %get-tuple-element.52), calls=%async_computation.3 | async-start | bytes 524288 | tf_op jit(solution)/shard_map/all_to_all | solution.py:414
  122.5 44.2 %collective-permute-start.24 = (bf16[8,16,16,512]{3,2,1,0:T(8,128)(2,1)}, bf16[8,16,16,512]{3,2,1,0:T(8,128)(2,1)}, u32[]{:S(2)}, u32[]{:S(2)}) collective-permute-start(bf16[8,16,16,512]{3,2,1,0:T(8,128)(2,1)} %get-tuple-element.59.wv), channel_id=1, source_target_pairs={{0,8},{8,0},{1,9},{9,1},{2,10},{10,2},{3,11},{11,3},{4,12},{12,4},... | collective-permute-start | bytes 6291464 | tf_op jit(solution)/shard_map/ppermute | solution.py:355
  122.6 46.3 %collective-permute-start.23 = (bf16[8,256,512]{2,1,0:T(8,128)(2,1)}, bf16[8,256,512]{2,1,0:T(8,128)(2,1)}, u32[]{:S(2)}, u32[]{:S(2)}) collective-permute-start(bf16[8,256,512]{2,1,0:T(8,128)(2,1)} %get-tuple-element.58.wk), channel_id=1, source_target_pairs={{0,8},{8,0},{1,9},{9,1},{2,10},{10,2},{3,11},{11,3},{4,12},{12,4},... | collective-permute-start | bytes 6291464 | tf_op jit(solution)/shard_map/ppermute | solution.py:355
  158.3 3.8 %copy-start.11 = (bf16[4,128,512]{2,1,0:T(8,128)(2,1)S(1)}, bf16[4,128,512]{2,1,0:T(8,128)(2,1)}, u32[]{:S(2)}) copy-start(bf16[4,128,512]{2,1,0:T(8,128)(2,1)} %get-tuple-element.57._) | copy-start | bytes 1572868
  160.9 28.4 %collective-permute-start.22 = (bf16[256,2048]{1,0:T(8,128)(2,1)}, bf16[256,2048]{1,0:T(8,128)(2,1)}, u32[]{:S(2)}, u32[]{:S(2)}) collective-permute-start(bf16[256,2048]{1,0:T(8,128)(2,1)} %shard_map.84._), channel_id=1, source_target_pairs={{0,8},{8,0},{1,9},{9,1},{2,10},{10,2},{3,11},{11,3},{4,12},{12,4},... | collective-permute-start | bytes 3145736 | tf_op jit(solution)/shard_map/ppermute | solution.py:355
  160.9 26.8 %collective-permute-start.25 = (bf16[4,128,512]{2,1,0:T(8,128)(2,1)S(1)}, bf16[4,128,512]{2,1,0:T(8,128)(2,1)S(1)}, u32[]{:S(2)}, u32[]{:S(2)}) collective-permute-start(bf16[4,128,512]{2,1,0:T(8,128)(2,1)S(1)} %copy-done.31), channel_id=1, source_target_pairs={{0,16},{16,32},{32,48},{48,0},{1,17},{17,33},{33,49},{49,1},{2,18}... | collective-permute-start | bytes 1572872 | tf_op jit(solution)/shard_map/ppermute | solution.py:47
  162.1 38.8 %collective-permute-start.26 = (bf16[4,128,512]{2,1,0:T(8,128)(2,1)S(1)}, bf16[4,128,512]{2,1,0:T(8,128)(2,1)S(1)}, u32[]{:S(2)}, u32[]{:S(2)}) collective-permute-start(bf16[4,128,512]{2,1,0:T(8,128)(2,1)S(1)} %copy-done.11), channel_id=1, source_target_pairs={{0,32},{16,48},{32,0},{48,16},{1,33},{17,49},{33,1},{49,17},{2,34}... | collective-permute-start | bytes 1572872 | tf_op jit(solution)/shard_map/ppermute | solution.py:47
  166.8 34.2 %collective-permute-start.27 = (bf16[4,128,512]{2,1,0:T(8,128)(2,1)}, bf16[4,128,512]{2,1,0:T(8,128)(2,1)S(1)}, u32[]{:S(2)}, u32[]{:S(2)}) collective-permute-start(bf16[4,128,512]{2,1,0:T(8,128)(2,1)} %get-tuple-element.65), channel_id=1, source_target_pairs={{0,48},{16,0},{32,16},{48,32},{1,49},{17,1},{33,17},{49,33},{2,50}... | collective-permute-start | bytes 1572872 | tf_op jit(solution)/shard_map/ppermute | solution.py:47
  168.9 32.0 %collective-permute-start.28 = (bf16[4,128,512]{2,1,0:T(8,128)(2,1)}, bf16[4,128,512]{2,1,0:T(8,128)(2,1)S(1)}, u32[]{:S(2)}, u32[]{:S(2)}) collective-permute-start(bf16[4,128,512]{2,1,0:T(8,128)(2,1)} %get-tuple-element.67), channel_id=1, source_target_pairs={{0,64},{64,128},{128,192},{192,0},{1,65},{65,129},{129,193},{193,1... | collective-permute-start | bytes 1572872 | tf_op jit(solution)/shard_map/ppermute | solution.py:47
  187.7 13.2 %copy-start.9 = (bf16[4,128,512]{2,1,0:T(8,128)(2,1)}, bf16[4,128,512]{2,1,0:T(8,128)(2,1)S(1)}, u32[]{:S(2)}) copy-start(bf16[4,128,512]{2,1,0:T(8,128)(2,1)S(1)} %collective-permute-done.25.refs_1_) | copy-start | bytes 1572868
  187.7 15.2 %collective-permute-start.29 = (bf16[4,128,512]{2,1,0:T(8,128)(2,1)}, bf16[4,128,512]{2,1,0:T(8,128)(2,1)S(1)}, u32[]{:S(2)}, u32[]{:S(2)}) collective-permute-start(bf16[4,128,512]{2,1,0:T(8,128)(2,1)} %get-tuple-element.68), channel_id=1, source_target_pairs={{0,128},{64,192},{128,0},{192,64},{1,129},{65,193},{129,1},{193,65... | collective-permute-start | bytes 1572872 | tf_op jit(solution)/shard_map/ppermute | solution.py:47
  189.3 22.4 %collective-permute-start.30 = (bf16[4,128,512]{2,1,0:T(8,128)(2,1)}, bf16[4,128,512]{2,1,0:T(8,128)(2,1)}, u32[]{:S(2)}, u32[]{:S(2)}) collective-permute-start(bf16[4,128,512]{2,1,0:T(8,128)(2,1)} %get-tuple-element.69), channel_id=1, source_target_pairs={{0,192},{64,0},{128,64},{192,128},{1,193},{65,1},{129,65},{193,129... | collective-permute-start | bytes 1572872 | tf_op jit(solution)/shard_map/ppermute | solution.py:47
  200.9 10.8 %copy-start.10 = (bf16[4,128,512]{2,1,0:T(8,128)(2,1)}, bf16[4,128,512]{2,1,0:T(8,128)(2,1)S(1)}, u32[]{:S(2)}) copy-start(bf16[4,128,512]{2,1,0:T(8,128)(2,1)S(1)} %collective-permute-done.26.refs_2_) | copy-start | bytes 1572868
  200.9 10.8 %copy-start.12 = (bf16[4,128,512]{2,1,0:T(8,128)(2,1)}, bf16[4,128,512]{2,1,0:T(8,128)(2,1)S(1)}, u32[]{:S(2)}) copy-start(bf16[4,128,512]{2,1,0:T(8,128)(2,1)S(1)} %collective-permute-done.27.refs_3_) | copy-start | bytes 1572868
  200.9 10.8 %copy-start.13 = (bf16[4,128,512]{2,1,0:T(8,128)(2,1)}, bf16[4,128,512]{2,1,0:T(8,128)(2,1)S(1)}, u32[]{:S(2)}) copy-start(bf16[4,128,512]{2,1,0:T(8,128)(2,1)S(1)} %collective-permute-done.28.refs_5_) | copy-start | bytes 1572868
  202.9 8.8 %copy-start.14 = (bf16[4,128,512]{2,1,0:T(8,128)(2,1)}, bf16[4,128,512]{2,1,0:T(8,128)(2,1)S(1)}, u32[]{:S(2)}) copy-start(bf16[4,128,512]{2,1,0:T(8,128)(2,1)S(1)} %collective-permute-done.29.refs_6_) | copy-start | bytes 1572868
  215.4 7.4 %collective-permute-start.31 = (bf16[128,512]{1,0:T(8,128)(2,1)}, bf16[128,512]{1,0:T(8,128)(2,1)S(1)}, u32[]{:S(2)}, u32[]{:S(2)}) collective-permute-start(bf16[128,512]{1,0:T(8,128)(2,1)} %get-tuple-element.71), channel_id=1, source_target_pairs={{0,64},{64,128},{128,192},{192,0},{1,65},{65,129},{129,193},{193,1... | collective-permute-start | bytes 393224 | tf_op jit(solution)/shard_map/ppermute | solution.py:47
  218.0 8.0 %collective-permute-start.32 = (bf16[128,512]{1,0:T(8,128)(2,1)}, bf16[128,512]{1,0:T(8,128)(2,1)S(1)}, u32[]{:S(2)}, u32[]{:S(2)}) collective-permute-start(bf16[128,512]{1,0:T(8,128)(2,1)} %get-tuple-element.72), channel_id=1, source_target_pairs={{0,128},{64,192},{128,0},{192,64},{1,129},{65,193},{129,1},{193,65... | collective-permute-start | bytes 393224 | tf_op jit(solution)/shard_map/ppermute | solution.py:47
  219.6 6.4 %collective-permute-start.33 = (bf16[128,512]{1,0:T(8,128)(2,1)}, bf16[128,512]{1,0:T(8,128)(2,1)S(1)}, u32[]{:S(2)}, u32[]{:S(2)}) collective-permute-start(bf16[128,512]{1,0:T(8,128)(2,1)} %get-tuple-element.73), channel_id=1, source_target_pairs={{0,192},{64,0},{128,64},{192,128},{1,193},{65,1},{129,65},{193,129... | collective-permute-start | bytes 393224 | tf_op jit(solution)/shard_map/ppermute | solution.py:47
  221.9 7.8 %collective-permute-start.34 = (bf16[128,512]{1,0:T(8,128)(2,1)}, bf16[128,512]{1,0:T(8,128)(2,1)S(1)}, u32[]{:S(2)}, u32[]{:S(2)}) collective-permute-start(bf16[128,512]{1,0:T(8,128)(2,1)} %get-tuple-element.75), channel_id=1, source_target_pairs={{0,16},{16,32},{32,48},{48,0},{1,17},{17,33},{33,49},{49,1},{2,18}... | collective-permute-start | bytes 393224 | tf_op jit(solution)/shard_map/ppermute | solution.py:47
  221.9 7.8 %collective-permute-start.35 = (bf16[128,512]{1,0:T(8,128)(2,1)}, bf16[128,512]{1,0:T(8,128)(2,1)S(1)}, u32[]{:S(2)}, u32[]{:S(2)}) collective-permute-start(bf16[128,512]{1,0:T(8,128)(2,1)} %get-tuple-element.76), channel_id=1, source_target_pairs={{0,32},{16,48},{32,0},{48,16},{1,33},{17,49},{33,1},{49,17},{2,34}... | collective-permute-start | bytes 393224 | tf_op jit(solution)/shard_map/ppermute | solution.py:47
  222.8 7.8 %copy-start.25 = (bf16[128,512]{1,0:T(8,128)(2,1)}, bf16[128,512]{1,0:T(8,128)(2,1)S(1)}, u32[]{:S(2)}) copy-start(bf16[128,512]{1,0:T(8,128)(2,1)S(1)} %collective-permute-done.31.refs_1_) | copy-start | bytes 393220
  222.8 7.8 %collective-permute-start.36 = (bf16[128,512]{1,0:T(8,128)(2,1)}, bf16[128,512]{1,0:T(8,128)(2,1)S(1)}, u32[]{:S(2)}, u32[]{:S(2)}) collective-permute-start(bf16[128,512]{1,0:T(8,128)(2,1)} %get-tuple-element.77), channel_id=1, source_target_pairs={{0,48},{16,0},{32,16},{48,32},{1,49},{17,1},{33,17},{49,33},{2,50}... | collective-permute-start | bytes 393224 | tf_op jit(solution)/shard_map/ppermute | solution.py:47
  226.0 4.7 %copy-start.26 = (bf16[128,512]{1,0:T(8,128)(2,1)}, bf16[128,512]{1,0:T(8,128)(2,1)S(1)}, u32[]{:S(2)}) copy-start(bf16[128,512]{1,0:T(8,128)(2,1)S(1)} %collective-permute-done.32.refs_2_) | copy-start | bytes 393220
  226.0 4.7 %copy-start.27 = (bf16[128,512]{1,0:T(8,128)(2,1)}, bf16[128,512]{1,0:T(8,128)(2,1)S(1)}, u32[]{:S(2)}) copy-start(bf16[128,512]{1,0:T(8,128)(2,1)S(1)} %collective-permute-done.33.refs_3_) | copy-start | bytes 393220
  (9 other events, 9.0 us)

commit v3 on v2

--- a/solution.py
+++ b/solution.py
@@ -360,7 +360,8 @@
     shard = lax.dynamic_slice_in_dim(kv_weight, core * 512, 512, 1)
     shards, left, right = [shard], shard, shard
     for _ in range(3):
-        left, right = shift(left, "z", 1), shift(right, "z", -1)
+        left = shift(left, "z", 1)
+        right = shift(right, "z", -1)
         shards += [left, right]
     shards.append(shift(left, "z", 1))
     place = lax.axis_index(("y", "x"))
@@ -368,7 +369,11 @@
     mine = jnp.broadcast_to(mine[None], (8, 16, 512))
     along_z = lax.all_to_all(mine, "z", 0, 0, tiled=True)
     a0, b0 = along_z[:, :, :256], along_z[:, :, 256:]
-    (a2, b2), (a1, b1), (a3, b3) = [(shift(a0, "x", d), shift(b0, "y", d)) for d in (2, 1, 3)]
+    got_a, got_b = {}, {}
+    for d in STEPS:
+        got_a[d] = shift(a0, "x", d)
+        got_b[d] = shift(b0, "y", d)
+    (a1, a2, a3), (b1, b2, b3) = ([got[d] for d in (1, 2, 3)] for got in (got_a, got_b))
     a = jnp.stack([a0, a1, a2, a3])
     b = jnp.stack([b0, b1, b2, b3])
     (p2, r2), (p1, r1), (p3, r3) = [(shift(a, "y", e), shift(b, "x", e)) for e in (2, 1, 3)]
@@ -456,7 +461,9 @@
     for d, to_x, to_y in ((2, a2, b2), (1, a1, b1), (3, a3, b3)):
         wa[d] = shift(to_x, "x", d)
         wb[d] = shift(to_y, "y", d)
-    (back,) = call(pack_kernel, [((rows, 2048), BF)], dkv, dq, out, a2, in_specs=[VMEM] * 3 + [ANY])
+    (back,) = call(
+        pack_kernel, [((rows, 2048), BF)], dkv, dq, out, a2, in_specs=[VMEM] * 3 + [ANY]
+    )
     a0, b0 = call(
         own_kernel, [sent] * 2, turned, dkv, back, in_specs=[VMEM] * 2 + [ANY],
         flops=2 * 512 * 512 * 1024,

time: 253 us -> 253 us (level)
  no operation moved by 1% of the time
where the time goes in v3:
time: 253 us; the launch traced here: 250 us
  waiting for transfers between devices  76.4 us (30%)
  Pallas kernels  68 us (27%)
  starting transfers between devices  67.7 us (27%)
  blocking collectives  29.9 us (12%)
  local copies, waits for them, and re-layouts  6.64 us (3%)
    pallas_call x14, Pallas kernels, call(): pl.pallas_call(body, out_shape=[jax.ShapeDtypeStruct(s, d) for s, d in ou...  58.2 us
    ppermute x31, starting transfers between devices, shift(): return lax.ppermute(x, axis, [(i, (i + step) % size) for i in range(size)])  50 us
    ppermute x31, waiting for transfers between devices, shift(): return lax.ppermute(x, axis, [(i, (i + step) % size) for i in range(size)])  49.3 us
    all_to_all x1, blocking collectives, exchange(): return lax.all_to_all(x, 'z', 0, 0, tiled=True)  15.2 us
    all_to_all x1, blocking collectives, on_device(): column = lax.all_to_all(column, ('core', 'z'), 0, 0, tiled=True)  14.7 us
    all_to_all x1, waiting for transfers between devices, exchange(): return lax.all_to_all(x, 'z', 0, 0, tiled=True)  10.5 us
    pallas_call x1, Pallas kernels, token_call(): pl.pallas_call(token_kernel, grid=(8,), out_shape=[jax.ShapeDtypeStruct((...  9.79 us
    all_to_all x2, waiting for transfers between devices, exchange(): x = lax.all_to_all(x, 'z', 0, 0, tiled=True)  7.07 us
  transfers between devices with their start and end apart: 41, of which 18 were waited for; matrix products, arithmetic and copies ran while one was open for 1% of the time, Pallas kernels for 19%

profile of v3, /device:TPU:0, one launch (start us, length us, event | category | flops | bytes accessed | tf_op | source)
XLA Modules:
  0.0 249.7 jit_solution(9707331008549740841)
XLA Ops:
  0.6 1.0 constant_dynamic-slice_fusion.2.refs_0_
  1.9 4.1 %collective-permute-start.2 = (bf16[256,512]{1,0:T(8,128)(2,1)S(1)}, bf16[256,512]{1,0:T(8,128)(2,1)S(1)}, u32[]{:S(2)}, u32[]{:S(2)}) collective-permute-start(bf16[256,512]{1,0:T(8,128)(2,1)S(1)} %constant_dynamic-slice_fusion.2.refs_0_), channel_id=1, source_target_pairs={{0,7},{1,0},{2,1},{3,2},{4,3},{5,4},{6,5},{7,6},{8,15},{9,8},{10,9... | collective-permute-start | bytes 786440 | tf_op jit(solution)/shard_map/ppermute | solution.py:47
  6.0 6.1 %collective-permute-done.1.refs_1_ = bf16[256,512]{1,0:T(8,128)(2,1)S(1)} collective-permute-done((bf16[256,512]{1,0:T(8,128)(2,1)S(1)}, bf16[256,512]{1,0:T(8,128)(2,1)S(1)}, u32[]{:S(2)}, u32[]{:S(2)}) %collective-permute-start.1) | collective-permute-done | bytes 262176 | tf_op jit(solution)/shard_map/ppermute | solution.py:47
  12.2 0.7 dynamic_slice.13
  13.5 6.1 %all-to-all-start = ((bf16[8,16,512]{2,1,0:T(8,128)(2,1)}), bf16[8,16,512]{2,1,0:T(8,128)(2,1)S(1)}, u32[]{:S(2)}, u32[]{:S(2)}) async-start(bf16[8,16,512]{2,1,0:T(8,128)(2,1)} %broadcast_in_dim.2), calls=%async_computation | async-start | bytes 262144 | tf_op jit(solution)/shard_map/all_to_all | solution.py:370
  19.7 3.3 %collective-permute-start.4 = (bf16[256,512]{1,0:T(8,128)(2,1)S(1)}, bf16[256,512]{1,0:T(8,128)(2,1)S(1)}, u32[]{:S(2)}, u32[]{:S(2)}) collective-permute-start(bf16[256,512]{1,0:T(8,128)(2,1)S(1)} %collective-permute-done.2.refs_2_), channel_id=1, source_target_pairs={{0,7},{1,0},{2,1},{3,2},{4,3},{5,4},{6,5},{7,6},{8,15},{9,8},{10,9... | collective-permute-start | bytes 786440 | tf_op jit(solution)/shard_map/ppermute | solution.py:47
  23.0 6.5 %all-to-all-done = bf16[8,16,512]{2,1,0:T(8,128)(2,1)S(1)} async-done(((bf16[8,16,512]{2,1,0:T(8,128)(2,1)}), bf16[8,16,512]{2,1,0:T(8,128)(2,1)S(1)}, u32[]{:S(2)}, u32[]{:S(2)}) %all-to-all-start) | async-done | bytes 131104 | tf_op jit(solution)/shard_map/all_to_all | solution.py:370
  29.5 1.6 collective-permute-start.8
  31.1 2.7 %collective-permute-start.9 = (bf16[8,16,256]{2,1,0:T(8,128)(2,1)S(1)}, bf16[8,16,256]{2,1,0:T(8,128)(2,1)S(1)}, u32[]{:S(2)}, u32[]{:S(2)}) collective-permute-start(bf16[8,16,256]{2,1,0:T(8,128)(2,1)S(1)} %get-tuple-element.81), channel_id=1, source_target_pairs={{0,32},{16,48},{32,0},{48,16},{1,33},{17,49},{33,1},{49,17},{2,34}... | collective-permute-start | bytes 196616 | tf_op jit(solution)/shard_map/ppermute | solution.py:47
  33.8 1.3 collective-permute-done.8
  35.1 1.5 collective-permute-start.10
  36.8 1.6 collective-permute-start.14
  38.4 0.9 collective-permute-done.10
  39.4 1.7 collective-permute-start.11
  41.5 1.6 collective-permute-start.7
  43.1 2.9 %collective-permute-start.15 = (bf16[8,16,256]{2,1,0:T(8,128)(2,1)S(1)}, bf16[8,16,256]{2,1,0:T(8,128)(2,1)S(1)}, u32[]{:S(2)}, u32[]{:S(2)}) collective-permute-start(bf16[8,16,256]{2,1,0:T(8,128)(2,1)S(1)} %get-tuple-element.80), channel_id=1, source_target_pairs={{0,128},{64,192},{128,0},{192,64},{1,129},{65,193},{129,1},{193,65... | collective-permute-start | bytes 196616 | tf_op jit(solution)/shard_map/ppermute | solution.py:47
  45.9 3.0 %collective-permute-done.15 = bf16[8,16,256]{2,1,0:T(8,128)(2,1)S(1)} collective-permute-done((bf16[8,16,256]{2,1,0:T(8,128)(2,1)S(1)}, bf16[8,16,256]{2,1,0:T(8,128)(2,1)S(1)}, u32[]{:S(2)}, u32[]{:S(2)}) %collective-permute-start.15) | collective-permute-done | bytes 65568 | tf_op jit(solution)/shard_map/ppermute | solution.py:47
  48.9 1.6 collective-permute-start.16
  50.5 3.4 %collective-permute-done.16 = bf16[8,16,256]{2,1,0:T(8,128)(2,1)S(1)} collective-permute-done((bf16[8,16,256]{2,1,0:T(8,128)(2,1)S(1)}, bf16[8,16,256]{2,1,0:T(8,128)(2,1)S(1)}, u32[]{:S(2)}, u32[]{:S(2)}) %collective-permute-start.16) | collective-permute-done | bytes 65568 | tf_op jit(solution)/shard_map/ppermute | solution.py:47
  53.9 2.8 %collective-permute-start.12 = (bf16[4,8,16,256]{3,2,1,0:T(8,128)(2,1)S(1)}, bf16[4,8,16,256]{3,2,1,0:T(8,128)(2,1)}, u32[]{:S(2)}, u32[]{:S(2)}) collective-permute-start(bf16[4,8,16,256]{3,2,1,0:T(8,128)(2,1)S(1)} %pad_maximum_fusion.refs_0_), channel_id=1, source_target_pairs={{0,128},{64,192},{128,0},{192,64},{1,129},{65,193},{129,1},{193,65... | collective-permute-start | bytes 786440 | tf_op jit(solution)/shard_map/ppermute | solution.py:47
  56.7 1.6 collective-permute-start.13
  58.7 3.9 %collective-permute-start.18 = (bf16[4,8,16,256]{3,2,1,0:T(8,128)(2,1)S(1)}, bf16[4,8,16,256]{3,2,1,0:T(8,128)(2,1)}, u32[]{:S(2)}, u32[]{:S(2)}) collective-permute-start(bf16[4,8,16,256]{3,2,1,0:T(8,128)(2,1)S(1)} %pad_maximum_fusion.1.refs_4_), channel_id=1, source_target_pairs={{0,32},{16,48},{32,0},{48,16},{1,33},{17,49},{33,1},{49,17},{2,34}... | collective-permute-start | bytes 786440 | tf_op jit(solution)/shard_map/ppermute | solution.py:47
  63.6 5.2 %shard_map.75 = (bf16[512,2048]{1,0:T(8,128)(2,1)}, bf16[16,128,512]{2,1,0:T(8,128)(2,1)}) custom-call(bf16[256,2048]{1,0:T(8,128)(2,1)} %own.1, bf16[256,2048]{1,0:T(8,128)(2,1)} %copy-done.6), custom_call_target="tpu_custom_call" | custom-call | bytes 6291456 | tf_op jit(solution)/shard_map/pallas_call | solution.py:35
  68.9 5.4 %shard_map.76 = (bf16[8,256,512]{2,1,0:T(8,128)(2,1)}, bf16[512,512]{1,0:T(8,128)(2,1)}) custom-call(bf16[512,2048]{1,0:T(8,128)(2,1)} %get-tuple-element.41.tok, bf16[256,512]{1,0:T(8,128)(2,1)} %copy-done.3, bf16[256,512]{1,0:T(8,128)(2,1)} %copy-done.15, bf16[256,512]{1,0:T(8,128)(2,1)} %copy-done.16, bf16[256,512]{1,0:T(8,128)(2,1)} %copy-done.17, ...), custom_call_target="tpu_custom_call" | custom-call | flops 1073741824 | bytes 6815744 | tf_op jit(solution)/shard_map/pallas_call | solution.py:35
  74.4 7.0 %shard_map.77 = (bf16[8,16,16,512]{3,2,1,0:T(8,128)(2,1)}, bf16[512,512]{1,0:T(8,128)(2,1)}, bf16[8,128,128]{2,1,0:T(8,128)(2,1)}) custom-call(bf16[512,2048]{1,0:T(8,128)(2,1)} %get-tuple-element.41.tok, bf16[512,512]{1,0:T(8,128)(2,1)} %get-tuple-element.42.key, bf16[4,8,16,256]{3,2,1,0:T(8,128)(2,1)} %copy-done.4, bf16[4,8,16,256]{3,2,1,0:T(8,128)(2,1)} %copy-done.20, ...), custom_call_target="tpu_custom_call" | custom-call | flops 1073741824 | bytes 7602176 | tf_op jit(solution)/shard_map/pallas_call | solution.py:35
  81.4 3.4 %all-to-all-start.1 = ((bf16[8,128,128]{2,1,0:T(8,128)(2,1)}), bf16[8,128,128]{2,1,0:T(8,128)(2,1)S(1)}, u32[]{:S(2)}, u32[]{:S(2)}) async-start(bf16[8,128,128]{2,1,0:T(8,128)(2,1)} %get-tuple-element.48), calls=%async_computation.1 | async-start | bytes 524288 | tf_op jit(solution)/shard_map/all_to_all | solution.py:419
  85.0 1.5 collective-permute-done.20.q_sib
  86.5 0.7 copy-done.24
  87.2 4.9 %shard_map.78 = (bf16[512,512]{1,0:T(8,128)(2,1)}, bf16[512,512]{1,0:T(8,128)(2,1)}, bf16[8,256,256]{2,1,0:T(8,128)(2,1)}, f32[512,512]{1,0:T(8,128)}) custom-call(bf16[256,1024]{1,0:T(8,128)(2,1)} %q_own.1, bf16[256,512]{1,0:T(8,128)(2,1)} %copy-done.24, bf16[512,512]{1,0:T(8,128)(2,1)} %get-tuple-element.42.key, bf16[512,512]{1,0:T(8,128)(2,1)} %get-tuple-element.43.val), custom_call_target="tpu_custom_call" | custom-call | flops 268435456 | bytes 4980736 | tf_op jit(solution)/shard_map/pallas_call | solution.py:35
  92.1 3.1 %all-to-all-done.1.i = bf16[8,128,128]{2,1,0:T(8,128)(2,1)S(1)} async-done(((bf16[8,128,128]{2,1,0:T(8,128)(2,1)}), bf16[8,128,128]{2,1,0:T(8,128)(2,1)S(1)}, u32[]{:S(2)}, u32[]{:S(2)}) %all-to-all-start.1) | async-done | bytes 262176 | tf_op jit(solution)/shard_map/all_to_all | solution.py:419
  95.2 0.7 copy-done.7
  95.9 1.7 shard_map.79
  97.6 4.0 %all-to-all-start.2 = ((bf16[8,128,128]{2,1,0:T(8,128)(2,1)}), bf16[8,128,128]{2,1,0:T(8,128)(2,1)S(1)}, u32[]{:S(2)}, u32[]{:S(2)}) async-start(bf16[8,128,128]{2,1,0:T(8,128)(2,1)} %shard_map.79), calls=%async_computation.2 | async-start | bytes 524288 | tf_op jit(solution)/shard_map/all_to_all | solution.py:423
  101.8 1.5 collective-permute-done.21.g_sib
  103.3 10.5 %all-to-all-done.2.before = bf16[8,128,128]{2,1,0:T(8,128)(2,1)S(1)} async-done(((bf16[8,128,128]{2,1,0:T(8,128)(2,1)}), bf16[8,128,128]{2,1,0:T(8,128)(2,1)S(1)}, u32[]{:S(2)}, u32[]{:S(2)}) %all-to-all-start.2) | async-done | bytes 262176 | tf_op jit(solution)/shard_map/all_to_all | solution.py:423
  113.8 0.7 copy-done
  114.5 4.6 %shard_map.80 = (bf16[512,512]{1,0:T(8,128)(2,1)}, bf16[512,512]{1,0:T(8,128)(2,1)}, bf16[8,128,128]{2,1,0:T(8,128)(2,1)}) custom-call(bf16[512,512]{1,0:T(8,128)(2,1)} %get-tuple-element.45.qf, bf16[256,1024]{1,0:T(8,128)(2,1)} %g_own.1, bf16[256,512]{1,0:T(8,128)(2,1)} %copy-done.23, f32[512,512]{1,0:T(8,128)} %get-tuple-element.47._.local, ...), custom_call_target="tpu_custom_call" | custom-call | flops 134217728 | bytes 3932160 | tf_op jit(solution)/shard_map/pallas_call | solution.py:35
  119.1 3.4 %all-to-all-start.3 = ((bf16[8,128,128]{2,1,0:T(8,128)(2,1)}), bf16[8,128,128]{2,1,0:T(8,128)(2,1)S(1)}, u32[]{:S(2)}, u32[]{:S(2)}) async-start(bf16[8,128,128]{2,1,0:T(8,128)(2,1)} %get-tuple-element.52), calls=%async_computation.3 | async-start | bytes 524288 | tf_op jit(solution)/shard_map/all_to_all | solution.py:419
  123.1 6.4 %shard_map.81 = (bf16[512,512]{1,0:T(8,128)(2,1)}, f32[512,512]{1,0:T(8,128)}, f32[512,512]{1,0:T(8,128)}) custom-call(bf16[512,512]{1,0:T(8,128)(2,1)} %get-tuple-element.44.qu, bf16[512,512]{1,0:T(8,128)(2,1)} %get-tuple-element.45.qf, bf16[512,512]{1,0:T(8,128)(2,1)} %get-tuple-element.42.key, bf16[512,512]{1,0:T(8,128)(2,1)} %get-tuple-element.43.val, ...), custom_call_target="tpu_custom_call" | custom-call | flops 671088640 | bytes 6553600 | tf_op jit(solution)/shard_map/pallas_call | solution.py:35
  129.6 4.0 %all-to-all-done.3.i = bf16[8,128,128]{2,1,0:T(8,128)(2,1)S(1)} async-done(((bf16[8,128,128]{2,1,0:T(8,128)(2,1)}), bf16[8,128,128]{2,1,0:T(8,128)(2,1)S(1)}, u32[]{:S(2)}, u32[]{:S(2)}) %all-to-all-start.3) | async-done | bytes 262176 | tf_op jit(solution)/shard_map/all_to_all | solution.py:419
  134.3 1.7 shard_map.82
  135.9 15.2 %all_to_all.30.after = bf16[8,128,128]{2,1,0:T(8,128)(2,1)} all-to-all(bf16[8,128,128]{2,1,0:T(8,128)(2,1)} %shard_map.82), channel_id=1, replica_groups=mesh['y'=4,'x'=4,'core'=2,'z'=8] {'z'}, dimensions={0} | all-to-all | bytes 524288 | tf_op jit(solution)/shard_map/all_to_all | solution.py:423
  151.1 7.1 %shard_map.83 = (bf16[512,1024]{1,0:T(8,128)(2,1)}, bf16[4,128,512]{2,1,0:T(8,128)(2,1)}, bf16[4,128,512]{2,1,0:T(8,128)(2,1)}, bf16[4,128,512]{2,1,0:T(8,128)(2...) custom-call(bf16[512,512]{1,0:T(8,128)(2,1)} %get-tuple-element.42.key, ...), custom_call_target="tpu_custom_call" | custom-call | flops 2147483648 | bytes 9699328 | tf_op jit(solution)/shard_map/pallas_call | solution.py:35
  158.3 2.6 %shard_map.84._ = bf16[256,2048]{1,0:T(8,128)(2,1)} custom-call(bf16[512,1024]{1,0:T(8,128)(2,1)} %get-tuple-element.54.dkv, bf16[512,512]{1,0:T(8,128)(2,1)} %get-tuple-element.55.dq, bf16[512,512]{1,0:T(8,128)(2,1)} %get-tuple-element.56.out.o, bf16[4,128,512]{2,1,0:T(8,128)(2,1)} %get-tuple-element.57._), custom_call_target="tpu_custom_call" | custom-call | bytes 3670016 | tf_op jit(solution)/shard_map/pallas_call | solution.py:35
  160.9 1.1 collective-permute-start.25
  162.7 4.0 %shard_map.86 = (bf16[4,128,512]{2,1,0:T(8,128)(2,1)}, bf16[4,128,512]{2,1,0:T(8,128)(2,1)}) custom-call(bf16[16,128,512]{2,1,0:T(8,128)(2,1)} %get-tuple-element.53.turned_hbm.turned, bf16[512,1024]{1,0:T(8,128)(2,1)} %get-tuple-element.54.dkv, bf16[256,2048]{1,0:T(8,128)(2,1)} %shard_map.84._), custom_call_target="tpu_custom_call" | custom-call | flops 536870912 | bytes 5242880 | tf_op jit(solution)/shard_map/pallas_call | solution.py:35
  166.8 2.2 collective-permute-start.27
  169.6 18.1 %collective-permute-done.25.refs_1_ = bf16[4,128,512]{2,1,0:T(8,128)(2,1)S(1)} collective-permute-done((bf16[4,128,512]{2,1,0:T(8,128)(2,1)S(1)}, bf16[4,128,512]{2,1,0:T(8,128)(2,1)S(1)}, u32[]{:S(2)}, u32[]{:S(2)}) %collective-permute-start.25) | collective-permute-done | bytes 524320 | tf_op jit(solution)/shard_map/ppermute | solution.py:47
  187.7 1.6 collective-permute-start.29
  189.3 1.8 collective-permute-start.30
  191.1 9.8 %shard_map.85 = (bf16[256,2048]{1,0:T(8,128)(2,1)}, bf16[256,1024]{1,0:T(8,128)(2,1)}, bf16[256,1024]{1,0:T(8,128)(2,1)}) custom-call(bf16[512,1024]{1,0:T(8,128)(2,1)} %get-tuple-element.54.dkv, bf16[256,2048]{1,0:T(8,128)(2,1)} %collective-permute-done.22.got, bf16[512,512]{1,0:T(8,128)(2,1)} %get-tuple-element.56.out.o, ...), custom_call_target="tpu_custom_call" | custom-call | flops 8589934592 | bytes 12582912 | tf_op jit(solution)/shard_map/pallas_call | solution.py:338
  201.0 2.0 collective-permute-done.29.refs_6_
  202.9 8.8 %collective-permute-done.30.refs_7_ = bf16[4,128,512]{2,1,0:T(8,128)(2,1)} collective-permute-done((bf16[4,128,512]{2,1,0:T(8,128)(2,1)}, bf16[4,128,512]{2,1,0:T(8,128)(2,1)}, u32[]{:S(2)}, u32[]{:S(2)}) %collective-permute-start.30) | collective-permute-done | bytes 524320 | tf_op jit(solution)/shard_map/ppermute | solution.py:47
  211.8 3.6 %shard_map.87 = (f32[128,512]{1,0:T(8,128)}, bf16[128,512]{1,0:T(8,128)(2,1)}, bf16[128,512]{1,0:T(8,128)(2,1)}, bf16[128,512]{1,0:T(8,128)(2,1)}, f32[128,512]{...) custom-call(bf16[4,128,512]{2,1,0:T(8,128)(2,1)} %get-tuple-element.63.refs_0_, ...), custom_call_target="tpu_custom_call" | custom-call | bytes 6553600 | tf_op jit(solution)/shard_map/pallas_call | solution.py:35
  215.4 2.6 %collective-permute-start.31 = (bf16[128,512]{1,0:T(8,128)(2,1)}, bf16[128,512]{1,0:T(8,128)(2,1)S(1)}, u32[]{:S(2)}, u32[]{:S(2)}) collective-permute-start(bf16[128,512]{1,0:T(8,128)(2,1)} %get-tuple-element.71), channel_id=1, source_target_pairs={{0,64},{64,128},{128,192},{192,0},{1,65},{65,129},{129,193},{193,1... | collective-permute-start | bytes 393224 | tf_op jit(solution)/shard_map/ppermute | solution.py:47
  218.0 1.6 collective-permute-start.32
  219.6 2.4 collective-permute-start.33
  221.9 0.9 collective-permute-start.35
  222.8 2.5 collective-permute-start.36
  226.0 3.8 %collective-permute-done.34.refs_5_ = bf16[128,512]{1,0:T(8,128)(2,1)S(1)} collective-permute-done((bf16[128,512]{1,0:T(8,128)(2,1)}, bf16[128,512]{1,0:T(8,128)(2,1)S(1)}, u32[]{:S(2)}, u32[]{:S(2)}) %collective-permute-start.34) | collective-permute-done | bytes 131104 | tf_op jit(solution)/shard_map/ppermute | solution.py:47
  229.7 0.9 collective-permute-done.36.refs_7_
  231.3 2.1 shard_map.88
  233.4 14.7 %all_to_all.31.i = bf16[16,8,1024]{2,1,0:T(8,128)(2,1)} all-to-all(bf16[16,8,1024]{2,1,0:T(8,128)(2,1)} %shard_map.88), channel_id=1, replica_groups=mesh['y'=4,'x'=4,'core'=2,'z'=8] {'core','z'}, dimensions={0} | all-to-all | bytes 524288 | tf_op jit(solution)/shard_map/all_to_all | solution.py:491
  248.1 1.6 shard_map.89
  (107 shorter events, 7.3 us)
Async XLA Ops:
  1.6 67.2 %copy-start.3 = (bf16[256,512]{1,0:T(8,128)(2,1)}, bf16[256,512]{1,0:T(8,128)(2,1)S(1)}, u32[]{:S(2)}) copy-start(bf16[256,512]{1,0:T(8,128)(2,1)S(1)} %constant_dynamic-slice_fusion.2.refs_0_) | copy-start | bytes 786436
  1.6 10.5 %collective-permute-start.1 = (bf16[256,512]{1,0:T(8,128)(2,1)S(1)}, bf16[256,512]{1,0:T(8,128)(2,1)S(1)}, u32[]{:S(2)}, u32[]{:S(2)}) collective-permute-start(bf16[256,512]{1,0:T(8,128)(2,1)S(1)} %constant_dynamic-slice_fusion.2.refs_0_), channel_id=1, source_target_pairs={{0,1},{1,2},{2,3},{3,4},{4,5},{5,6},{6,7},{7,0},{8,9},{9,10},{10,1... | collective-permute-start | bytes 786440 | tf_op jit(solution)/shard_map/ppermute | solution.py:47
  1.9 60.7 %collective-permute-start = (bf16[256,2048]{1,0:T(8,128)(2,1)}, bf16[256,2048]{1,0:T(8,128)(2,1)S(1)}, u32[]{:S(2)}, u32[]{:S(2)}) collective-permute-start(bf16[256,2048]{1,0:T(8,128)(2,1)} %own.1), channel_id=1, source_target_pairs={{0,8},{8,0},{1,9},{9,1},{2,10},{10,2},{3,11},{11,3},{4,12},{12,4},... | collective-permute-start | bytes 3145736 | tf_op jit(solution)/shard_map/ppermute | solution.py:355
  1.9 17.8 %collective-permute-start.2 = (bf16[256,512]{1,0:T(8,128)(2,1)S(1)}, bf16[256,512]{1,0:T(8,128)(2,1)S(1)}, u32[]{:S(2)}, u32[]{:S(2)}) collective-permute-start(bf16[256,512]{1,0:T(8,128)(2,1)S(1)} %constant_dynamic-slice_fusion.2.refs_0_), channel_id=1, source_target_pairs={{0,7},{1,0},{2,1},{3,2},{4,3},{5,4},{6,5},{7,6},{8,15},{9,8},{10,9... | collective-permute-start | bytes 786440 | tf_op jit(solution)/shard_map/ppermute | solution.py:47
  12.2 56.7 %copy-start.15 = (bf16[256,512]{1,0:T(8,128)(2,1)}, bf16[256,512]{1,0:T(8,128)(2,1)S(1)}, u32[]{:S(2)}) copy-start(bf16[256,512]{1,0:T(8,128)(2,1)S(1)} %collective-permute-done.1.refs_1_) | copy-start | bytes 786436
  12.2 10.8 %collective-permute-start.3 = (bf16[256,512]{1,0:T(8,128)(2,1)S(1)}, bf16[256,512]{1,0:T(8,128)(2,1)S(1)}, u32[]{:S(2)}, u32[]{:S(2)}) collective-permute-start(bf16[256,512]{1,0:T(8,128)(2,1)S(1)} %collective-permute-done.1.refs_1_), channel_id=1, source_target_pairs={{0,1},{1,2},{2,3},{3,4},{4,5},{5,6},{6,7},{7,0},{8,9},{9,10},{10,1... | collective-permute-start | bytes 786440 | tf_op jit(solution)/shard_map/ppermute | solution.py:47
  13.5 15.9 %all-to-all-start = ((bf16[8,16,512]{2,1,0:T(8,128)(2,1)}), bf16[8,16,512]{2,1,0:T(8,128)(2,1)S(1)}, u32[]{:S(2)}, u32[]{:S(2)}) async-start(bf16[8,16,512]{2,1,0:T(8,128)(2,1)} %broadcast_in_dim.2), calls=%async_computation | async-start | bytes 262144 | tf_op jit(solution)/shard_map/all_to_all | solution.py:370
  19.7 49.1 %copy-start.16 = (bf16[256,512]{1,0:T(8,128)(2,1)}, bf16[256,512]{1,0:T(8,128)(2,1)S(1)}, u32[]{:S(2)}) copy-start(bf16[256,512]{1,0:T(8,128)(2,1)S(1)} %collective-permute-done.2.refs_2_) | copy-start | bytes 786436
  19.7 21.3 %collective-permute-start.4 = (bf16[256,512]{1,0:T(8,128)(2,1)S(1)}, bf16[256,512]{1,0:T(8,128)(2,1)S(1)}, u32[]{:S(2)}, u32[]{:S(2)}) collective-permute-start(bf16[256,512]{1,0:T(8,128)(2,1)S(1)} %collective-permute-done.2.refs_2_), channel_id=1, source_target_pairs={{0,7},{1,0},{2,1},{3,2},{4,3},{5,4},{6,5},{7,6},{8,15},{9,8},{10,9... | collective-permute-start | bytes 786440 | tf_op jit(solution)/shard_map/ppermute | solution.py:47
  23.0 45.8 %copy-start.17 = (bf16[256,512]{1,0:T(8,128)(2,1)}, bf16[256,512]{1,0:T(8,128)(2,1)S(1)}, u32[]{:S(2)}) copy-start(bf16[256,512]{1,0:T(8,128)(2,1)S(1)} %collective-permute-done.3.refs_3_) | copy-start | bytes 786436
  23.0 18.5 %collective-permute-start.5 = (bf16[256,512]{1,0:T(8,128)(2,1)S(1)}, bf16[256,512]{1,0:T(8,128)(2,1)S(1)}, u32[]{:S(2)}, u32[]{:S(2)}) collective-permute-start(bf16[256,512]{1,0:T(8,128)(2,1)S(1)} %collective-permute-done.3.refs_3_), channel_id=1, source_target_pairs={{0,1},{1,2},{2,3},{3,4},{4,5},{5,6},{6,7},{7,0},{8,9},{9,10},{10,1... | collective-permute-start | bytes 786440 | tf_op jit(solution)/shard_map/ppermute | solution.py:47
  29.5 5.6 %collective-permute-start.8 = (bf16[8,16,256]{2,1,0:T(8,128)(2,1)S(1)}, bf16[8,16,256]{2,1,0:T(8,128)(2,1)S(1)}, u32[]{:S(2)}, u32[]{:S(2)}) collective-permute-start(bf16[8,16,256]{2,1,0:T(8,128)(2,1)S(1)} %get-tuple-element.81), channel_id=1, source_target_pairs={{0,16},{16,32},{32,48},{48,0},{1,17},{17,33},{33,49},{49,1},{2,18}... | collective-permute-start | bytes 196616 | tf_op jit(solution)/shard_map/ppermute | solution.py:47
  31.1 5.8 %collective-permute-start.9 = (bf16[8,16,256]{2,1,0:T(8,128)(2,1)S(1)}, bf16[8,16,256]{2,1,0:T(8,128)(2,1)S(1)}, u32[]{:S(2)}, u32[]{:S(2)}) collective-permute-start(bf16[8,16,256]{2,1,0:T(8,128)(2,1)S(1)} %get-tuple-element.81), channel_id=1, source_target_pairs={{0,32},{16,48},{32,0},{48,16},{1,33},{17,49},{33,1},{49,17},{2,34}... | collective-permute-start | bytes 196616 | tf_op jit(solution)/shard_map/ppermute | solution.py:47
  35.1 4.3 %collective-permute-start.10 = (bf16[8,16,256]{2,1,0:T(8,128)(2,1)S(1)}, bf16[8,16,256]{2,1,0:T(8,128)(2,1)S(1)}, u32[]{:S(2)}, u32[]{:S(2)}) collective-permute-start(bf16[8,16,256]{2,1,0:T(8,128)(2,1)S(1)} %get-tuple-element.81), channel_id=1, source_target_pairs={{0,48},{16,0},{32,16},{48,32},{1,49},{17,1},{33,17},{49,33},{2,50}... | collective-permute-start | bytes 196616 | tf_op jit(solution)/shard_map/ppermute | solution.py:47
  36.8 6.2 %collective-permute-start.14 = (bf16[8,16,256]{2,1,0:T(8,128)(2,1)S(1)}, bf16[8,16,256]{2,1,0:T(8,128)(2,1)S(1)}, u32[]{:S(2)}, u32[]{:S(2)}) collective-permute-start(bf16[8,16,256]{2,1,0:T(8,128)(2,1)S(1)} %get-tuple-element.80), channel_id=1, source_target_pairs={{0,64},{64,128},{128,192},{192,0},{1,65},{65,129},{129,193},{193,1... | collective-permute-start | bytes 196616 | tf_op jit(solution)/shard_map/ppermute | solution.py:47
  39.4 34.9 %copy-start.4 = (bf16[4,8,16,256]{3,2,1,0:T(8,128)(2,1)}, bf16[4,8,16,256]{3,2,1,0:T(8,128)(2,1)S(1)}, u32[]{:S(2)}) copy-start(bf16[4,8,16,256]{3,2,1,0:T(8,128)(2,1)S(1)} %pad_maximum_fusion.refs_0_) | copy-start | bytes 786436
  39.4 17.4 %collective-permute-start.11 = (bf16[4,8,16,256]{3,2,1,0:T(8,128)(2,1)S(1)}, bf16[4,8,16,256]{3,2,1,0:T(8,128)(2,1)S(1)}, u32[]{:S(2)}, u32[]{:S(2)}) collective-permute-start(bf16[4,8,16,256]{3,2,1,0:T(8,128)(2,1)S(1)} %pad_maximum_fusion.refs_0_), channel_id=1, source_target_pairs={{0,64},{64,128},{128,192},{192,0},{1,65},{65,129},{129,193},{193,1... | collective-permute-start | bytes 786440 | tf_op jit(solution)/shard_map/ppermute | solution.py:47
  41.0 27.8 %copy-start.18 = (bf16[256,512]{1,0:T(8,128)(2,1)}, bf16[256,512]{1,0:T(8,128)(2,1)S(1)}, u32[]{:S(2)}) copy-start(bf16[256,512]{1,0:T(8,128)(2,1)S(1)} %collective-permute-done.4.refs_4_) | copy-start | bytes 786436
  41.0 17.3 %collective-permute-start.6 = (bf16[256,512]{1,0:T(8,128)(2,1)S(1)}, bf16[256,512]{1,0:T(8,128)(2,1)S(1)}, u32[]{:S(2)}, u32[]{:S(2)}) collective-permute-start(bf16[256,512]{1,0:T(8,128)(2,1)S(1)} %collective-permute-done.4.refs_4_), channel_id=1, source_target_pairs={{0,7},{1,0},{2,1},{3,2},{4,3},{5,4},{6,5},{7,6},{8,15},{9,8},{10,9... | collective-permute-start | bytes 786440 | tf_op jit(solution)/shard_map/ppermute | solution.py:47
  41.5 27.4 %copy-start.19 = (bf16[256,512]{1,0:T(8,128)(2,1)}, bf16[256,512]{1,0:T(8,128)(2,1)S(1)}, u32[]{:S(2)}) copy-start(bf16[256,512]{1,0:T(8,128)(2,1)S(1)} %collective-permute-done.5.refs_5_) | copy-start | bytes 786436
  41.5 17.2 %collective-permute-start.7 = (bf16[256,512]{1,0:T(8,128)(2,1)S(1)}, bf16[256,512]{1,0:T(8,128)(2,1)S(1)}, u32[]{:S(2)}, u32[]{:S(2)}) collective-permute-start(bf16[256,512]{1,0:T(8,128)(2,1)S(1)} %collective-permute-done.5.refs_5_), channel_id=1, source_target_pairs={{0,1},{1,2},{2,3},{3,4},{4,5},{5,6},{6,7},{7,0},{8,9},{9,10},{10,1... | collective-permute-start | bytes 786440 | tf_op jit(solution)/shard_map/ppermute | solution.py:47
  43.1 5.9 %collective-permute-start.15 = (bf16[8,16,256]{2,1,0:T(8,128)(2,1)S(1)}, bf16[8,16,256]{2,1,0:T(8,128)(2,1)S(1)}, u32[]{:S(2)}, u32[]{:S(2)}) collective-permute-start(bf16[8,16,256]{2,1,0:T(8,128)(2,1)S(1)} %get-tuple-element.80), channel_id=1, source_target_pairs={{0,128},{64,192},{128,0},{192,64},{1,129},{65,193},{129,1},{193,65... | collective-permute-start | bytes 196616 | tf_op jit(solution)/shard_map/ppermute | solution.py:47
  48.9 5.0 %collective-permute-start.16 = (bf16[8,16,256]{2,1,0:T(8,128)(2,1)S(1)}, bf16[8,16,256]{2,1,0:T(8,128)(2,1)S(1)}, u32[]{:S(2)}, u32[]{:S(2)}) collective-permute-start(bf16[8,16,256]{2,1,0:T(8,128)(2,1)S(1)} %get-tuple-element.80), channel_id=1, source_target_pairs={{0,192},{64,0},{128,64},{192,128},{1,193},{65,1},{129,65},{193,129... | collective-permute-start | bytes 196616 | tf_op jit(solution)/shard_map/ppermute | solution.py:47
  53.9 20.4 %collective-permute-start.12 = (bf16[4,8,16,256]{3,2,1,0:T(8,128)(2,1)S(1)}, bf16[4,8,16,256]{3,2,1,0:T(8,128)(2,1)}, u32[]{:S(2)}, u32[]{:S(2)}) collective-permute-start(bf16[4,8,16,256]{3,2,1,0:T(8,128)(2,1)S(1)} %pad_maximum_fusion.refs_0_), channel_id=1, source_target_pairs={{0,128},{64,192},{128,0},{192,64},{1,129},{65,193},{129,1},{193,65... | collective-permute-start | bytes 786440 | tf_op jit(solution)/shard_map/ppermute | solution.py:47
  56.7 17.6 %copy-start.5 = (bf16[4,8,16,256]{3,2,1,0:T(8,128)(2,1)}, bf16[4,8,16,256]{3,2,1,0:T(8,128)(2,1)S(1)}, u32[]{:S(2)}) copy-start(bf16[4,8,16,256]{3,2,1,0:T(8,128)(2,1)S(1)} %pad_maximum_fusion.1.refs_4_) | copy-start | bytes 786436
  56.7 17.6 %copy-start.20 = (bf16[4,8,16,256]{3,2,1,0:T(8,128)(2,1)}, bf16[4,8,16,256]{3,2,1,0:T(8,128)(2,1)S(1)}, u32[]{:S(2)}) copy-start(bf16[4,8,16,256]{3,2,1,0:T(8,128)(2,1)S(1)} %collective-permute-done.11.refs_1_) | copy-start | bytes 786436
  56.7 17.6 %collective-permute-start.13 = (bf16[4,8,16,256]{3,2,1,0:T(8,128)(2,1)S(1)}, bf16[4,8,16,256]{3,2,1,0:T(8,128)(2,1)}, u32[]{:S(2)}, u32[]{:S(2)}) collective-permute-start(bf16[4,8,16,256]{3,2,1,0:T(8,128)(2,1)S(1)} %pad_maximum_fusion.refs_0_), channel_id=1, source_target_pairs={{0,192},{64,0},{128,64},{192,128},{1,193},{65,1},{129,65},{193,129... | collective-permute-start | bytes 786440 | tf_op jit(solution)/shard_map/ppermute | solution.py:47
  58.4 4.2 %copy-start.21 = (bf16[256,512]{1,0:T(8,128)(2,1)}, bf16[256,512]{1,0:T(8,128)(2,1)S(1)}, u32[]{:S(2)}) copy-start(bf16[256,512]{1,0:T(8,128)(2,1)S(1)} %collective-permute-done.6.refs_6_) | copy-start | bytes 786436
  58.4 16.0 %collective-permute-start.17 = (bf16[4,8,16,256]{3,2,1,0:T(8,128)(2,1)S(1)}, bf16[4,8,16,256]{3,2,1,0:T(8,128)(2,1)}, u32[]{:S(2)}, u32[]{:S(2)}) collective-permute-start(bf16[4,8,16,256]{3,2,1,0:T(8,128)(2,1)S(1)} %pad_maximum_fusion.1.refs_4_), channel_id=1, source_target_pairs={{0,16},{16,32},{32,48},{48,0},{1,17},{17,33},{33,49},{49,1},{2,18}... | collective-permute-start | bytes 786440 | tf_op jit(solution)/shard_map/ppermute | solution.py:47
  58.7 3.9 %copy-start.22 = (bf16[256,512]{1,0:T(8,128)(2,1)}, bf16[256,512]{1,0:T(8,128)(2,1)S(1)}, u32[]{:S(2)}) copy-start(bf16[256,512]{1,0:T(8,128)(2,1)S(1)} %collective-permute-done.7.refs_7_) | copy-start | bytes 786436
  58.7 15.7 %collective-permute-start.18 = (bf16[4,8,16,256]{3,2,1,0:T(8,128)(2,1)S(1)}, bf16[4,8,16,256]{3,2,1,0:T(8,128)(2,1)}, u32[]{:S(2)}, u32[]{:S(2)}) collective-permute-start(bf16[4,8,16,256]{3,2,1,0:T(8,128)(2,1)S(1)} %pad_maximum_fusion.1.refs_4_), channel_id=1, source_target_pairs={{0,32},{16,48},{32,0},{48,16},{1,33},{17,49},{33,1},{49,17},{2,34}... | collective-permute-start | bytes 786440 | tf_op jit(solution)/shard_map/ppermute | solution.py:47
  62.6 11.7 %collective-permute-start.19 = (bf16[4,8,16,256]{3,2,1,0:T(8,128)(2,1)S(1)}, bf16[4,8,16,256]{3,2,1,0:T(8,128)(2,1)}, u32[]{:S(2)}, u32[]{:S(2)}) collective-permute-start(bf16[4,8,16,256]{3,2,1,0:T(8,128)(2,1)S(1)} %pad_maximum_fusion.1.refs_4_), channel_id=1, source_target_pairs={{0,48},{16,0},{32,16},{48,32},{1,49},{17,1},{33,17},{49,33},{2,50}... | collective-permute-start | bytes 786440 | tf_op jit(solution)/shard_map/ppermute | solution.py:47
  74.4 10.5 %copy-start.1 = (bf16[256,1024]{1,0:T(8,128)(2,1)S(1)}, bf16[256,1024]{1,0:T(8,128)(2,1)}, u32[]{:S(2)}) copy-start(bf16[256,1024]{1,0:T(8,128)(2,1)} %q_own.1) | copy-start | bytes 1572868
  81.4 13.8 %all-to-all-start.1 = ((bf16[8,128,128]{2,1,0:T(8,128)(2,1)}), bf16[8,128,128]{2,1,0:T(8,128)(2,1)S(1)}, u32[]{:S(2)}, u32[]{:S(2)}) async-start(bf16[8,128,128]{2,1,0:T(8,128)(2,1)} %get-tuple-element.48), calls=%async_computation.1 | async-start | bytes 524288 | tf_op jit(solution)/shard_map/all_to_all | solution.py:419
  84.9 16.8 %copy-start.2 = (bf16[256,1024]{1,0:T(8,128)(2,1)S(1)}, bf16[256,1024]{1,0:T(8,128)(2,1)}, u32[]{:S(2)}) copy-start(bf16[256,1024]{1,0:T(8,128)(2,1)} %g_own.1) | copy-start | bytes 1572868
  84.9 1.6 collective-permute-start.20
  97.6 16.2 %all-to-all-start.2 = ((bf16[8,128,128]{2,1,0:T(8,128)(2,1)}), bf16[8,128,128]{2,1,0:T(8,128)(2,1)S(1)}, u32[]{:S(2)}, u32[]{:S(2)}) async-start(bf16[8,128,128]{2,1,0:T(8,128)(2,1)} %shard_map.79), calls=%async_computation.2 | async-start | bytes 524288 | tf_op jit(solution)/shard_map/all_to_all | solution.py:423
  101.7 1.6 collective-permute-start.21
  103.3 10.5 %copy-start.23 = (bf16[256,512]{1,0:T(8,128)(2,1)}, bf16[256,512]{1,0:T(8,128)(2,1)S(1)}, u32[]{:S(2)}) copy-start(bf16[256,512]{1,0:T(8,128)(2,1)S(1)} %collective-permute-done.21.g_sib) | copy-start | bytes 786436
  119.1 14.4 %all-to-all-start.3 = ((bf16[8,128,128]{2,1,0:T(8,128)(2,1)}), bf16[8,128,128]{2,1,0:T(8,128)(2,1)S(1)}, u32[]{:S(2)}, u32[]{:S(2)}) async-start(bf16[8,128,128]{2,1,0:T(8,128)(2,1)} %get-tuple-element.52), calls=%async_computation.3 | async-start | bytes 524288 | tf_op jit(solution)/shard_map/all_to_all | solution.py:419
  122.5 44.2 %collective-permute-start.24 = (bf16[8,16,16,512]{3,2,1,0:T(8,128)(2,1)}, bf16[8,16,16,512]{3,2,1,0:T(8,128)(2,1)}, u32[]{:S(2)}, u32[]{:S(2)}) collective-permute-start(bf16[8,16,16,512]{3,2,1,0:T(8,128)(2,1)} %get-tuple-element.59.wv), channel_id=1, source_target_pairs={{0,8},{8,0},{1,9},{9,1},{2,10},{10,2},{3,11},{11,3},{4,12},{12,4},... | collective-permute-start | bytes 6291464 | tf_op jit(solution)/shard_map/ppermute | solution.py:355
  122.6 46.3 %collective-permute-start.23 = (bf16[8,256,512]{2,1,0:T(8,128)(2,1)}, bf16[8,256,512]{2,1,0:T(8,128)(2,1)}, u32[]{:S(2)}, u32[]{:S(2)}) collective-permute-start(bf16[8,256,512]{2,1,0:T(8,128)(2,1)} %get-tuple-element.58.wk), channel_id=1, source_target_pairs={{0,8},{8,0},{1,9},{9,1},{2,10},{10,2},{3,11},{11,3},{4,12},{12,4},... | collective-permute-start | bytes 6291464 | tf_op jit(solution)/shard_map/ppermute | solution.py:355
  158.3 3.8 %copy-start.11 = (bf16[4,128,512]{2,1,0:T(8,128)(2,1)S(1)}, bf16[4,128,512]{2,1,0:T(8,128)(2,1)}, u32[]{:S(2)}) copy-start(bf16[4,128,512]{2,1,0:T(8,128)(2,1)} %get-tuple-element.57._) | copy-start | bytes 1572868
  160.9 28.4 %collective-permute-start.22 = (bf16[256,2048]{1,0:T(8,128)(2,1)}, bf16[256,2048]{1,0:T(8,128)(2,1)}, u32[]{:S(2)}, u32[]{:S(2)}) collective-permute-start(bf16[256,2048]{1,0:T(8,128)(2,1)} %shard_map.84._), channel_id=1, source_target_pairs={{0,8},{8,0},{1,9},{9,1},{2,10},{10,2},{3,11},{11,3},{4,12},{12,4},... | collective-permute-start | bytes 3145736 | tf_op jit(solution)/shard_map/ppermute | solution.py:355
  160.9 26.8 %collective-permute-start.25 = (bf16[4,128,512]{2,1,0:T(8,128)(2,1)S(1)}, bf16[4,128,512]{2,1,0:T(8,128)(2,1)S(1)}, u32[]{:S(2)}, u32[]{:S(2)}) collective-permute-start(bf16[4,128,512]{2,1,0:T(8,128)(2,1)S(1)} %copy-done.31), channel_id=1, source_target_pairs={{0,16},{16,32},{32,48},{48,0},{1,17},{17,33},{33,49},{49,1},{2,18}... | collective-permute-start | bytes 1572872 | tf_op jit(solution)/shard_map/ppermute | solution.py:47
  162.1 38.8 %collective-permute-start.26 = (bf16[4,128,512]{2,1,0:T(8,128)(2,1)S(1)}, bf16[4,128,512]{2,1,0:T(8,128)(2,1)S(1)}, u32[]{:S(2)}, u32[]{:S(2)}) collective-permute-start(bf16[4,128,512]{2,1,0:T(8,128)(2,1)S(1)} %copy-done.11), channel_id=1, source_target_pairs={{0,32},{16,48},{32,0},{48,16},{1,33},{17,49},{33,1},{49,17},{2,34}... | collective-permute-start | bytes 1572872 | tf_op jit(solution)/shard_map/ppermute | solution.py:47
  166.8 34.2 %collective-permute-start.27 = (bf16[4,128,512]{2,1,0:T(8,128)(2,1)}, bf16[4,128,512]{2,1,0:T(8,128)(2,1)S(1)}, u32[]{:S(2)}, u32[]{:S(2)}) collective-permute-start(bf16[4,128,512]{2,1,0:T(8,128)(2,1)} %get-tuple-element.65), channel_id=1, source_target_pairs={{0,48},{16,0},{32,16},{48,32},{1,49},{17,1},{33,17},{49,33},{2,50}... | collective-permute-start | bytes 1572872 | tf_op jit(solution)/shard_map/ppermute | solution.py:47
  168.9 32.0 %collective-permute-start.28 = (bf16[4,128,512]{2,1,0:T(8,128)(2,1)}, bf16[4,128,512]{2,1,0:T(8,128)(2,1)S(1)}, u32[]{:S(2)}, u32[]{:S(2)}) collective-permute-start(bf16[4,128,512]{2,1,0:T(8,128)(2,1)} %get-tuple-element.67), channel_id=1, source_target_pairs={{0,64},{64,128},{128,192},{192,0},{1,65},{65,129},{129,193},{193,1... | collective-permute-start | bytes 1572872 | tf_op jit(solution)/shard_map/ppermute | solution.py:47
  187.7 13.2 %copy-start.9 = (bf16[4,128,512]{2,1,0:T(8,128)(2,1)}, bf16[4,128,512]{2,1,0:T(8,128)(2,1)S(1)}, u32[]{:S(2)}) copy-start(bf16[4,128,512]{2,1,0:T(8,128)(2,1)S(1)} %collective-permute-done.25.refs_1_) | copy-start | bytes 1572868
  187.7 15.2 %collective-permute-start.29 = (bf16[4,128,512]{2,1,0:T(8,128)(2,1)}, bf16[4,128,512]{2,1,0:T(8,128)(2,1)S(1)}, u32[]{:S(2)}, u32[]{:S(2)}) collective-permute-start(bf16[4,128,512]{2,1,0:T(8,128)(2,1)} %get-tuple-element.68), channel_id=1, source_target_pairs={{0,128},{64,192},{128,0},{192,64},{1,129},{65,193},{129,1},{193,65... | collective-permute-start | bytes 1572872 | tf_op jit(solution)/shard_map/ppermute | solution.py:47
  189.3 22.4 %collective-permute-start.30 = (bf16[4,128,512]{2,1,0:T(8,128)(2,1)}, bf16[4,128,512]{2,1,0:T(8,128)(2,1)}, u32[]{:S(2)}, u32[]{:S(2)}) collective-permute-start(bf16[4,128,512]{2,1,0:T(8,128)(2,1)} %get-tuple-element.69), channel_id=1, source_target_pairs={{0,192},{64,0},{128,64},{192,128},{1,193},{65,1},{129,65},{193,129... | collective-permute-start | bytes 1572872 | tf_op jit(solution)/shard_map/ppermute | solution.py:47
  200.9 10.8 %copy-start.10 = (bf16[4,128,512]{2,1,0:T(8,128)(2,1)}, bf16[4,128,512]{2,1,0:T(8,128)(2,1)S(1)}, u32[]{:S(2)}) copy-start(bf16[4,128,512]{2,1,0:T(8,128)(2,1)S(1)} %collective-permute-done.26.refs_2_) | copy-start | bytes 1572868
  200.9 10.8 %copy-start.12 = (bf16[4,128,512]{2,1,0:T(8,128)(2,1)}, bf16[4,128,512]{2,1,0:T(8,128)(2,1)S(1)}, u32[]{:S(2)}) copy-start(bf16[4,128,512]{2,1,0:T(8,128)(2,1)S(1)} %collective-permute-done.27.refs_3_) | copy-start | bytes 1572868
  200.9 10.8 %copy-start.13 = (bf16[4,128,512]{2,1,0:T(8,128)(2,1)}, bf16[4,128,512]{2,1,0:T(8,128)(2,1)S(1)}, u32[]{:S(2)}) copy-start(bf16[4,128,512]{2,1,0:T(8,128)(2,1)S(1)} %collective-permute-done.28.refs_5_) | copy-start | bytes 1572868
  202.9 8.8 %copy-start.14 = (bf16[4,128,512]{2,1,0:T(8,128)(2,1)}, bf16[4,128,512]{2,1,0:T(8,128)(2,1)S(1)}, u32[]{:S(2)}) copy-start(bf16[4,128,512]{2,1,0:T(8,128)(2,1)S(1)} %collective-permute-done.29.refs_6_) | copy-start | bytes 1572868
  215.4 7.4 %collective-permute-start.31 = (bf16[128,512]{1,0:T(8,128)(2,1)}, bf16[128,512]{1,0:T(8,128)(2,1)S(1)}, u32[]{:S(2)}, u32[]{:S(2)}) collective-permute-start(bf16[128,512]{1,0:T(8,128)(2,1)} %get-tuple-element.71), channel_id=1, source_target_pairs={{0,64},{64,128},{128,192},{192,0},{1,65},{65,129},{129,193},{193,1... | collective-permute-start | bytes 393224 | tf_op jit(solution)/shard_map/ppermute | solution.py:47
  218.0 8.0 %collective-permute-start.32 = (bf16[128,512]{1,0:T(8,128)(2,1)}, bf16[128,512]{1,0:T(8,128)(2,1)S(1)}, u32[]{:S(2)}, u32[]{:S(2)}) collective-permute-start(bf16[128,512]{1,0:T(8,128)(2,1)} %get-tuple-element.72), channel_id=1, source_target_pairs={{0,128},{64,192},{128,0},{192,64},{1,129},{65,193},{129,1},{193,65... | collective-permute-start | bytes 393224 | tf_op jit(solution)/shard_map/ppermute | solution.py:47
  219.6 6.4 %collective-permute-start.33 = (bf16[128,512]{1,0:T(8,128)(2,1)}, bf16[128,512]{1,0:T(8,128)(2,1)S(1)}, u32[]{:S(2)}, u32[]{:S(2)}) collective-permute-start(bf16[128,512]{1,0:T(8,128)(2,1)} %get-tuple-element.73), channel_id=1, source_target_pairs={{0,192},{64,0},{128,64},{192,128},{1,193},{65,1},{129,65},{193,129... | collective-permute-start | bytes 393224 | tf_op jit(solution)/shard_map/ppermute | solution.py:47
  221.9 7.8 %collective-permute-start.34 = (bf16[128,512]{1,0:T(8,128)(2,1)}, bf16[128,512]{1,0:T(8,128)(2,1)S(1)}, u32[]{:S(2)}, u32[]{:S(2)}) collective-permute-start(bf16[128,512]{1,0:T(8,128)(2,1)} %get-tuple-element.75), channel_id=1, source_target_pairs={{0,16},{16,32},{32,48},{48,0},{1,17},{17,33},{33,49},{49,1},{2,18}... | collective-permute-start | bytes 393224 | tf_op jit(solution)/shard_map/ppermute | solution.py:47
  221.9 7.8 %collective-permute-start.35 = (bf16[128,512]{1,0:T(8,128)(2,1)}, bf16[128,512]{1,0:T(8,128)(2,1)S(1)}, u32[]{:S(2)}, u32[]{:S(2)}) collective-permute-start(bf16[128,512]{1,0:T(8,128)(2,1)} %get-tuple-element.76), channel_id=1, source_target_pairs={{0,32},{16,48},{32,0},{48,16},{1,33},{17,49},{33,1},{49,17},{2,34}... | collective-permute-start | bytes 393224 | tf_op jit(solution)/shard_map/ppermute | solution.py:47
  222.8 7.8 %copy-start.25 = (bf16[128,512]{1,0:T(8,128)(2,1)}, bf16[128,512]{1,0:T(8,128)(2,1)S(1)}, u32[]{:S(2)}) copy-start(bf16[128,512]{1,0:T(8,128)(2,1)S(1)} %collective-permute-done.31.refs_1_) | copy-start | bytes 393220
  222.8 7.8 %collective-permute-start.36 = (bf16[128,512]{1,0:T(8,128)(2,1)}, bf16[128,512]{1,0:T(8,128)(2,1)S(1)}, u32[]{:S(2)}, u32[]{:S(2)}) collective-permute-start(bf16[128,512]{1,0:T(8,128)(2,1)} %get-tuple-element.77), channel_id=1, source_target_pairs={{0,48},{16,0},{32,16},{48,32},{1,49},{17,1},{33,17},{49,33},{2,50}... | collective-permute-start | bytes 393224 | tf_op jit(solution)/shard_map/ppermute | solution.py:47
  226.0 4.7 %copy-start.26 = (bf16[128,512]{1,0:T(8,128)(2,1)}, bf16[128,512]{1,0:T(8,128)(2,1)S(1)}, u32[]{:S(2)}) copy-start(bf16[128,512]{1,0:T(8,128)(2,1)S(1)} %collective-permute-done.32.refs_2_) | copy-start | bytes 393220
  226.0 4.7 %copy-start.27 = (bf16[128,512]{1,0:T(8,128)(2,1)}, bf16[128,512]{1,0:T(8,128)(2,1)S(1)}, u32[]{:S(2)}) copy-start(bf16[128,512]{1,0:T(8,128)(2,1)S(1)} %collective-permute-done.33.refs_3_) | copy-start | bytes 393220
  (9 other events, 9.0 us)
